TPU v7x, 32 devices: a whole 2x2x4 slice. The times are simulated.
32 devices in a mesh: sector: 4 (over z), axial: 8 (over y, x, core).
Axes of the slice: x: 2, y: 2, z: 4, core: 2. Of those that a mesh axis runs over, the one named last changes fastest.
Arguments:
- kbb: float32 [4096, 64, 64], P(('sector', 'axial')), as said below
- interior: bfloat16 [4096, 256, 64], P(('sector', 'axial')), may hold values from -0.075683594 to 0.075683594
- node_lists: int32 [4096, 64], P(('sector', 'axial')), may hold values from -1 to 63
- owners: int32 [4096, 1], P(('sector', 'axial')), may hold values from 0 to 31; in each aligned block of 128 rows (0 to 127, 128 to 255, ...) at most 8 rows name the same one
- patch_ids: int32 [4096], P(('sector', 'axial')), may hold values from 0 to 63
- counts: int32 [32], P(('sector', 'axial')), may hold values from 96 to 128
- capacity: float32 [131072], P(('sector', 'axial')), may hold values from 0.2 to 2
- links: int32 [2, 512, 2], P(None, ('sector', 'axial')), may hold values from 0 to 63
- conduct: float32 [2, 512, 64], P(None, ('sector', 'axial')), may hold values from 0.5 to 4
- loads: float32 [131072, 128], P(('sector', 'axial')), may hold values from -24 to 24
Outputs:
- current_estimate: float32 [131072, 128], P(('sector', 'axial'))
- remaining_imbalance: float32 [131072, 128], P(('sector', 'axial'))
Inputs may be any that keep to these rules, and one draw needn't show every extreme that they name: `owners`: no owner is named by more than 8 of one device's slots, live or not, and in every draw some owner is named by exactly 8 of some device's slots. The live slots of a device are its first counts slots; the others are padding. `kbb`: the boundary block is symmetric with non-positive entries off the diagonal whose row sums stay under its diagonal.
All inputs are finite; a program needn't handle non-finite values.
Results may differ from a plain program's by a relative error of at most 0.0003.
Values sent between devices are 32-bit elements; how exact they have to be, the bound alone decides.
No kernel may reach another device: no remote copies, remote signals or barrier semaphores. Data moves between devices by JAX's collectives and lax.ppermute only.
A program may use at most 128 MiB of HBM per device.

v0:
```python
import jax
import jax.numpy as jnp
from jax import lax
from jax.sharding import PartitionSpec as P

ITERS = 3


highest = lax.Precision.HIGHEST


def from_behind(array, axis, by):
    length = lax.axis_size(axis)
    return lax.ppermute(array, axis, [(i, (i + by) % length) for i in range(length)])


def shifted(block, axis, distance):
    devices = range(lax.axis_size(axis))
    route = [(i - distance, i) for i in devices if i - distance in devices]
    return lax.ppermute(block, axis, route)


def onehot_rows(index, count):
    return (index[:, None] == jnp.arange(count, dtype=jnp.int32)[None, :]).astype(jnp.float32)


def spread_field(index, values, count):
    return jnp.einsum("lp,lir->pir", onehot_rows(index, count), values, precision=highest)


def spread_flat(index, values, count):
    return jnp.einsum("lp,li->pi", onehot_rows(index, count), values, precision=highest)


def shards(kbb, interior, node_lists, owners, patch_ids, counts, capacity, links, conduct, loads):
    elem_slots, bound_nodes = node_lists.shape
    devices = lax.axis_size("sector") * lax.axis_size("axial")
    slots_each = 2 * elem_slots // devices
    total_slots = devices * slots_each
    points_in_partition, scenario_vectors = loads.shape
    patch_dev = points_in_partition // bound_nodes
    schur = kbb - jnp.einsum("eib,eic->ebc", interior, interior, preferred_element_type=jnp.float32)
    live = (jnp.arange(elem_slots, dtype=jnp.int32) < counts[0]).astype(jnp.int32)
    owner_hot = onehot_rows(owners[:, 0], devices)
    ranks = jnp.sum(jnp.cumsum(owner_hot, axis=0) * owner_hot, axis=1).astype(jnp.int32) - 1
    target = owners[:, 0] * slots_each + ranks
    send_blocks = (
        jnp.zeros((total_slots, bound_nodes, bound_nodes), jnp.float32).at[target].set(schur)
    )
    send_nodes = jnp.full((total_slots, bound_nodes), -1, jnp.int32).at[target].set(node_lists)
    send_patch = jnp.zeros((total_slots,), jnp.int32).at[target].set(patch_ids)
    send_live = jnp.zeros((total_slots,), jnp.int32).at[target].set(live)
    blocks_in, nodes_in, patch_in, live_in = (
        lax.all_to_all(send_blocks, ("sector", "axial"), split_axis=0, concat_axis=0, tiled=True),
        lax.all_to_all(send_nodes, ("sector", "axial"), split_axis=0, concat_axis=0, tiled=True),
        lax.all_to_all(send_patch, ("sector", "axial"), split_axis=0, concat_axis=0, tiled=True),
        lax.all_to_all(send_live, ("sector", "axial"), split_axis=0, concat_axis=0, tiled=True),
    )
    picker = (
        nodes_in[:, :, None] == jnp.arange(bound_nodes, dtype=jnp.int32)[None, None, :]
    ).astype(jnp.float32)
    half = jnp.einsum("rsj,rst->rjt", picker, blocks_in, precision=highest)
    placed = jnp.einsum("rjt,rtk->rjk", half, picker, precision=highest)
    weights = onehot_rows(patch_in, patch_dev) * live_in[:, None].astype(jnp.float32)
    assembled = jnp.einsum("rp,rjk->pjk", weights, placed, precision=highest)
    sector_own = links[0, :, 0]
    sector_far = links[0, :, 1]
    sector_gain = conduct[0]
    axial_own = links[1, :, 0]
    axial_far = links[1, :, 1]
    axial_gain = conduct[1]
    sector_in_far, sector_in_gain = from_behind((sector_far, sector_gain), "sector", 1)
    axial_in_far, axial_in_gain = shifted((axial_far, axial_gain), "axial", 1)
    heat = capacity.reshape(patch_dev, bound_nodes)
    diagonal = heat + jnp.diagonal(assembled, axis1=1, axis2=2)
    diagonal = (
        diagonal
        + spread_flat(sector_own, sector_gain, patch_dev)
        + spread_flat(sector_in_far, sector_in_gain, patch_dev)
    )
    diagonal = (
        diagonal
        + spread_flat(axial_own, axial_gain, patch_dev)
        + spread_flat(axial_in_far, axial_in_gain, patch_dev)
    )

    def precond_sum(remaining_imbalance, precond):
        return lax.psum(jnp.sum(remaining_imbalance * precond, axis=(0, 1)), ("sector", "axial"))

    remaining_imbalance = loads.reshape(patch_dev, bound_nodes, scenario_vectors)
    current_estimate = jnp.zeros_like(remaining_imbalance)
    scale = diagonal[:, :, None]
    precond = remaining_imbalance / scale
    update_vector = precond
    norm_now = precond_sum(remaining_imbalance, precond)
    for sweep in range(ITERS):
        result = heat[:, :, None] * update_vector + jnp.einsum(
            "pij,pjr->pir", assembled, update_vector, precision=highest
        )
        beyond = from_behind(update_vector[sector_in_far], "sector", -1)
        flux = sector_gain[:, :, None] * (update_vector[sector_own] - beyond)
        passed = from_behind(flux, "sector", 1)
        result = (
            result
            + spread_field(sector_own, flux, patch_dev)
            - spread_field(sector_in_far, passed, patch_dev)
        )
        beyond = shifted(update_vector[axial_in_far], "axial", -1)
        flux = axial_gain[:, :, None] * (update_vector[axial_own] - beyond)
        passed = shifted(flux, "axial", 1)
        result = (
            result
            + spread_field(axial_own, flux, patch_dev)
            - spread_field(axial_in_far, passed, patch_dev)
        )
        update_factor = norm_now / lax.psum(
            jnp.sum(update_vector * result, axis=(0, 1)), ("sector", "axial")
        )
        current_estimate = current_estimate + update_factor * update_vector
        remaining_imbalance = remaining_imbalance - update_factor * result
        if sweep + 1 < ITERS:
            precond = remaining_imbalance / scale
            norm_next = precond_sum(remaining_imbalance, precond)
            update_vector = precond + norm_next / norm_now * update_vector
            norm_now = norm_next
    return (
        current_estimate.reshape(points_in_partition, scenario_vectors),
        remaining_imbalance.reshape(points_in_partition, scenario_vectors),
    )


def solution(mesh):
    placed = (
        P(("sector", "axial"), None, None),
        P(("sector", "axial"), None, None),
        P(("sector", "axial"), None),
        P(("sector", "axial"), None),
        P(("sector", "axial")),
        P(("sector", "axial")),
        P(("sector", "axial")),
        P(None, ("sector", "axial"), None),
        P(None, ("sector", "axial"), None),
        P(("sector", "axial"), None),
    )
    return jax.shard_map(
        shards,
        mesh=mesh,
        in_specs=placed,
        out_specs=(P(("sector", "axial"), None), P(("sector", "axial"), None)),
        check_vma=False,
    )
```

profile of v0, /device:TPU:0, one launch (start us, length us, event | category | flops | bytes accessed | tf_op | source)
XLA Modules:
  0.0 622.2 jit_solution(7202846408577687185)
XLA Ops:
  5.4 7.3 %all-to-all-start.1 = ((s32[32,8,1]{1,2,0:T(1,128)}), s32[32,8,1]{1,2,0:T(1,128)S(1)}, u32[]{:S(2)}, u32[]{:S(2)}) async-start(s32[32,8,1]{1,2,0:T(1,128)} %bitcast.5), calls=%async_computation.1 | async-start | bytes 32768 | tf_op jit(solution)/shard_map/all_to_all | solution.py:57
  14.5 5.3 all-to-all-done.1
  22.3 5.6 copy.75
  29.7 5.8 all-to-all-start.2
  35.5 7.9 %convolution_subtract_fusion = f32[128,64,64]{2,1,0:T(8,128)} fusion(f32[128,64,64]{2,1,0:T(8,128)} %copy.75, bf16[128,256,64]{1,2,0:T(8,128)(2,1)} %param.11), kind=kOutput, calls=%fused_computation.25 | convolution fusion | flops 268959744 | bytes 8388608 | tf_op jit(solution)/shard_map/eib,eic->ebc/dot_general | solution.py:42
  43.4 4.3 broadcast_in_dim.11
  47.7 19.4 %scatter_fusion = f32[256,64,64]{2,1,0:T(8,128)} fusion(f32[256,64,64]{2,1,0:T(8,128)} %broadcast_in_dim.11, s32[128]{0:T(128)S(1)} %fusion.85, f32[128,64,64]{2,1,0:T(8,128)} %convolution_subtract_fusion), kind=kCustom, calls=%fused_computation.16 | custom fusion | bytes 6291968 | tf_op jit(solution)/shard_map/scatter | solution.py:48
  67.1 9.8 %reshape.288 = f32[32,1,32768]{2,1,0:T(1,128)} reshape(f32[256,64,64]{2,1,0:T(8,128)} %scatter_fusion) | data formatting | bytes 8388608
  76.9 6.0 all-to-all-start.3
  87.6 3.9 collective-permute-start.2
  95.2 81.8 %all-to-all-done.3 = f32[32,1,32768]{2,1,0:T(1,128)} async-done(((f32[32,1,32768]{2,1,0:T(1,128)}), f32[32,1,32768]{2,1,0:T(1,128)}, u32[]{:S(2)}, u32[]{:S(2)}) %all-to-all-start.3) | async-done | bytes 4194336 | tf_op jit(solution)/shard_map/all_to_all | solution.py:54
  177.4 13.7 %reduce.9 = f32[32,32768]{1,0:T(8,128)} reduce(f32[32,1,32768]{2,1,0:T(1,128)} %all-to-all-done.3, f32[]{:T(128)} %broadcast.166), dimensions={1}, to_apply=%all_to_all.27.reduce_sub_computation | reduce | bytes 8388612 | tf_op jit(solution)/shard_map/all_to_all | solution.py:54
  191.2 7.4 %reshape.289 = f32[256,64,64]{2,1,0:T(8,128)} reshape(f32[32,32768]{1,0:T(8,128)} %reduce.9) | data formatting | bytes 8388608
  198.5 11.8 %fusion.3 = f32[256,64,64]{2,1,0:T(8,128)S(1)} fusion(f32[256,64,64]{2,1,0:T(8,128)} %reshape.289, s32[256,64]{1,0:T(8,128)S(1)} %bitcast.83), kind=kOutput, calls=%fused_computation.21 | convolution fusion | flops 806354944 | bytes 8454144 | tf_op jit(solution)/shard_map/rsj,rst->rjt/dot_general | solution.py:62
  210.3 8.2 %fusion.2 = f32[256,64,64]{2,1,0:T(8,128)S(1)} fusion(f32[256,64,64]{2,1,0:T(8,128)S(1)} %fusion.3, s32[256,64]{1,0:T(8,128)S(1)} %bitcast.84), kind=kOutput, calls=%fused_computation.20 | convolution fusion | flops 806354944 | bytes 8454144 | tf_op jit(solution)/shard_map/rjt,rtk->rjk/dot_general | solution.py:63
  218.5 11.0 %fusion = f32[64,64,64]{2,0,1:T(8,128)} fusion(f32[256,64,64]{2,1,0:T(8,128)S(1)} %fusion.2, f32[256]{0:T(256)S(1)} %convert_element_type.50, s32[256]{0:T(256)S(1)} %eq.56), kind=kOutput, calls=%fused_computation.17 | convolution fusion | flops 805339136 | bytes 5244928 | tf_op jit(solution)/shard_map/rp,rjk->pjk/dot_general | solution.py:65
  255.3 8.2 %collective-permute-done.4 = f32[16,64,128]{2,1,0:T(8,128)S(1)} collective-permute-done((f32[16,64,128]{2,1,0:T(8,128)}, f32[16,64,128]{2,1,0:T(8,128)S(1)}, u32[]{:S(2)}, u32[]{:S(2)}) %collective-permute-start.4) | collective-permute-done | bytes 524320 | tf_op jit(solution)/shard_map/ppermute | solution.py:14
  267.8 12.4 %collective-permute-done.5 = f32[16,64,128]{2,1,0:T(8,128)S(1)} collective-permute-done((f32[16,64,128]{2,1,0:T(8,128)S(1)}, f32[16,64,128]{2,1,0:T(8,128)S(1)}, u32[]{:S(2)}, u32[]{:S(2)}) %collective-permute-start.5) | collective-permute-done | bytes 524320 | tf_op jit(solution)/shard_map/ppermute | solution.py:14
  281.3 13.9 %multiply_reduce_fusion.4 = (f32[128]{0:T(128)S(1)}, f32[64,64,128]{2,1,0:T(8,128)}) fusion(f32[64,64,128]{2,1,0:T(8,128)S(1)} %copy-done.6, f32[64,64,128]{2,0,1:T(8,128)S(1)} %fusion.36, f32[64,64,128]{2,0,1:T(8,128)S(1)} %fusion.38, f32[64,64,128]{2,0,1:T(8,128)S(1)} %fusion.40, f32[64,64,128]{2,0,1:T(8,128)S(1)} %fusion.42, ...), kind=kOutput, calls=%fused_computation.48 | convolution fusion | flops 406847360 | bytes 13648384 | tf_op jit(solution)/shard_map/pij,pjr->pir/dot_general | solution.py:97
  295.2 38.3 %all-reduce = (f32[128]{0:T(128)S(1)}, f32[128]{0:T(128)S(1)}) all-reduce(f32[128]{0:T(128)S(1)} %fusion.6, f32[128]{0:T(128)S(1)} %get-tuple-element.18), channel_id=1, replica_groups=mesh['sector'=4,'axial'=8] {'sector','axial'}, use_global_device_ids=true, to_apply=%region_7.8 | all-reduce | flops 256 | bytes 2048 | tf_op jit(solution)/shard_map/psum | solution.py:88
  336.4 40.8 %psum.44 = f32[128]{0:T(128)S(1)} all-reduce(f32[128]{0:T(128)S(1)} %get-tuple-element.6), channel_id=1, replica_groups=mesh['sector'=4,'axial'=8] {'sector','axial'}, use_global_device_ids=true, to_apply=%region_11.12 | all-reduce | flops 128 | bytes 1024 | tf_op jit(solution)/shard_map/psum | solution.py:88
  398.2 4.3 collective-permute-done.8
  407.3 12.2 %collective-permute-done.9 = f32[16,64,128]{2,1,0:T(8,128)S(1)} collective-permute-done((f32[16,64,128]{2,1,0:T(8,128)S(1)}, f32[16,64,128]{2,1,0:T(8,128)S(1)}, u32[]{:S(2)}, u32[]{:S(2)}) %collective-permute-start.9) | collective-permute-done | bytes 524320 | tf_op jit(solution)/shard_map/ppermute | solution.py:14
  420.7 13.9 %multiply_reduce_fusion.2 = (f32[128]{0:T(128)S(1)}, f32[64,64,128]{2,1,0:T(8,128)}) fusion(f32[64,64,128]{2,1,0:T(8,128)S(1)} %copy-done.1, f32[64,64,128]{2,0,1:T(8,128)S(1)} %fusion.28, f32[64,64,128]{2,0,1:T(8,128)S(1)} %fusion.30, f32[64,64,128]{2,0,1:T(8,128)S(1)} %fusion.32, f32[64,64,128]{2,0,1:T(8,128)S(1)} %fusion.34, ...), kind=kOutput, calls=%fused_computation.44 | convolution fusion | flops 406847360 | bytes 13648384 | tf_op jit(solution)/shard_map/pij,pjr->pir/dot_general | solution.py:97
  434.6 39.9 %psum.45 = f32[128]{0:T(128)S(1)} all-reduce(f32[128]{0:T(128)S(1)} %get-tuple-element.20), channel_id=1, replica_groups=mesh['sector'=4,'axial'=8] {'sector','axial'}, use_global_device_ids=true, to_apply=%region_13.14 | all-reduce | flops 128 | bytes 1024 | tf_op jit(solution)/shard_map/psum | solution.py:116
  478.0 40.9 %psum.46 = f32[128]{0:T(128)S(1)} all-reduce(f32[128]{0:T(128)S(1)} %get-tuple-element.4), channel_id=1, replica_groups=mesh['sector'=4,'axial'=8] {'sector','axial'}, use_global_device_ids=true, to_apply=%region_15.16 | all-reduce | flops 128 | bytes 1024 | tf_op jit(solution)/shard_map/psum | solution.py:88
  518.9 3.6 multiply_add_fusion.1
  540.4 4.3 collective-permute-done.12
  549.5 12.2 %collective-permute-done.13 = f32[16,64,128]{2,1,0:T(8,128)S(1)} collective-permute-done((f32[16,64,128]{2,1,0:T(8,128)S(1)}, f32[16,64,128]{2,1,0:T(8,128)S(1)}, u32[]{:S(2)}, u32[]{:S(2)}) %collective-permute-start.13) | collective-permute-done | bytes 524320 | tf_op jit(solution)/shard_map/ppermute | solution.py:14
  562.9 13.9 %multiply_reduce_fusion = (f32[128]{0:T(128)S(1)}, f32[64,64,128]{2,1,0:T(8,128)}) fusion(f32[64,64,128]{2,1,0:T(8,128)S(1)} %copy-done.5, f32[64,64,128]{2,0,1:T(8,128)S(1)} %fusion.20, f32[64,64,128]{2,0,1:T(8,128)S(1)} %fusion.22, f32[64,64,128]{2,0,1:T(8,128)S(1)} %fusion.24, f32[64,64,128]{2,0,1:T(8,128)S(1)} %fusion.26, ...), kind=kOutput, calls=%fused_computation.40 | convolution fusion | flops 406847360 | bytes 13648384 | tf_op jit(solution)/shard_map/pij,pjr->pir/dot_general | solution.py:97
  576.8 39.7 %psum.47 = f32[128]{0:T(128)S(1)} all-reduce(f32[128]{0:T(128)S(1)} %get-tuple-element.22), channel_id=1, replica_groups=mesh['sector'=4,'axial'=8] {'sector','axial'}, use_global_device_ids=true, to_apply=%region_17.18 | all-reduce | flops 128 | bytes 1024 | tf_op jit(solution)/shard_map/psum | solution.py:116
  616.5 5.3 multiply_subtract_fusion
  (130 shorter events, 107.1 us)
Async XLA Ops:
  5.4 14.4 %all-to-all-start.1 = ((s32[32,8,1]{1,2,0:T(1,128)}), s32[32,8,1]{1,2,0:T(1,128)S(1)}, u32[]{:S(2)}, u32[]{:S(2)}) async-start(s32[32,8,1]{1,2,0:T(1,128)} %bitcast.5), calls=%async_computation.1 | async-start | bytes 32768 | tf_op jit(solution)/shard_map/all_to_all | solution.py:57
  19.8 9.9 %all-to-all-start = ((s32[32,8,1]{1,2,0:T(1,128)}), s32[32,8,1]{1,2,0:T(1,128)S(1)}, u32[]{:S(2)}, u32[]{:S(2)}) async-start(s32[32,8,1]{1,2,0:T(1,128)} %bitcast.3), calls=%async_computation | async-start | bytes 32768 | tf_op jit(solution)/shard_map/all_to_all | solution.py:56
  22.3 5.6 copy-start.8
  29.7 47.2 %all-to-all-start.2 = ((s32[32,1,512]{2,1,0:T(1,128)}), s32[32,1,512]{2,1,0:T(1,128)S(1)}, u32[]{:S(2)}, u32[]{:S(2)}) async-start(s32[32,1,512]{2,1,0:T(1,128)} %reshape.290), calls=%async_computation.2 | async-start | bytes 131072 | tf_op jit(solution)/shard_map/all_to_all | solution.py:55
  76.9 6.0 copy-start.7
  76.9 7.7 %copy-start.10 = (s32[2,16,2]{1,2,0:T(2,128)S(1)}, s32[2,16,2]{1,2,0:T(2,128)}, u32[]{:S(2)}) copy-start(s32[2,16,2]{1,2,0:T(2,128)} %param.17) | copy-start | bytes 772
  76.9 15.0 %copy-start.9 = (f32[4096]{0:T(1024)S(1)}, f32[4096]{0:T(1024)}, u32[]{:S(2)}) copy-start(f32[4096]{0:T(1024)} %param.16) | copy-start | bytes 49156
  76.9 100.0 %all-to-all-start.3 = ((f32[32,1,32768]{2,1,0:T(1,128)}), f32[32,1,32768]{2,1,0:T(1,128)}, u32[]{:S(2)}, u32[]{:S(2)}) async-start(f32[32,1,32768]{2,1,0:T(1,128)} %reshape.288), calls=%async_computation.3 | async-start | bytes 8388608 | tf_op jit(solution)/shard_map/all_to_all | solution.py:54
  82.9 151.7 %collective-permute-start.1 = (f32[16,64]{1,0:T(8,128)S(1)}, f32[16,64]{1,0:T(8,128)S(1)}, u32[]{:S(2)}, u32[]{:S(2)}) collective-permute-start(f32[16,64]{1,0:T(8,128)S(1)} %get-tuple-element.9), channel_id=1, source_target_pairs={{0,8},{8,16},{16,24},{24,0},{1,9},{9,17},{17,25},{25,1},{2,10},{10... | collective-permute-start | bytes 12296 | tf_op jit(solution)/shard_map/ppermute | solution.py:14
  84.6 149.9 %collective-permute-start = (s32[16]{0:T(128)S(1)}, s32[16]{0:T(128)S(1)}, u32[]{:S(2)}, u32[]{:S(2)}) collective-permute-start(s32[16]{0:T(128)S(1)} %get-tuple-element.13), channel_id=1, source_target_pairs={{0,8},{8,16},{16,24},{24,0},{1,9},{9,17},{17,25},{25,1},{2,10},{10... | collective-permute-start | bytes 200 | tf_op jit(solution)/shard_map/ppermute | solution.py:14
  86.1 148.8 %collective-permute-start.3 = (f32[16,64]{1,0:T(8,128)S(1)}, f32[16,64]{1,0:T(8,128)S(1)}, u32[]{:S(2)}, u32[]{:S(2)}) collective-permute-start(f32[16,64]{1,0:T(8,128)S(1)} %get-tuple-element.8), channel_id=1, source_target_pairs={{0,1},{1,2},{2,3},{3,4},{4,5},{5,6},{6,7},{8,9},{9,10},{10,11},{11... | collective-permute-start | bytes 12296 | tf_op jit(solution)/shard_map/ppermute | solution.py:20
  87.6 4.7 collective-permute-start.2
  229.6 5.6 copy-start
  239.8 11.4 %collective-permute-start.6 = (f32[16,64,128]{2,1,0:T(8,128)}, f32[16,64,128]{2,1,0:T(8,128)}, u32[]{:S(2)}, u32[]{:S(2)}) collective-permute-start(f32[16,64,128]{2,1,0:T(8,128)} %gather_fusion.4), channel_id=1, source_target_pairs={{1,0},{2,1},{3,2},{4,3},{5,4},{6,5},{7,6},{9,8},{10,9},{11,10},{12... | collective-permute-start | bytes 1572872 | tf_op jit(solution)/shard_map/ppermute | solution.py:20
  248.6 14.8 %collective-permute-start.4 = (f32[16,64,128]{2,1,0:T(8,128)}, f32[16,64,128]{2,1,0:T(8,128)S(1)}, u32[]{:S(2)}, u32[]{:S(2)}) collective-permute-start(f32[16,64,128]{2,1,0:T(8,128)} %gather_fusion.2), channel_id=1, source_target_pairs={{0,24},{8,0},{16,8},{24,16},{1,25},{9,1},{17,9},{25,17},{2,26},{10... | collective-permute-start | bytes 1572872 | tf_op jit(solution)/shard_map/ppermute | solution.py:14
  252.5 14.1 %collective-permute-start.7 = (f32[16,64,128]{2,1,0:T(8,128)S(1)}, f32[16,64,128]{2,1,0:T(8,128)S(1)}, u32[]{:S(2)}, u32[]{:S(2)}) collective-permute-start(f32[16,64,128]{2,1,0:T(8,128)S(1)} %subtract_multiply_fusion.4), channel_id=1, source_target_pairs={{0,1},{1,2},{2,3},{3,4},{4,5},{5,6},{6,7},{8,9},{9,10},{10,11},{11... | collective-permute-start | bytes 1572872 | tf_op jit(solution)/shard_map/ppermute | solution.py:20
  263.7 16.4 %collective-permute-start.5 = (f32[16,64,128]{2,1,0:T(8,128)S(1)}, f32[16,64,128]{2,1,0:T(8,128)S(1)}, u32[]{:S(2)}, u32[]{:S(2)}) collective-permute-start(f32[16,64,128]{2,1,0:T(8,128)S(1)} %subtract_multiply_fusion.5), channel_id=1, source_target_pairs={{0,8},{8,16},{16,24},{24,0},{1,9},{9,17},{17,25},{25,1},{2,10},{10... | collective-permute-start | bytes 1572872 | tf_op jit(solution)/shard_map/ppermute | solution.py:14
  266.5 14.7 %copy-start.2 = (f32[64,64,64]{2,0,1:T(8,128)S(1)}, f32[64,64,64]{2,0,1:T(8,128)}, u32[]{:S(2)}) copy-start(f32[64,64,64]{2,0,1:T(8,128)} %fusion) | copy-start | bytes 3145732
  266.6 14.7 %copy-start.6 = (f32[64,64,128]{2,1,0:T(8,128)S(1)}, f32[64,64,128]{2,1,0:T(8,128)}, u32[]{:S(2)}) copy-start(f32[64,64,128]{2,1,0:T(8,128)} %broadcast_divide_fusion) | copy-start | bytes 6291460
  383.3 10.2 %collective-permute-start.10 = (f32[16,64,128]{2,1,0:T(8,128)}, f32[16,64,128]{2,1,0:T(8,128)}, u32[]{:S(2)}, u32[]{:S(2)}) collective-permute-start(f32[16,64,128]{2,1,0:T(8,128)} %gather_fusion.8), channel_id=1, source_target_pairs={{1,0},{2,1},{3,2},{4,3},{5,4},{6,5},{7,6},{9,8},{10,9},{11,10},{12... | collective-permute-start | bytes 1572872 | tf_op jit(solution)/shard_map/ppermute | solution.py:20
  387.5 15.0 %collective-permute-start.8 = (f32[16,64,128]{2,1,0:T(8,128)}, f32[16,64,128]{2,1,0:T(8,128)}, u32[]{:S(2)}, u32[]{:S(2)}) collective-permute-start(f32[16,64,128]{2,1,0:T(8,128)} %gather_fusion.6), channel_id=1, source_target_pairs={{0,24},{8,0},{16,8},{24,16},{1,25},{9,1},{17,9},{25,17},{2,26},{10... | collective-permute-start | bytes 1572872 | tf_op jit(solution)/shard_map/ppermute | solution.py:14
  394.8 11.4 %collective-permute-start.11 = (f32[16,64,128]{2,1,0:T(8,128)S(1)}, f32[16,64,128]{2,1,0:T(8,128)S(1)}, u32[]{:S(2)}, u32[]{:S(2)}) collective-permute-start(f32[16,64,128]{2,1,0:T(8,128)S(1)} %subtract_multiply_fusion.2), channel_id=1, source_target_pairs={{0,1},{1,2},{2,3},{3,4},{4,5},{5,6},{6,7},{8,9},{9,10},{10,11},{11... | collective-permute-start | bytes 1572872 | tf_op jit(solution)/shard_map/ppermute | solution.py:20
  403.7 15.8 %collective-permute-start.9 = (f32[16,64,128]{2,1,0:T(8,128)S(1)}, f32[16,64,128]{2,1,0:T(8,128)S(1)}, u32[]{:S(2)}, u32[]{:S(2)}) collective-permute-start(f32[16,64,128]{2,1,0:T(8,128)S(1)} %subtract_multiply_fusion.3), channel_id=1, source_target_pairs={{0,8},{8,16},{16,24},{24,0},{1,9},{9,17},{17,25},{25,1},{2,10},{10... | collective-permute-start | bytes 1572872 | tf_op jit(solution)/shard_map/ppermute | solution.py:14
  406.1 14.6 %copy-start.1 = (f32[64,64,128]{2,1,0:T(8,128)S(1)}, f32[64,64,128]{2,1,0:T(8,128)}, u32[]{:S(2)}) copy-start(f32[64,64,128]{2,1,0:T(8,128)} %multiply_add_fusion.2) | copy-start | bytes 6291460
  406.2 14.6 %copy-start.3 = (f32[64,64,64]{2,0,1:T(8,128)S(1)}, f32[64,64,64]{2,0,1:T(8,128)}, u32[]{:S(2)}) copy-start(f32[64,64,64]{2,0,1:T(8,128)} %fusion) | copy-start | bytes 3145732
  525.5 10.3 %collective-permute-start.14 = (f32[16,64,128]{2,1,0:T(8,128)}, f32[16,64,128]{2,1,0:T(8,128)}, u32[]{:S(2)}, u32[]{:S(2)}) collective-permute-start(f32[16,64,128]{2,1,0:T(8,128)} %gather_fusion.12), channel_id=1, source_target_pairs={{1,0},{2,1},{3,2},{4,3},{5,4},{6,5},{7,6},{9,8},{10,9},{11,10},{12... | collective-permute-start | bytes 1572872 | tf_op jit(solution)/shard_map/ppermute | solution.py:20
  529.7 15.0 %collective-permute-start.12 = (f32[16,64,128]{2,1,0:T(8,128)}, f32[16,64,128]{2,1,0:T(8,128)}, u32[]{:S(2)}, u32[]{:S(2)}) collective-permute-start(f32[16,64,128]{2,1,0:T(8,128)} %gather_fusion.10), channel_id=1, source_target_pairs={{0,24},{8,0},{16,8},{24,16},{1,25},{9,1},{17,9},{25,17},{2,26},{10... | collective-permute-start | bytes 1572872 | tf_op jit(solution)/shard_map/ppermute | solution.py:14
  537.0 11.4 %collective-permute-start.15 = (f32[16,64,128]{2,1,0:T(8,128)S(1)}, f32[16,64,128]{2,1,0:T(8,128)S(1)}, u32[]{:S(2)}, u32[]{:S(2)}) collective-permute-start(f32[16,64,128]{2,1,0:T(8,128)S(1)} %subtract_multiply_fusion), channel_id=1, source_target_pairs={{0,1},{1,2},{2,3},{3,4},{4,5},{5,6},{6,7},{8,9},{9,10},{10,11},{11... | collective-permute-start | bytes 1572872 | tf_op jit(solution)/shard_map/ppermute | solution.py:20
  545.9 15.8 %collective-permute-start.13 = (f32[16,64,128]{2,1,0:T(8,128)S(1)}, f32[16,64,128]{2,1,0:T(8,128)S(1)}, u32[]{:S(2)}, u32[]{:S(2)}) collective-permute-start(f32[16,64,128]{2,1,0:T(8,128)S(1)} %subtract_multiply_fusion.1), channel_id=1, source_target_pairs={{0,8},{8,16},{16,24},{24,0},{1,9},{9,17},{17,25},{25,1},{2,10},{10... | collective-permute-start | bytes 1572872 | tf_op jit(solution)/shard_map/ppermute | solution.py:14
  548.3 14.6 %copy-start.4 = (f32[64,64,64]{2,0,1:T(8,128)S(1)}, f32[64,64,64]{2,0,1:T(8,128)}, u32[]{:S(2)}) copy-start(f32[64,64,64]{2,0,1:T(8,128)} %fusion) | copy-start | bytes 3145732
  548.3 14.6 %copy-start.5 = (f32[64,64,128]{2,1,0:T(8,128)S(1)}, f32[64,64,128]{2,1,0:T(8,128)}, u32[]{:S(2)}) copy-start(f32[64,64,128]{2,1,0:T(8,128)} %multiply_add_fusion.1) | copy-start | bytes 6291460
where the time goes:
time: 633 us; the launch traced here: 622 us
  blocking collectives  200 us (32%)
  waiting for transfers between devices  141 us (22%)
  matrix products  95.7 us (15%)
  local copies, waits for them, and re-layouts  89.2 us (14%)
  starting transfers between devices  49.5 us (8%)
  other arithmetic  44.9 us (7%)
    psum x3, blocking collectives, precond_sum(): lax.psum(jnp.sum(remaining_imbalance * precond, axis=(0, 1)), ('sector',...  120 us
    all_to_all x1, waiting for transfers between devices, shards(): lax.all_to_all(send_blocks, ('sector', 'axial'), split_axis=0, concat_axi...  81.8 us
    psum x2, blocking collectives, shards(): lax.psum(jnp.sum(update_vector * result, axis=(0, 1)), ('sector', 'axial'))  79.6 us
    ppermute x8, waiting for transfers between devices, from_behind(): lax.ppermute(array, axis, [(i, (i + by) % length) for i in range(length)])  53.5 us
    dot_general x3, matrix products, shards(): jnp.einsum('pij,pjr->pir', assembled, update_vector, precision=highest)  41.7 us
    unnamed x28, local copies, waits for them, and re-layouts  23.7 us
    scatter x1, local copies, waits for them, and re-layouts, shards(): jnp.zeros((total_slots, bound_nodes, bound_nodes), jnp.float32).at[target]  19.4 us
    ppermute x8, starting transfers between devices, shifted(): return lax.ppermute(block, axis, route)  18.9 us
  transfers between devices with their start and end apart: 20, of which 9 were waited for; matrix products, arithmetic and copies ran while one was open for 24% of the time, Pallas kernels for 0%

commit v1 on v0

v1 whole, which is shorter than its diff:
```python
import functools
import jax
import jax.numpy as jnp
from jax import lax
from jax.experimental import pallas as pl
from jax.experimental.pallas import tpu as pltpu
from jax.sharding import PartitionSpec as P

AXES = ("sector", "axial")
F32 = jnp.float32
BF16 = jnp.bfloat16
VMEM = pl.BlockSpec(memory_space=pltpu.VMEM)
SMEM = pl.BlockSpec(memory_space=pltpu.SMEM)
NT = (((1,), (1,)), ((), ()))
CHUNK = 8


def struct(*shape, dtype=F32):
    return jax.ShapeDtypeStruct(shape, dtype)


def iota(shape, dim):
    return lax.broadcasted_iota(jnp.int32, shape, dim)


def split(value):
    high = value.astype(BF16)
    return high, (value - high.astype(F32)).astype(BF16)


def dot(left, right, dims=(((1,), (0,)), ((), ()))):
    return lax.dot_general(left, right, dims, preferred_element_type=F32)


def pack_kernel(slots_each, owners, patches, counts, kbb, inner, nodes, payload, meta, blocks, node_rows, tally):
    step = pl.program_id(0)
    chunk, bn, _ = inner.shape
    half, quarter = bn // 2, bn // 4
    elems = kbb.shape[2]

    @pl.when(step == 0)
    def _():
        for i in range(half):
            blocks[pl.ds(i, elems, stride=half), :] = jnp.concatenate([kbb[i], kbb[i + half]], axis=0).T
        node_rows[...] = nodes[...].T
        meta[...] = jnp.zeros_like(meta)

        def clear(i, carry):
            tally[i] = 0
            return carry

        lax.fori_loop(0, meta.shape[0] // slots_each, clear, 0)

    row_id = iota((bn, bn), 0)
    col_id = iota((bn, bn), 1)
    lower = (row_id > col_id)[:half, :half]
    upper = (row_id < col_id)[:half, :half]
    lane = iota((1, 128), 1)
    for e in range(chunk):
        index = step * chunk + e
        both = blocks[pl.ds(pl.multiple_of(index * half, half), half), :]
        block = jnp.concatenate([both[:, :bn], both[:, bn:]], axis=0)
        coupling = inner[e]
        block = block - dot(coupling, coupling, NT)
        high, low = split(block)
        pick = (node_rows[pl.ds(index, 1), :] == row_id).astype(F32).astype(BF16)
        left = dot(jnp.concatenate([pick, pick], axis=1), jnp.concatenate([high, low], axis=0))
        high, low = split(left)
        placed = dot(high, pick, NT) + dot(low, pick, NT)
        triangles = jnp.where(lower, placed[:half, :half], jnp.where(upper, placed[half:, half:], 0.0))
        packed = jnp.concatenate([triangles, placed[:half, half:]], axis=1)
        packed = jnp.concatenate([packed[:quarter], packed[quarter:]], axis=1)
        diag = jnp.sum(jnp.where(row_id == col_id, placed, 0.0), axis=0, keepdims=True)
        owner = owners[index]
        rank = tally[owner]
        tally[owner] = rank + 1
        slot = owner * slots_each + rank
        payload[pl.ds(pl.multiple_of(slot * quarter, quarter), quarter), :] = packed
        tag = jnp.where(index < counts[0], patches[index] + 1, 0).astype(F32)
        meta[pl.ds(slot, 1), :] = jnp.where(lane < bn, jnp.concatenate([diag, diag], axis=1), jnp.where(lane == bn, tag, 0.0))


def pack_call(devices, owners, patches, counts, kbb, inner, nodes):
    elems, bn, ni = inner.shape
    slots_each = 2 * elems // devices
    slots = devices * slots_each
    whole = lambda *shape: pl.BlockSpec(shape, lambda i: (0,) * len(shape))
    return pl.pallas_call(
        functools.partial(pack_kernel, slots_each),
        grid=(elems // CHUNK,),
        in_specs=[
            SMEM,
            SMEM,
            SMEM,
            whole(bn, bn, elems),
            pl.BlockSpec((CHUNK, bn, ni), lambda i: (i, 0, 0)),
            whole(bn, elems),
        ],
        out_specs=[whole(slots * bn // 4, 128), whole(slots, 128)],
        out_shape=[struct(slots * bn // 4, 128), struct(slots, 128)],
        scratch_shapes=[
            pltpu.VMEM((elems * bn // 2, 128), F32),
            pltpu.VMEM((elems, bn), jnp.int32),
            pltpu.SMEM((devices,), jnp.int32),
        ],
        name="pack",
    )(owners, patches, counts, kbb, inner, nodes)


def send_values(picked, gains, field, sends):
    count = sends[0].shape[0]
    for which, send in enumerate(sends):

        def one(k, carry):
            send[k] = gains[which * count + k] * field[picked[which * count + k]]
            return carry

        lax.fori_loop(0, count, one, 0, unroll=2)


def take_values(placed, received, result):
    count = received[0].shape[0]
    for which, got in enumerate(received):

        def one(k, carry):
            patch = placed[which * count + k]
            result[patch] = result[patch] - got[k]
            return carry

        lax.fori_loop(0, count, one, 0, unroll=2)


def diagonal_kernel(tags, picked, meta, capacity, gain_rows, loads, inverse, gains, field, s0, s1, s2, s3, total):
    patch_dev, bn = capacity.shape
    total[pl.ds(0, patch_dev), :] = jnp.concatenate([capacity[...], capacity[...]], axis=1)

    def add(i, carry):
        patch = tags[i]
        total[pl.ds(patch, 1), :] = total[pl.ds(patch, 1), :] + meta[pl.ds(i, 1), :]
        return carry

    lax.fori_loop(0, meta.shape[0], add, 0, unroll=4)

    def link(i, carry):
        patch = picked[i]
        total[pl.ds(patch, 1), :] = total[pl.ds(patch, 1), :] + gain_rows[pl.ds(i, 1), :]
        return carry

    lax.fori_loop(0, gain_rows.shape[0], link, 0, unroll=4)
    columns = (1.0 / total[pl.ds(0, patch_dev), :][:, :bn]).T
    for p in range(patch_dev):
        column = jnp.broadcast_to(columns[:, p : p + 1], (bn, 128))
        inverse[p] = column
        field[p] = column * loads[p]
    columns = gain_rows[...][:, :bn].T
    for k in range(gain_rows.shape[0]):
        gains[k] = jnp.broadcast_to(columns[:, k : k + 1], (bn, 128))
    send_values(picked, gains, field, (s0, s1, s2, s3))


def times_blocks(blocks, value):
    high, low = split(value)
    return dot(blocks, jnp.concatenate([high, high, low], axis=0))


def folded(value):
    rows = value.shape[0]
    total = value[0:8]
    for i in range(8, rows, 8):
        total = total + value[i : i + 8]
    return total


def publish(partial, sums):
    rows = [jnp.sum(s[...], axis=0, keepdims=True) for s in sums]
    block = jnp.concatenate(rows + [jnp.zeros((8 - len(rows), 128), F32)], axis=0)

    def one(d, carry):
        partial[d] = block
        return carry

    lax.fori_loop(0, partial.shape[0], one, 0)


def gathered(received):
    return jnp.sum(received[...], axis=0)


def assemble_kernel(
    tags, picked, placed, payload, loads, field, inverse, gains, g0, g1, g2, g3,
    blocks, image, after, s0, s1, s2, s3, partial, packed, sum0, sum1,
):
    patch_dev, bn, _ = loads.shape
    half, quarter = bn // 2, bn // 4
    packed[...] = jnp.zeros_like(packed)

    def add(i, carry):
        patch = tags[i]
        packed[patch] = packed[patch] + payload[pl.ds(pl.multiple_of(i * quarter, quarter), quarter), :]
        return carry

    lax.fori_loop(0, tags.shape[0], add, 0, unroll=4)
    row_id = iota((half, bn), 0)
    col_id = iota((half, bn), 1)

    def build(p, carry):
        both = packed[p]
        rows = jnp.concatenate([both[:, :bn], both[:, bn:]], axis=0)
        top = jnp.where((col_id >= half) | (row_id > col_id), rows, 0.0)
        second = jnp.where((col_id < half) & (row_id < col_id), rows, 0.0)
        second = jnp.concatenate([jnp.zeros((half, half), F32), second[:, :half]], axis=1)
        whole = jnp.concatenate([top, second], axis=0)
        high, low = split(whole + whole.T)
        three = jnp.concatenate([high, low, high], axis=1)
        blocks[p] = three
        image[p] = loads[p] + times_blocks(three, field[p])
        return carry

    lax.fori_loop(0, patch_dev, build, 0, unroll=2)
    take_values(placed, (g0, g1, g2, g3), image)
    sum0[...] = jnp.zeros_like(sum0)
    sum1[...] = jnp.zeros_like(sum1)

    def finish(p, carry):
        here, value = image[p], field[p]
        after[p] = inverse[p] * here
        sum0[...] += folded(loads[p] * value)
        sum1[...] += folded(here * value)
        return carry

    lax.fori_loop(0, patch_dev, finish, 0, unroll=2)
    send_values(picked, gains, after, (s0, s1, s2, s3))
    publish(partial, (sum0, sum1))


def local_kernel(blocks, field, result):
    def one(p, carry):
        result[p] = times_blocks(blocks[p], field[p])
        return carry

    lax.fori_loop(0, field.shape[0], one, 0, unroll=2)


def second_kernel(picked, placed, local, image, inverse, gains, g0, g1, g2, g3, result, after, s0, s1, s2, s3):
    def one(p, carry):
        result[p] = image[p] + local[p]
        return carry

    lax.fori_loop(0, local.shape[0], one, 0, unroll=2)
    take_values(placed, (g0, g1, g2, g3), result)

    def scale(p, carry):
        after[p] = inverse[p] * result[p]
        return carry

    lax.fori_loop(0, local.shape[0], scale, 0, unroll=2)
    send_values(picked, gains, after, (s0, s1, s2, s3))


def first_step_kernel(sums, loads, field, image, second, inverse, left, left_image, left_scaled, partial, a0, a1, a2):
    first = gathered(sums)
    alpha = first[0:1] / first[1:2]
    a0[...] = jnp.zeros_like(a0)
    a1[...] = jnp.zeros_like(a1)
    a2[...] = jnp.zeros_like(a2)

    def one(p, carry):
        r = loads[p] - alpha * image[p]
        w = image[p] - alpha * second[p]
        u = inverse[p] * r
        left[p] = r
        left_image[p] = w
        left_scaled[p] = u
        a0[...] += folded(r * u)
        a1[...] += folded(u * w)
        a2[...] += folded(u * image[p] + field[p] * w)
        return carry

    lax.fori_loop(0, loads.shape[0], one, 0, unroll=2)
    publish(partial, (a0, a1, a2))


def second_step_kernel(
    sums0, sums1, placed, local, g0, g1, g2, g3, field, image, second, r1, w1, u1, inverse,
    r2_out, w2_out, s1_out, p1_out, u2_out, partial, third, a0, a1, a2,
):
    patch_dev = local.shape[0]
    first, then = gathered(sums0), gathered(sums1)
    alpha0 = first[0:1] / first[1:2]
    beta1 = then[0:1] / first[0:1]
    alpha1 = then[0:1] / (then[1:2] + beta1 * (then[2:3] + beta1 * first[1:2]))

    def start(p, carry):
        third[p] = second[p] + local[p]
        return carry

    lax.fori_loop(0, patch_dev, start, 0, unroll=2)
    take_values(placed, (g0, g1, g2, g3), third)
    a0[...] = jnp.zeros_like(a0)
    a1[...] = jnp.zeros_like(a1)
    a2[...] = jnp.zeros_like(a2)

    def one(p, carry):
        n0, w = second[p], w1[p]
        s1 = w + beta1 * image[p]
        z1 = (n0 - alpha0 * third[p]) + beta1 * n0
        r2 = r1[p] - alpha1 * s1
        w2 = w - alpha1 * z1
        u2 = inverse[p] * r2
        p1 = u1[p] + beta1 * field[p]
        r2_out[p] = r2
        w2_out[p] = w2
        s1_out[p] = s1
        p1_out[p] = p1
        u2_out[p] = u2
        a0[...] += folded(r2 * u2)
        a1[...] += folded(u2 * w2)
        a2[...] += folded(u2 * s1 + p1 * w2)
        return carry

    lax.fori_loop(0, patch_dev, one, 0)
    publish(partial, (a0, a1, a2))


def last_kernel(sums0, sums1, sums2, field, r2, w2, s1, p1, u2, estimate, left):
    first, then, last = gathered(sums0), gathered(sums1), gathered(sums2)
    alpha0 = first[0:1] / first[1:2]
    beta1 = then[0:1] / first[0:1]
    curve1 = then[1:2] + beta1 * (then[2:3] + beta1 * first[1:2])
    alpha1 = then[0:1] / curve1
    beta2 = last[0:1] / then[0:1]
    alpha2 = last[0:1] / (last[1:2] + beta2 * (last[2:3] + beta2 * curve1))

    def one(p, carry):
        direction = u2[p] + beta2 * p1[p]
        estimate[p] = alpha0 * field[p] + alpha1 * p1[p] + alpha2 * direction
        left[p] = r2[p] - alpha2 * (w2[p] + beta2 * s1[p])
        return carry

    lax.fori_loop(0, field.shape[0], one, 0, unroll=2)


def call(kernel, name, ins, outs, scratch=(), flops=0):
    ints = lambda a: a.ndim == 1 and a.dtype == jnp.int32
    moved = sum(a.size * a.dtype.itemsize for a in ins) + sum(s.size * s.dtype.itemsize for s in outs)
    return pl.pallas_call(
        kernel,
        in_specs=[SMEM if ints(a) else VMEM for a in ins],
        out_specs=[VMEM] * len(outs),
        out_shape=list(outs),
        scratch_shapes=list(scratch),
        cost_estimate=pl.CostEstimate(flops=flops, bytes_accessed=moved, transcendentals=0),
        name=name,
    )(*ins)


def everywhere(partial):
    return lax.all_to_all(partial, AXES, split_axis=0, concat_axis=0, tiled=True)


def onward(value, axis, wrap):
    n = lax.axis_size(axis)
    return lax.ppermute(value, axis, [(i, (i + 1) % n) for i in range(n) if wrap or i + 1 < n])


def back(value, axis, wrap):
    n = lax.axis_size(axis)
    return lax.ppermute(value, axis, [((i + 1) % n, i) for i in range(n) if wrap or i + 1 < n])


def exchange(s0, s1, s2, s3):
    return (
        onward(s0, "sector", True),
        back(s1, "sector", True),
        onward(s2, "axial", False),
        back(s3, "axial", False),
    )


def shards(kbb, interior, node_lists, owners, patch_ids, counts, capacity, links, conduct, loads):
    elems, bn = node_lists.shape
    devices = lax.axis_size("sector") * lax.axis_size("axial")
    points, cases = loads.shape
    patch_dev = points // bn
    count = conduct.shape[1]

    sent = jnp.concatenate(
        [conduct, links[:, :, 1:].astype(F32), jnp.zeros((2, count, 127 - bn), F32)], axis=2
    )
    from_sector = onward(sent[0], "sector", True)
    from_axial = onward(sent[1], "axial", False)
    own, far = links[:, :, 0], links[:, :, 1]
    far_sector = from_sector[:, bn].astype(jnp.int32)
    far_axial = from_axial[:, bn].astype(jnp.int32)
    picked = jnp.concatenate([own[0], far_sector, own[1], far_axial])
    placed = jnp.concatenate([far_sector, own[0], far_axial, own[1]])
    gain_rows = jnp.concatenate([sent[0], from_sector, sent[1], from_axial])

    payload, meta = pack_call(
        devices, owners.reshape(elems), patch_ids, counts,
        kbb.transpose(1, 2, 0), interior.transpose(0, 2, 1), node_lists.T,
    )
    slots = meta.shape[0]
    meta = everywhere(meta.reshape(devices, slots // devices, 128)).reshape(slots, 128)
    tags = meta[:, bn].astype(jnp.int32)
    tags = jnp.where(tags > 0, tags - 1, patch_dev)
    payload = everywhere(payload.reshape(devices, -1, 128)).reshape(slots * bn // 4, 128)

    loads = loads.reshape(patch_dev, bn, cases)
    vec = struct(patch_dev, bn, cases)
    buf = struct(count, bn, cases)
    total = struct(devices, 8, cases)
    acc = pltpu.VMEM((8, cases), F32)
    inverse, gains, field, *sends = call(
        diagonal_kernel, "diagonal",
        (tags, picked, meta, capacity.reshape(patch_dev, bn), gain_rows, loads),
        (vec, struct(4 * count, bn, cases), vec, buf, buf, buf, buf),
        (pltpu.VMEM((patch_dev + 8, 128), F32),),
    )
    got = exchange(*sends)
    blocks, image, after, *rest = call(
        assemble_kernel, "assemble",
        (tags, picked, placed, payload, loads, field, inverse, gains, *got),
        (struct(patch_dev, bn, 3 * bn, dtype=BF16), vec, vec, buf, buf, buf, buf, total),
        (pltpu.VMEM((patch_dev + 1, bn // 4, 128), F32), acc, acc),
    )
    *sends, partial = rest
    got = exchange(*sends)
    sums0 = everywhere(partial)
    (local,) = call(local_kernel, "local", (blocks, after), (vec,))
    second, after, *sends = call(
        second_kernel, "second",
        (picked, placed, local, image, inverse, gains, *got),
        (vec, vec, buf, buf, buf, buf),
    )
    got = exchange(*sends)
    r1, w1, u1, partial = call(
        first_step_kernel, "first_step",
        (sums0, loads, field, image, second, inverse), (vec, vec, vec, total), (acc, acc, acc),
    )
    sums1 = everywhere(partial)
    (local,) = call(local_kernel, "local", (blocks, after), (vec,))
    r2, w2, s1, p1, u2, partial = call(
        second_step_kernel, "second_step",
        (sums0, sums1, placed, local, *got, field, image, second, r1, w1, u1, inverse),
        (vec, vec, vec, vec, vec, total),
        (pltpu.VMEM((patch_dev, bn, cases), F32), acc, acc, acc),
    )
    sums2 = everywhere(partial)
    estimate, left = call(
        last_kernel, "last", (sums0, sums1, sums2, field, r2, w2, s1, p1, u2), (vec, vec)
    )
    return estimate.reshape(points, cases), left.reshape(points, cases)


def solution(mesh):
    wide = P(AXES, None)
    deep = P(AXES, None, None)
    return jax.shard_map(
        shards,
        mesh=mesh,
        in_specs=(
            deep, deep, wide, wide, P(AXES), P(AXES), P(AXES),
            P(None, AXES, None), P(None, AXES, None), wide,
        ),
        out_specs=(wide, wide),
        check_vma=False,
    )
```

time: 633 us -> 283 us (0.45); the launches traced: 622 us -> 283 us
  blocking collectives: 200 us -> 56.7 us
  Pallas kernels: 0 us -> 119 us
  matrix products: 95.7 us -> 0 us
  local copies, waits for them, and re-layouts: 89.2 us -> 5.51 us
  waiting for transfers between devices: 141 us -> 63.3 us
  other arithmetic: 44.9 us -> 2.48 us
  starting transfers between devices: 49.5 us -> 34.6 us
    psum x5 -> x0, blocking collectives: 200 us -> none  [the longest x3 120 us: precond_sum(): lax.psum(jnp.sum(remaining_imbalance * precond, axis=(0, 1)), ('sector',...]
    pallas_call x0 -> x9, Pallas kernels: none -> 119 us  [the longest x8 87.2 us: call(): pl.pallas_call(kernel, in_specs=[SMEM if ints(a) else VMEM for a in ins],...]
    dot_general x23 -> x0, matrix products: 95.7 us -> none  [the longest x3 41.7 us: shards(): jnp.einsum('pij,pjr->pir', assembled, update_vector, precision=highest)]
    all_to_all x4 -> x2, waiting for transfers between devices: 87 us -> 0.01 us  [everywhere(): lax.all_to_all(partial, AXES, split_axis=0, concat_axis=0, tiled=True)]
    all_to_all x0 -> x3, blocking collectives: none -> 56.7 us  [everywhere(): lax.all_to_all(partial, AXES, split_axis=0, concat_axis=0, tiled=True)]
    gather x14 -> x0, local copies, waits for them, and re-layouts: 32.5 us -> none  [the longest x3 8.92 us: shards(): beyond = from_behind(update_vector[sector_in_far], 'sector', -1)]
    scatter x4 -> x0, local copies, waits for them, and re-layouts: 22.4 us -> none  [the longest x1 19.4 us: shards(): jnp.zeros((total_slots, bound_nodes, bound_nodes), jnp.float32).at[target]]
    unnamed x28 -> x36, local copies, waits for them, and re-layouts: 23.7 us -> 4.65 us
  transfers between devices with their start and end apart: 20 -> 16, of which waited for: 9 -> 5; matrix products, arithmetic and copies ran while one was open for 24% -> 1% of each run, Pallas kernels for 0% -> 12%
where the time goes in v1:
time: 283 us
  Pallas kernels  119 us (42%)
  waiting for transfers between devices  63.3 us (22%)
  blocking collectives  56.7 us (20%)
  starting transfers between devices  34.6 us (12%)
  local copies, waits for them, and re-layouts  5.51 us (2%)
    pallas_call x8, Pallas kernels, call(): pl.pallas_call(kernel, in_specs=[SMEM if ints(a) else VMEM for a in ins],...  87.2 us
    all_to_all x3, blocking collectives, everywhere(): lax.all_to_all(partial, AXES, split_axis=0, concat_axis=0, tiled=True)  56.7 us
    ppermute x8, waiting for transfers between devices, onward(): lax.ppermute(value, axis, [(i, (i + 1) % n) for i in range(n) if wrap or...  45.7 us
    pallas_call x1, Pallas kernels, pack_call(): pl.pallas_call(functools.partial(pack_kernel, slots_each), grid=(elems //...  31.6 us
    ppermute x8, starting transfers between devices, onward(): lax.ppermute(value, axis, [(i, (i + 1) % n) for i in range(n) if wrap or...  21.8 us
    ppermute x6, waiting for transfers between devices, back(): lax.ppermute(value, axis, [((i + 1) % n, i) for i in range(n) if wrap or...  17.6 us
    ppermute x6, starting transfers between devices, back(): lax.ppermute(value, axis, [((i + 1) % n, i) for i in range(n) if wrap or...  7.32 us
  transfers between devices with their start and end apart: 16, of which 5 were waited for; matrix products, arithmetic and copies ran while one was open for 1% of the time, Pallas kernels for 12%

profile of v1, /device:TPU:0, one launch (start us, length us, event | category | flops | bytes accessed | tf_op | source)
XLA Modules:
  0.0 282.8 jit_solution(17092490195745091666)
XLA Ops:
  1.3 31.6 %pack.1 = (f32[4096,128]{1,0:T(8,128)}, f32[256,128]{1,0:T(8,128)}) custom-call(s32[128]{0:T(128)} %bitcast.32, s32[128]{0:T(128)} %patches.1, s32[1]{0:T(128)S(6)} %copy.17.counts, f32[64,64,128]{2,1,0:T(8,128)} %bitcast.25, bf16[128,64,256]{2,1,0:T(8,128)(2,1)} %bitcast.24, s32[64,128]{1,0:T(8,128)} %bitcast.30), custom_call_target="tpu_custom_call" | custom-call | tf_op jit(solution)/shard_map/pack/pallas_call | solution.py:88
  32.9 15.5 %all_to_all.25 = f32[32,8,128]{2,1,0:T(8,128)S(1)} all-to-all(f32[32,8,128]{2,1,0:T(8,128)} %bitcast.29), channel_id=1, replica_groups=mesh['sector'=4,'axial'=8] {'sector','axial'}, dimensions={0} | all-to-all | bytes 262144 | tf_op jit(solution)/shard_map/all_to_all | solution.py:358
  48.4 2.9 %all-to-all-start.1 = ((f32[32,128,128]{2,1,0:T(8,128)}), f32[32,128,128]{2,1,0:T(8,128)S(1)}, u32[]{:S(2)}, u32[]{:S(2)}) async-start(f32[32,128,128]{2,1,0:T(8,128)} %bitcast.26), calls=%async_computation.1 | async-start | bytes 4194304 | tf_op jit(solution)/shard_map/all_to_all | solution.py:358
  51.6 1.7 collective-permute-start
  53.3 1.8 collective-permute-start.1
  55.7 34.4 %collective-permute-done = f32[16,128]{1,0:T(8,128)S(1)} collective-permute-done((f32[16,128]{1,0:T(8,128)S(1)}, f32[16,128]{1,0:T(8,128)S(1)}, u32[]{:S(2)}, u32[]{:S(2)}) %collective-permute-start) | collective-permute-done | bytes 8224 | tf_op jit(solution)/shard_map/ppermute | solution.py:363
  92.6 8.2 %diagonal.1 = (f32[64,64,128]{2,1,0:T(8,128)}, f32[64,64,128]{2,1,0:T(8,128)}, f32[64,64,128]{2,1,0:T(8,128)}, f32[16,64,128]{2,1,0:T(8,128)}, f32[16,64,128]{2,...) custom-call(s32[256]{0:T(256)} %select_reduce_fusion.tags, s32[64]{0:T(128)} %get-tuple-element.75.picked, ...), custom_call_target="tpu_custom_call" | custom-call | bytes 10667264 | tf_op jit(solution)/shard_map/diagonal/pallas_call | solution.py:346
  100.8 8.9 %collective-permute-start.2 = (f32[16,64,128]{2,1,0:T(8,128)}, f32[16,64,128]{2,1,0:T(8,128)S(1)}, u32[]{:S(2)}, u32[]{:S(2)}) collective-permute-start(f32[16,64,128]{2,1,0:T(8,128)} %get-tuple-element.42), channel_id=1, source_target_pairs={{0,8},{8,16},{16,24},{24,0},{1,9},{9,17},{17,25},{25,1},{2,10},{10... | collective-permute-start | bytes 1572872 | tf_op jit(solution)/shard_map/ppermute | solution.py:363
  109.7 1.6 collective-permute-start.4
  111.3 1.3 collective-permute-start.5
  112.6 9.7 %collective-permute-done.2.g0 = f32[16,64,128]{2,1,0:T(8,128)S(1)} collective-permute-done((f32[16,64,128]{2,1,0:T(8,128)}, f32[16,64,128]{2,1,0:T(8,128)S(1)}, u32[]{:S(2)}, u32[]{:S(2)}) %collective-permute-start.2) | collective-permute-done | bytes 524320 | tf_op jit(solution)/shard_map/ppermute | solution.py:363
  122.3 10.3 %collective-permute-done.3.g1 = f32[16,64,128]{2,1,0:T(8,128)S(1)} collective-permute-done((f32[16,64,128]{2,1,0:T(8,128)}, f32[16,64,128]{2,1,0:T(8,128)S(1)}, u32[]{:S(2)}, u32[]{:S(2)}) %collective-permute-start.3) | collective-permute-done | bytes 524320 | tf_op jit(solution)/shard_map/ppermute | solution.py:368
  134.8 23.7 %assemble.1 = (bf16[64,64,192]{2,1,0:T(8,128)(2,1)}, f32[64,64,128]{2,1,0:T(8,128)}, f32[64,64,128]{2,1,0:T(8,128)}, f32[16,64,128]{2,1,0:T(8,128)}, f32[16,64,1...) custom-call(s32[256]{0:T(256)} %select_reduce_fusion.tags, ...), custom_call_target="tpu_custom_call" | custom-call | bytes 20579840 | tf_op jit(solution)/shard_map/assemble/pallas_call | solution.py:346
  158.5 2.4 collective-permute-start.6
  160.9 2.0 collective-permute-start.7
  163.0 1.3 collective-permute-start.8
  164.3 1.3 collective-permute-start.9
  165.6 8.8 %local.2 = f32[64,64,128]{2,1,0:T(8,128)} custom-call(bf16[64,64,192]{2,1,0:T(8,128)(2,1)} %get-tuple-element.48.blocks, f32[64,64,128]{2,1,0:T(8,128)} %get-tuple-element.49.field), custom_call_target="tpu_custom_call" | custom-call | bytes 5767168 | tf_op jit(solution)/shard_map/local/pallas_call | solution.py:346
  174.4 1.6 collective-permute-done.6.g0
  176.0 7.3 %collective-permute-done.7.g1 = f32[16,64,128]{2,1,0:T(8,128)S(1)} collective-permute-done((f32[16,64,128]{2,1,0:T(8,128)}, f32[16,64,128]{2,1,0:T(8,128)S(1)}, u32[]{:S(2)}, u32[]{:S(2)}) %collective-permute-start.7) | collective-permute-done | bytes 524320 | tf_op jit(solution)/shard_map/ppermute | solution.py:368
  184.4 8.0 %second.1 = (f32[64,64,128]{2,1,0:T(8,128)}, f32[64,64,128]{2,1,0:T(8,128)}, f32[16,64,128]{2,1,0:T(8,128)}, f32[16,64,128]{2,1,0:T(8,128)}, f32[16,64,128]{2,1,0:T(8,128)}, /*index=5*/f32[16,64,128]{2,1,0:T(8,128)}) custom-call(s32[64]{0:T(128)} %get-tuple-element.75.picked, s32[64]{0:T(128)} %get-tuple-element.74.placed, f32[64,64,128]{2,1,0:T(8,128)} %local.2, ...), custom_call_target="tpu_custom_call" | custom-call | bytes 16777728 | tf_op jit(solution)/shard_map/second/pallas_call | solution.py:346
  192.5 2.7 collective-permute-start.10
  195.2 1.4 collective-permute-start.11
  196.6 1.3 collective-permute-start.12
  197.9 1.3 collective-permute-start.13
  199.2 27.0 %all_to_all.26.sums.sums0 = f32[32,8,128]{2,1,0:T(8,128)} all-to-all(f32[32,8,128]{2,1,0:T(8,128)S(1)} %copy-done.14), channel_id=1, replica_groups=mesh['sector'=4,'axial'=8] {'sector','axial'}, dimensions={0} | all-to-all | bytes 262144 | tf_op jit(solution)/shard_map/all_to_all | solution.py:358
  226.2 8.3 %first_step.1 = (f32[64,64,128]{2,1,0:T(8,128)}, f32[64,64,128]{2,1,0:T(8,128)}, f32[64,64,128]{2,1,0:T(8,128)}, f32[32,8,128]{2,1,0:T(8,128)}) custom-call(f32[32,8,128]{2,1,0:T(8,128)} %all_to_all.26.sums.sums0, f32[64,64,128]{2,1,0:T(8,128)} %bitcast.22, f32[64,64,128]{2,1,0:T(8,128)} %get-tuple-element.39.field, f32[64,64,128]{2,1,0:T(8,128)} %get-tuple-element.47.image, ...), custom_call_target="tpu_custom_call" | custom-call | bytes 17039360 | tf_op jit(solution)/shard_map/first_step/pallas_call | solution.py:346
  234.5 2.6 all-to-all-start.3
  237.1 8.8 %local.3 = f32[64,64,128]{2,1,0:T(8,128)} custom-call(bf16[64,64,192]{2,1,0:T(8,128)(2,1)} %get-tuple-element.48.blocks, f32[64,64,128]{2,1,0:T(8,128)} %get-tuple-element.56.field), custom_call_target="tpu_custom_call" | custom-call | bytes 5767168 | tf_op jit(solution)/shard_map/local/pallas_call | solution.py:346
  247.3 13.5 %second_step.1 = (f32[64,64,128]{2,1,0:T(8,128)}, f32[64,64,128]{2,1,0:T(8,128)}, f32[64,64,128]{2,1,0:T(8,128)}, f32[64,64,128]{2,1,0:T(8,128)}, f32[64,64,128]{2,1,0:T(8,128)}, /*index=5*/f32[32,8,128]{2,1,0:T(8,128)}) custom-call(f32[32,8,128]{2,1,0:T(8,128)} %all_to_all.26.sums.sums0, f32[32,8,128]{2,1,0:T(8,128)} %copy-done.1, ...), custom_call_target="tpu_custom_call" | custom-call | bytes 29753600 | tf_op jit(solution)/shard_map/second_step/pallas_call | solution.py:346
  260.8 14.2 %all_to_all.27.sums2 = f32[32,8,128]{2,1,0:T(8,128)} all-to-all(f32[32,8,128]{2,1,0:T(8,128)} %get-tuple-element.64), channel_id=1, replica_groups=mesh['sector'=4,'axial'=8] {'sector','axial'}, dimensions={0} | all-to-all | bytes 262144 | tf_op jit(solution)/shard_map/all_to_all | solution.py:358
  275.0 7.8 %last.1 = (f32[64,64,128]{2,1,0:T(8,128)}, f32[64,64,128]{2,1,0:T(8,128)}) custom-call(f32[32,8,128]{2,1,0:T(8,128)} %all_to_all.26.sums.sums0, f32[32,8,128]{2,1,0:T(8,128)} %copy-done.1, f32[32,8,128]{2,1,0:T(8,128)} %all_to_all.27.sums2, f32[64,64,128]{2,1,0:T(8,128)} %get-tuple-element.39.field, f32[64,64,128]{2,1,0:T(8,128)} %get-tuple-element.65.r2, ...), custom_call_target="tpu_custom_call" | custom-call | bytes 17170432 | tf_op jit(solution)/shard_map/last/pallas_call | solution.py:346
  (62 shorter events, 8.0 us)
Async XLA Ops:
  48.4 43.4 %copy-start.2 = (f32[32,8,128]{2,1,0:T(8,128)}, f32[32,8,128]{2,1,0:T(8,128)S(1)}, u32[]{:S(2)}) copy-start(f32[32,8,128]{2,1,0:T(8,128)S(1)} %all_to_all.25) | copy-start | bytes 393220
  48.4 2.9 %copy-start.17 = (s32[2,16,2]{1,2,0:T(2,128)S(1)}, s32[2,16,2]{1,2,0:T(2,128)}, u32[]{:S(2)}) copy-start(s32[2,16,2]{1,2,0:T(2,128)} %param.17) | copy-start | bytes 772
  48.4 3.1 %copy-start.15 = (f32[2,16,64]{2,1,0:T(8,128)S(1)}, f32[2,16,64]{2,1,0:T(8,128)}, u32[]{:S(2)}) copy-start(f32[2,16,64]{2,1,0:T(8,128)} %param.18) | copy-start | bytes 24580
  48.4 6.6 %copy-start.16 = (f32[4096]{0:T(1024)S(1)}, f32[4096]{0:T(1024)}, u32[]{:S(2)}) copy-start(f32[4096]{0:T(1024)} %param.16) | copy-start | bytes 49156
  48.4 85.0 %all-to-all-start.1 = ((f32[32,128,128]{2,1,0:T(8,128)}), f32[32,128,128]{2,1,0:T(8,128)S(1)}, u32[]{:S(2)}, u32[]{:S(2)}) async-start(f32[32,128,128]{2,1,0:T(8,128)} %bitcast.26), calls=%async_computation.1 | async-start | bytes 4194304 | tf_op jit(solution)/shard_map/all_to_all | solution.py:358
  51.6 38.6 %collective-permute-start = (f32[16,128]{1,0:T(8,128)S(1)}, f32[16,128]{1,0:T(8,128)S(1)}, u32[]{:S(2)}, u32[]{:S(2)}) collective-permute-start(f32[16,128]{1,0:T(8,128)S(1)} %get-tuple-element.72), channel_id=1, source_target_pairs={{0,8},{8,16},{16,24},{24,0},{1,9},{9,17},{17,25},{25,1},{2,10},{10... | collective-permute-start | bytes 24584 | tf_op jit(solution)/shard_map/ppermute | solution.py:363
  53.3 37.1 %collective-permute-start.1 = (f32[16,128]{1,0:T(8,128)S(1)}, f32[16,128]{1,0:T(8,128)S(1)}, u32[]{:S(2)}, u32[]{:S(2)}) collective-permute-start(f32[16,128]{1,0:T(8,128)S(1)} %get-tuple-element.73), channel_id=1, source_target_pairs={{0,1},{1,2},{2,3},{3,4},{4,5},{5,6},{6,7},{8,9},{9,10},{10,11},{11... | collective-permute-start | bytes 24584 | tf_op jit(solution)/shard_map/ppermute | solution.py:363
  100.8 21.5 %collective-permute-start.2 = (f32[16,64,128]{2,1,0:T(8,128)}, f32[16,64,128]{2,1,0:T(8,128)S(1)}, u32[]{:S(2)}, u32[]{:S(2)}) collective-permute-start(f32[16,64,128]{2,1,0:T(8,128)} %get-tuple-element.42), channel_id=1, source_target_pairs={{0,8},{8,16},{16,24},{24,0},{1,9},{9,17},{17,25},{25,1},{2,10},{10... | collective-permute-start | bytes 1572872 | tf_op jit(solution)/shard_map/ppermute | solution.py:363
  109.7 22.9 %collective-permute-start.3 = (f32[16,64,128]{2,1,0:T(8,128)}, f32[16,64,128]{2,1,0:T(8,128)S(1)}, u32[]{:S(2)}, u32[]{:S(2)}) collective-permute-start(f32[16,64,128]{2,1,0:T(8,128)} %get-tuple-element.43), channel_id=1, source_target_pairs={{8,0},{16,8},{24,16},{0,24},{9,1},{17,9},{25,17},{1,25},{10,2},{18... | collective-permute-start | bytes 1572872 | tf_op jit(solution)/shard_map/ppermute | solution.py:368
  109.7 22.9 %collective-permute-start.4 = (f32[16,64,128]{2,1,0:T(8,128)}, f32[16,64,128]{2,1,0:T(8,128)S(1)}, u32[]{:S(2)}, u32[]{:S(2)}) collective-permute-start(f32[16,64,128]{2,1,0:T(8,128)} %get-tuple-element.44), channel_id=1, source_target_pairs={{0,1},{1,2},{2,3},{3,4},{4,5},{5,6},{6,7},{8,9},{9,10},{10,11},{11... | collective-permute-start | bytes 1572872 | tf_op jit(solution)/shard_map/ppermute | solution.py:363
  111.3 22.1 %collective-permute-start.5 = (f32[16,64,128]{2,1,0:T(8,128)}, f32[16,64,128]{2,1,0:T(8,128)}, u32[]{:S(2)}, u32[]{:S(2)}) collective-permute-start(f32[16,64,128]{2,1,0:T(8,128)} %get-tuple-element.45), channel_id=1, source_target_pairs={{1,0},{2,1},{3,2},{4,3},{5,4},{6,5},{7,6},{9,8},{10,9},{11,10},{12... | collective-permute-start | bytes 1572872 | tf_op jit(solution)/shard_map/ppermute | solution.py:368
  122.3 11.1 %copy-start.7 = (f32[16,64,128]{2,1,0:T(8,128)}, f32[16,64,128]{2,1,0:T(8,128)S(1)}, u32[]{:S(2)}) copy-start(f32[16,64,128]{2,1,0:T(8,128)S(1)} %collective-permute-done.2.g0) | copy-start | bytes 1572868
  132.6 1.0 copy-start.8
  132.6 0.8 copy-start.9
  133.4 1.3 copy-start
  158.5 17.5 %collective-permute-start.6 = (f32[16,64,128]{2,1,0:T(8,128)}, f32[16,64,128]{2,1,0:T(8,128)S(1)}, u32[]{:S(2)}, u32[]{:S(2)}) collective-permute-start(f32[16,64,128]{2,1,0:T(8,128)} %get-tuple-element.50), channel_id=1, source_target_pairs={{0,8},{8,16},{16,24},{24,0},{1,9},{9,17},{17,25},{25,1},{2,10},{10... | collective-permute-start | bytes 1572872 | tf_op jit(solution)/shard_map/ppermute | solution.py:363
  160.9 22.4 %collective-permute-start.7 = (f32[16,64,128]{2,1,0:T(8,128)}, f32[16,64,128]{2,1,0:T(8,128)S(1)}, u32[]{:S(2)}, u32[]{:S(2)}) collective-permute-start(f32[16,64,128]{2,1,0:T(8,128)} %get-tuple-element.51), channel_id=1, source_target_pairs={{8,0},{16,8},{24,16},{0,24},{9,1},{17,9},{25,17},{1,25},{10,2},{18... | collective-permute-start | bytes 1572872 | tf_op jit(solution)/shard_map/ppermute | solution.py:368
  163.0 20.3 %collective-permute-start.8 = (f32[16,64,128]{2,1,0:T(8,128)}, f32[16,64,128]{2,1,0:T(8,128)S(1)}, u32[]{:S(2)}, u32[]{:S(2)}) collective-permute-start(f32[16,64,128]{2,1,0:T(8,128)} %get-tuple-element.52), channel_id=1, source_target_pairs={{0,1},{1,2},{2,3},{3,4},{4,5},{5,6},{6,7},{8,9},{9,10},{10,11},{11... | collective-permute-start | bytes 1572872 | tf_op jit(solution)/shard_map/ppermute | solution.py:363
  164.3 19.0 %collective-permute-start.9 = (f32[16,64,128]{2,1,0:T(8,128)}, f32[16,64,128]{2,1,0:T(8,128)S(1)}, u32[]{:S(2)}, u32[]{:S(2)}) collective-permute-start(f32[16,64,128]{2,1,0:T(8,128)} %get-tuple-element.53), channel_id=1, source_target_pairs={{1,0},{2,1},{3,2},{4,3},{5,4},{6,5},{7,6},{9,8},{10,9},{11,10},{12... | collective-permute-start | bytes 1572872 | tf_op jit(solution)/shard_map/ppermute | solution.py:368
  176.0 7.3 %copy-start.10 = (f32[16,64,128]{2,1,0:T(8,128)}, f32[16,64,128]{2,1,0:T(8,128)S(1)}, u32[]{:S(2)}) copy-start(f32[16,64,128]{2,1,0:T(8,128)S(1)} %collective-permute-done.6.g0) | copy-start | bytes 1572868
  183.3 1.0 copy-start.12
  183.3 1.1 copy-start.13
  184.4 14.8 %copy-start.14 = (f32[32,8,128]{2,1,0:T(8,128)S(1)}, f32[32,8,128]{2,1,0:T(8,128)}, u32[]{:S(2)}) copy-start(f32[32,8,128]{2,1,0:T(8,128)} %get-tuple-element.46) | copy-start | bytes 393220
  192.5 53.5 %collective-permute-start.10 = (f32[16,64,128]{2,1,0:T(8,128)}, f32[16,64,128]{2,1,0:T(8,128)S(1)}, u32[]{:S(2)}, u32[]{:S(2)}) collective-permute-start(f32[16,64,128]{2,1,0:T(8,128)} %get-tuple-element.57), channel_id=1, source_target_pairs={{0,8},{8,16},{16,24},{24,0},{1,9},{9,17},{17,25},{25,1},{2,10},{10... | collective-permute-start | bytes 1572872 | tf_op jit(solution)/shard_map/ppermute | solution.py:363
  195.2 50.7 %collective-permute-start.11 = (f32[16,64,128]{2,1,0:T(8,128)}, f32[16,64,128]{2,1,0:T(8,128)S(1)}, u32[]{:S(2)}, u32[]{:S(2)}) collective-permute-start(f32[16,64,128]{2,1,0:T(8,128)} %get-tuple-element.58), channel_id=1, source_target_pairs={{8,0},{16,8},{24,16},{0,24},{9,1},{17,9},{25,17},{1,25},{10,2},{18... | collective-permute-start | bytes 1572872 | tf_op jit(solution)/shard_map/ppermute | solution.py:368
  196.6 49.3 %collective-permute-start.12 = (f32[16,64,128]{2,1,0:T(8,128)}, f32[16,64,128]{2,1,0:T(8,128)S(1)}, u32[]{:S(2)}, u32[]{:S(2)}) collective-permute-start(f32[16,64,128]{2,1,0:T(8,128)} %get-tuple-element.59), channel_id=1, source_target_pairs={{0,1},{1,2},{2,3},{3,4},{4,5},{5,6},{6,7},{8,9},{9,10},{10,11},{11... | collective-permute-start | bytes 1572872 | tf_op jit(solution)/shard_map/ppermute | solution.py:363
  197.9 48.0 %collective-permute-start.13 = (f32[16,64,128]{2,1,0:T(8,128)}, f32[16,64,128]{2,1,0:T(8,128)S(1)}, u32[]{:S(2)}, u32[]{:S(2)}) collective-permute-start(f32[16,64,128]{2,1,0:T(8,128)} %get-tuple-element.60), channel_id=1, source_target_pairs={{1,0},{2,1},{3,2},{4,3},{5,4},{6,5},{7,6},{9,8},{10,9},{11,10},{12... | collective-permute-start | bytes 1572872 | tf_op jit(solution)/shard_map/ppermute | solution.py:368
  234.5 11.4 %all-to-all-start.3 = ((f32[32,8,128]{2,1,0:T(8,128)}), f32[32,8,128]{2,1,0:T(8,128)S(1)}, u32[]{:S(2)}, u32[]{:S(2)}) async-start(f32[32,8,128]{2,1,0:T(8,128)} %get-tuple-element.55), calls=%async_computation.3 | async-start | bytes 262144 | tf_op jit(solution)/shard_map/all_to_all | solution.py:358
  245.9 0.8 copy-start.3
  245.9 1.0 copy-start.4
  246.0 1.2 copy-start.5
  246.0 1.4 copy-start.6
  (2 other events, 1.5 us)

commit v2 on v1

v2 whole, which is shorter than its diff:
```python
import functools
import jax
import jax.numpy as jnp
from jax import lax
from jax.experimental import pallas as pl
from jax.experimental.pallas import tpu as pltpu
from jax.sharding import PartitionSpec as P

AXES = ("sector", "axial")
F32 = jnp.float32
BF16 = jnp.bfloat16
VMEM = pl.BlockSpec(memory_space=pltpu.VMEM)
HBM = pl.BlockSpec(memory_space=pltpu.HBM)
SMEM = pl.BlockSpec(memory_space=pltpu.SMEM)
NT = (((1,), (1,)), ((), ()))
CHUNK = 16
GROUP = 16
LIMIT = 14 << 20
WIDE = 60 << 20


def struct(*shape, dtype=F32):
    return jax.ShapeDtypeStruct(shape, dtype)


def iota(shape, dim):
    return lax.broadcasted_iota(jnp.int32, shape, dim)


def split(value):
    high = value.astype(BF16)
    return high, (value - high.astype(F32)).astype(BF16)


def dot(left, right, dims=(((1,), (0,)), ((), ()))):
    return lax.dot_general(left, right, dims, preferred_element_type=F32)


def pack_kernel(slots_each, owners, patches, counts, kbb, inner, nodes, payload, meta, blocks, node_rows, tally):
    step = pl.program_id(0)
    chunk, bn, _ = inner.shape
    half, quarter = bn // 2, bn // 4
    elems = kbb.shape[2]

    @pl.when(step == 0)
    def _():
        for i in range(half):
            blocks[pl.ds(i, elems, stride=half), :] = jnp.concatenate([kbb[i], kbb[i + half]], axis=0).T
        node_rows[...] = nodes[...].T
        meta[...] = jnp.zeros_like(meta)

        def clear(i, carry):
            tally[i] = 0
            return carry

        lax.fori_loop(0, meta.shape[0] // slots_each, clear, 0)

    row_id = iota((bn, bn), 0)
    col_id = iota((bn, bn), 1)
    lower = (row_id > col_id)[:half, :half]
    upper = (row_id < col_id)[:half, :half]
    lane = iota((1, 128), 1)
    for first in range(0, chunk, GROUP):
        group = range(GROUP)
        where = [step * chunk + first + e for e in group]
        grams = [dot(inner[first + e], inner[first + e], NT) for e in group]
        picks = [(node_rows[pl.ds(i, 1), :] == row_id).astype(F32).astype(BF16) for i in where]
        pairs = []
        for e in group:
            both = blocks[pl.ds(pl.multiple_of(where[e] * half, half), half), :]
            block = jnp.concatenate([both[:, :bn], both[:, bn:]], axis=0)
            pairs.append(split(block - grams[e]))
        lefts = [dot(jnp.concatenate([picks[e], picks[e]], axis=1), jnp.concatenate(pairs[e], axis=0)) for e in group]
        pairs = [split(left) for left in lefts]
        placed_all = [dot(pairs[e][0], picks[e], NT) + dot(pairs[e][1], picks[e], NT) for e in group]
        for e in group:
            placed, index = placed_all[e], where[e]
            triangles = jnp.where(lower, placed[:half, :half], jnp.where(upper, placed[half:, half:], 0.0))
            packed = jnp.concatenate([triangles, placed[:half, half:]], axis=1)
            packed = jnp.concatenate([packed[:quarter], packed[quarter:]], axis=1)
            diag = jnp.sum(jnp.where(row_id == col_id, placed, 0.0), axis=0, keepdims=True)
            owner = owners[index]
            rank = tally[owner]
            tally[owner] = rank + 1
            slot = owner * slots_each + rank
            payload[pl.ds(pl.multiple_of(slot * quarter, quarter), quarter), :] = packed
            tag = jnp.where(index < counts[0], patches[index] + 1, 0).astype(F32)
            meta[pl.ds(slot, 1), :] = jnp.where(
                lane < bn, jnp.concatenate([diag, diag], axis=1), jnp.where(lane == bn, tag, 0.0)
            )


def pack_call(devices, owners, patches, counts, kbb, inner, nodes):
    elems, bn, ni = inner.shape
    slots_each = 2 * elems // devices
    slots = devices * slots_each
    whole = lambda *shape: pl.BlockSpec(shape, lambda i: (0,) * len(shape))
    return pl.pallas_call(
        functools.partial(pack_kernel, slots_each),
        grid=(elems // CHUNK,),
        in_specs=[
            SMEM,
            SMEM,
            SMEM,
            whole(bn, bn, elems),
            pl.BlockSpec((CHUNK, bn, ni), lambda i: (i, 0, 0)),
            whole(bn, elems),
        ],
        out_specs=[whole(slots * bn // 4, 128), whole(slots, 128)],
        out_shape=[struct(slots * bn // 4, 128), struct(slots, 128)],
        scratch_shapes=[
            pltpu.VMEM((elems * bn // 2, 128), F32),
            pltpu.VMEM((elems, bn), jnp.int32),
            pltpu.SMEM((devices,), jnp.int32),
        ],
        compiler_params=pltpu.CompilerParams(vmem_limit_bytes=WIDE),
        name="pack",
    )(owners, patches, counts, kbb, inner, nodes)


def send_values(picked, gains, field, sends):
    count = sends[0].shape[0]
    for which, send in enumerate(sends):

        def one(k, carry):
            send[k] = gains[which * count + k] * field[picked[which * count + k]]
            return carry

        lax.fori_loop(0, count, one, 0, unroll=4)


def take_values(placed, received, result):
    count = received[0].shape[0]
    for which, got in enumerate(received):

        def one(k, carry):
            patch = placed[which * count + k]
            result[patch] = result[patch] - got[k]
            return carry

        lax.fori_loop(0, count, one, 0, unroll=4)


def gather_kernel(index0, index1, loads, gains, out0, out1, sems):
    bn = loads.shape[1]
    count = out0.shape[0]
    copies = []
    for which, (index, out) in enumerate(((index0, out0), (index1, out1))):
        for k in range(count):
            copies.append(pltpu.make_async_copy(loads.at[index[k]], out.at[k, pl.ds(0, bn)], sems.at[which]))
    for copy in copies:
        copy.start()
    if out0.shape[1] > bn:
        for which, out in enumerate((out0, out1)):
            rows = jnp.concatenate([gains[which], gains[which]], axis=1)
            for k in range(count):
                out[k, pl.ds(bn, 8), :] = jnp.broadcast_to(rows[k : k + 1], (8, 128))
    for copy in copies:
        copy.wait()


def gather_call(index0, index1, loads, gains, extra):
    out = struct(index0.shape[0], loads.shape[1] + extra, loads.shape[2])
    return pl.pallas_call(
        gather_kernel,
        in_specs=[SMEM, SMEM, pl.BlockSpec(memory_space=pl.ANY), VMEM],
        out_specs=[VMEM, VMEM],
        out_shape=[out, out],
        scratch_shapes=[pltpu.SemaphoreType.DMA((2,))],
        compiler_params=pltpu.CompilerParams(vmem_limit_bytes=WIDE),
        name="gather",
    )(index0, index1, loads, gains)


def diagonal_kernel(
    tags, picked, meta, capacity, conduct, g0, g2, loads, inverse, field, gains, t0, t1, t2, t3, total, gain_rows,
):
    patch_dev, bn = capacity.shape
    count = conduct.shape[1]
    for which, got in enumerate((g0, g2)):
        gain_rows[pl.ds(2 * which * count, count), :] = jnp.concatenate([conduct[which], conduct[which]], axis=1)
        for k in range(count):
            gain_rows[pl.ds((2 * which + 1) * count + k, 1), :] = got[k, pl.ds(bn, 1), :]
    total[pl.ds(0, patch_dev), :] = jnp.concatenate([capacity[...], capacity[...]], axis=1)

    def add(i, carry):
        patch = tags[i]
        total[pl.ds(patch, 1), :] = total[pl.ds(patch, 1), :] + meta[pl.ds(i, 1), :]
        return carry

    lax.fori_loop(0, meta.shape[0], add, 0, unroll=4)

    def link(i, carry):
        patch = picked[i]
        total[pl.ds(patch, 1), :] = total[pl.ds(patch, 1), :] + gain_rows[pl.ds(i, 1), :]
        return carry

    lax.fori_loop(0, gain_rows.shape[0], link, 0, unroll=4)
    over = 1.0 / total[pl.ds(0, patch_dev), :]
    total[pl.ds(0, patch_dev), :] = over
    columns = over[:, :bn].T
    for p in range(patch_dev):
        column = jnp.broadcast_to(columns[:, p : p + 1], (bn, 128))
        inverse[p] = column
        field[p] = column * loads[p]
    for which, rows in enumerate((t0, t1, t2, t3)):
        for k in range(count):
            i = which * count + k
            rows[pl.ds(k, 1), :] = total[pl.ds(picked[i], 1), :] * gain_rows[pl.ds(i, 1), :]
    columns = gain_rows[...][:, :bn].T
    for k in range(gain_rows.shape[0]):
        gains[k] = jnp.broadcast_to(columns[:, k : k + 1], (bn, 128))


def edges_kernel(placed, loads, t0, t1, t2, t3, g0, g1, g2, g3, image):
    bn = loads.shape[1]
    count = t0.shape[0]
    image[...] = loads[...]
    for which, (rows, got) in enumerate(((t0, g0), (t1, g1), (t2, g2), (t3, g3))):
        columns = rows[...][:, :bn].T
        for k in range(count):
            patch = placed[which * count + k]
            image[patch] = image[patch] - jnp.broadcast_to(columns[:, k : k + 1], (bn, 128)) * got[k, pl.ds(0, bn), :]


def stacked(value):
    high, low = split(value)
    return jnp.concatenate([high, high, low], axis=0)


def folded(value):
    total = value[0:8]
    for i in range(8, value.shape[0], 8):
        total = total + value[i : i + 8]
    return total


def publish(partial, sums):
    rows = [jnp.sum(s, axis=0, keepdims=True) for s in sums]
    block = jnp.concatenate(rows + [jnp.zeros((8 - len(rows), 128), F32)], axis=0)
    for d in range(partial.shape[0]):
        partial[d] = block


def gathered(received):
    return jnp.sum(received[...], axis=0)


def zeros(n):
    return (jnp.zeros((8, 128), F32),) * n


def assemble_kernel(
    tags, picked, payload, start_in, field_in, inverse_in, loads_in, gains_in,
    image, blocks, after, s0, s1, s2, s3, partial, field, inverse, loads, gains, packed, sems,
):
    patch_dev, bn, _ = image.shape
    half, quarter = bn // 2, bn // 4
    banks = packed.shape[0]
    slots = tags.shape[0]
    pairs = ((start_in, image), (field_in, field), (inverse_in, inverse), (loads_in, loads), (gains_in, gains))
    fetches = [pltpu.make_async_copy(src, dst, sems.at[i]) for i, (src, dst) in enumerate(pairs)]
    for copy in fetches:
        copy.start()
    packed[...] = jnp.zeros_like(packed)

    def add(j, carry):
        for bank in range(banks):
            i = j * banks + bank
            patch = tags[i]
            packed[bank, patch] = packed[bank, patch] + payload[pl.ds(pl.multiple_of(i * quarter, quarter), quarter), :]
        return carry

    lax.fori_loop(0, slots // banks, add, 0, unroll=2)
    fetches[0].wait()
    fetches[1].wait()
    row_id = iota((half, bn), 0)
    col_id = iota((half, bn), 1)
    kept = (col_id >= half) | (row_id > col_id)
    moved = (col_id < half) & (row_id < col_id)

    def build(j, carry):
        group = [j * GROUP + g for g in range(GROUP)]
        wholes = []
        for p in group:
            both = packed[0, p]
            for bank in range(1, banks):
                both = both + packed[bank, p]
            rows = jnp.concatenate([both[:, :bn], both[:, bn:]], axis=0)
            second = jnp.where(moved, rows, 0.0)[:, :half]
            second = jnp.concatenate([jnp.zeros((half, half), F32), second], axis=1)
            wholes.append(jnp.concatenate([jnp.where(kept, rows, 0.0), second], axis=0))
        wholes = [w + w.T for w in wholes]
        threes = []
        for w in wholes:
            high, low = split(w)
            threes.append(jnp.concatenate([high, low, high], axis=1))
        for p, three in zip(group, threes):
            blocks[p] = three
        products = [dot(three, stacked(field[p])) for p, three in zip(group, threes)]
        for p, product in zip(group, products):
            image[p] = image[p] + product
        return carry

    lax.fori_loop(0, patch_dev // GROUP, build, 0)
    for copy in fetches[2:]:
        copy.wait()

    def finish(p, carry):
        here, value = image[p], field[p]
        after[p] = inverse[p] * here
        return carry[0] + folded(loads[p] * value), carry[1] + folded(here * value)

    sums = lax.fori_loop(0, patch_dev, finish, zeros(2), unroll=2)
    send_values(picked, gains, after, (s0, s1, s2, s3))
    publish(partial, sums)


def local_kernel(blocks, field, base, result):
    def some(j, carry):
        group = [j * GROUP + g for g in range(GROUP)]
        products = [dot(blocks[p], stacked(field[p])) for p in group]
        for p, product in zip(group, products):
            result[p] = base[p] + product
        return carry

    lax.fori_loop(0, field.shape[0] // GROUP, some, 0)


def second_kernel(picked, placed, inverse, gains, g0, g1, g2, g3, base, result, after, s0, s1, s2, s3):
    take_values(placed, (g0, g1, g2, g3), result)

    def scale(p, carry):
        after[p] = inverse[p] * result[p]
        return carry

    lax.fori_loop(0, inverse.shape[0], scale, 0, unroll=2)
    send_values(picked, gains, after, (s0, s1, s2, s3))


def first_step_kernel(sums, loads, field, image, second, inverse, left, left_image, partial):
    first = gathered(sums)
    alpha = first[0:1] / first[1:2]

    def one(p, carry):
        r = loads[p] - alpha * image[p]
        w = image[p] - alpha * second[p]
        u = inverse[p] * r
        left[p] = r
        left_image[p] = w
        return (
            carry[0] + folded(r * u),
            carry[1] + folded(u * w),
            carry[2] + folded(u * image[p] + field[p] * w),
        )

    publish(partial, lax.fori_loop(0, loads.shape[0], one, zeros(3), unroll=2))


def second_step_kernel(
    sums0, sums1, placed, g0, g1, g2, g3, field, image, second, r1, w1, inverse, base,
    third, r2_out, w2_out, partial,
):
    first, then = gathered(sums0), gathered(sums1)
    alpha0 = first[0:1] / first[1:2]
    beta1 = then[0:1] / first[0:1]
    alpha1 = then[0:1] / (then[1:2] + beta1 * (then[2:3] + beta1 * first[1:2]))
    take_values(placed, (g0, g1, g2, g3), third)

    def one(p, carry):
        n0, w, r = second[p], w1[p], r1[p]
        s1 = w + beta1 * image[p]
        z1 = (n0 - alpha0 * third[p]) + beta1 * n0
        r2 = r - alpha1 * s1
        w2 = w - alpha1 * z1
        u2 = inverse[p] * r2
        p1 = inverse[p] * r + beta1 * field[p]
        r2_out[p] = r2
        w2_out[p] = w2
        return (
            carry[0] + folded(r2 * u2),
            carry[1] + folded(u2 * w2),
            carry[2] + folded(u2 * s1 + p1 * w2),
        )

    publish(partial, lax.fori_loop(0, field.shape[0], one, zeros(3)))


def last_kernel(sums0, sums1, sums2, field, image, inverse, r1, w1, r2, w2, estimate, left):
    first, then, last = gathered(sums0), gathered(sums1), gathered(sums2)
    alpha0 = first[0:1] / first[1:2]
    beta1 = then[0:1] / first[0:1]
    curve1 = then[1:2] + beta1 * (then[2:3] + beta1 * first[1:2])
    alpha1 = then[0:1] / curve1
    beta2 = last[0:1] / then[0:1]
    alpha2 = last[0:1] / (last[1:2] + beta2 * (last[2:3] + beta2 * curve1))

    def one(p, carry):
        p1 = inverse[p] * r1[p] + beta1 * field[p]
        direction = inverse[p] * r2[p] + beta2 * p1
        estimate[p] = alpha0 * field[p] + alpha1 * p1 + alpha2 * direction
        left[p] = r2[p] - alpha2 * (w2[p] + beta2 * (w1[p] + beta1 * image[p]))
        return carry

    lax.fori_loop(0, field.shape[0], one, 0, unroll=2)


def call(kernel, name, ins, outs, scratch=(), flops=0, alias=None, limit=None, far=()):
    ints = lambda a: a.ndim == 1 and a.dtype == jnp.int32
    moved = sum(a.size * a.dtype.itemsize for a in ins) + sum(s.size * s.dtype.itemsize for s in outs)
    return pl.pallas_call(
        kernel,
        in_specs=[SMEM if ints(a) else HBM if i in far else VMEM for i, a in enumerate(ins)],
        out_specs=[VMEM] * len(outs),
        out_shape=list(outs),
        scratch_shapes=list(scratch),
        input_output_aliases=alias or {},
        cost_estimate=pl.CostEstimate(flops=flops, bytes_accessed=moved, transcendentals=0),
        compiler_params=pltpu.CompilerParams(vmem_limit_bytes=limit or LIMIT),
        name=name,
    )(*[pltpu.with_memory_space_constraint(a, pltpu.HBM) if i in far else a for i, a in enumerate(ins)])


def everywhere(partial):
    return lax.all_to_all(partial, AXES, split_axis=0, concat_axis=0, tiled=True)


def onward(value, axis, wrap):
    n = lax.axis_size(axis)
    return lax.ppermute(value, axis, [(i, (i + 1) % n) for i in range(n) if wrap or i + 1 < n])


def back(value, axis, wrap):
    n = lax.axis_size(axis)
    return lax.ppermute(value, axis, [((i + 1) % n, i) for i in range(n) if wrap or i + 1 < n])


def exchange(s0, s1, s2, s3):
    return (
        onward(s0, "sector", True),
        back(s1, "sector", True),
        onward(s2, "axial", False),
        back(s3, "axial", False),
    )


def shards(kbb, interior, node_lists, owners, patch_ids, counts, capacity, links, conduct, loads):
    elems, bn = node_lists.shape
    devices = lax.axis_size("sector") * lax.axis_size("axial")
    points, cases = loads.shape
    patch_dev = points // bn
    count = conduct.shape[1]
    loads = loads.reshape(patch_dev, bn, cases)
    vec = struct(patch_dev, bn, cases)
    buf = struct(count, bn, cases)
    total = struct(devices, 8, cases)

    table = links.transpose(0, 2, 1)
    own_sector, own_axial = table[0, 0], table[1, 0]
    s0, s2 = gather_call(own_sector, own_axial, loads, conduct, 8)
    owners, far_sector, far_axial, s0, s2 = lax.optimization_barrier((owners, table[0, 1], table[1, 1], s0, s2))
    g0, g2 = onward(s0, "sector", True), onward(s2, "axial", False)
    far_sector, far_axial = onward(far_sector, "sector", True), onward(far_axial, "axial", False)
    payload, meta = pack_call(
        devices, owners.reshape(elems), patch_ids, counts,
        kbb.transpose(1, 2, 0), interior.transpose(0, 2, 1), node_lists.T,
    )
    slots = meta.shape[0]
    payload, meta, g0, g2, far_sector, far_axial = lax.optimization_barrier(
        (payload, meta, g0, g2, far_sector, far_axial)
    )
    s1, s3 = gather_call(far_sector, far_axial, loads, conduct, 0)
    meta, s1, s3 = lax.optimization_barrier((meta, s1, s3))
    g1, g3 = back(s1, "sector", True), back(s3, "axial", False)
    meta = everywhere(meta.reshape(devices, slots // devices, 128)).reshape(slots, 128)
    payload, g1, g3 = lax.optimization_barrier((payload, g1, g3))
    payload = everywhere(payload.reshape(devices, -1, 128)).reshape(slots * bn // 4, 128)
    picked = jnp.concatenate([own_sector, far_sector, own_axial, far_axial])
    placed = jnp.concatenate([far_sector, own_sector, far_axial, own_axial])
    tags = meta[:, bn].astype(jnp.int32)
    tags = jnp.where(tags > 0, tags - 1, patch_dev)
    row = struct(count, 128)
    inverse, field, gains, *rows = call(
        diagonal_kernel, "diagonal",
        (tags, picked, meta, capacity.reshape(patch_dev, bn), conduct, g0, g2, loads),
        (vec, vec, struct(4 * count, bn, cases), row, row, row, row),
        (pltpu.VMEM((patch_dev + 8, 128), F32), pltpu.VMEM((4 * count, 128), F32)), limit=WIDE,
    )
    rows = exchange(*rows)
    (start,) = call(edges_kernel, "edges", (placed, loads, *rows, g0, g1, g2, g3), (vec,), limit=WIDE)
    image, blocks, after, *rest = call(
        assemble_kernel, "assemble",
        (tags, picked, payload, start, field, inverse, loads, gains),
        (vec, struct(patch_dev, bn, 3 * bn, dtype=BF16), vec, buf, buf, buf, buf, total,
         vec, vec, vec, struct(4 * count, bn, cases)),
        (pltpu.VMEM((4, patch_dev + 1, bn // 4, 128), F32), pltpu.SemaphoreType.DMA((5,))),
        far=(3, 4, 5, 6, 7),
    )
    *sends, partial, field, inverse, loads, gains = rest
    got = exchange(*sends)
    sums0 = everywhere(partial)
    after, sums0 = lax.optimization_barrier((after, sums0))
    (base,) = call(local_kernel, "local", (blocks, after, image), (vec,))
    second, after, *sends = call(
        second_kernel, "second", (picked, placed, inverse, gains, *got, base),
        (vec, vec, buf, buf, buf, buf), alias={8: 0},
    )
    got = exchange(*sends)
    r1, w1, partial = call(
        first_step_kernel, "first_step", (sums0, loads, field, image, second, inverse), (vec, vec, total)
    )
    sums1 = everywhere(partial)
    after, sums1 = lax.optimization_barrier((after, sums1))
    (base,) = call(local_kernel, "local", (blocks, after, second), (vec,))
    _, r2, w2, partial = call(
        second_step_kernel, "second_step",
        (sums0, sums1, placed, *got, field, image, second, r1, w1, inverse, base),
        (vec, vec, vec, total), alias={13: 0},
    )
    sums2 = everywhere(partial)
    estimate, left = call(
        last_kernel, "last", (sums0, sums1, sums2, field, image, inverse, r1, w1, r2, w2), (vec, vec)
    )
    return estimate.reshape(points, cases), left.reshape(points, cases)


def solution(mesh):
    wide = P(AXES, None)
    deep = P(AXES, None, None)
    return jax.shard_map(
        shards,
        mesh=mesh,
        in_specs=(
            deep, deep, wide, wide, P(AXES), P(AXES), P(AXES),
            P(None, AXES, None), P(None, AXES, None), wide,
        ),
        out_specs=(wide, wide),
        check_vma=False,
    )
```

time: 283 us -> 198 us (0.70)
  Pallas kernels: 119 us -> 50.3 us
  waiting for transfers between devices: 63.3 us -> 39 us
  starting transfers between devices: 34.6 us -> 45.5 us
    pallas_call x8 -> x11, Pallas kernels: 87.2 us -> 37.9 us  [the longest x9 31.7 us: call(): pl.pallas_call(kernel, in_specs=[SMEM if ints(a) else HBM if i in far els...]
    ppermute x8 -> x10, waiting for transfers between devices: 45.7 us -> 22.5 us  [onward(): lax.ppermute(value, axis, [(i, (i + 1) % n) for i in range(n) if wrap or...]
    pallas_call x1, Pallas kernels: 31.6 us -> 12.4 us  [pack_call(): pl.pallas_call(functools.partial(pack_kernel, slots_each), grid=(elems //...]
    ppermute x6 -> x8, waiting for transfers between devices: 17.6 us -> 7.88 us  [back(): lax.ppermute(value, axis, [((i + 1) % n, i) for i in range(n) if wrap or...]
    all_to_all x2, waiting for transfers between devices: 0.01 us -> 8.62 us  [everywhere(): lax.all_to_all(partial, AXES, split_axis=0, concat_axis=0, tiled=True)]
    ppermute x6 -> x8, starting transfers between devices: 7.32 us -> 12.4 us  [back(): lax.ppermute(value, axis, [((i + 1) % n, i) for i in range(n) if wrap or...]
    unnamed x36 -> x38, local copies, waits for them, and re-layouts: 4.65 us -> 1.16 us
    ppermute x8 -> x10, starting transfers between devices: 21.8 us -> 25.2 us  [onward(): lax.ppermute(value, axis, [(i, (i + 1) % n) for i in range(n) if wrap or...]
  transfers between devices with their start and end apart: 16 -> 20, of which waited for: 5 -> 4; matrix products, arithmetic and copies ran while one was open for 1% -> 1% of each run, Pallas kernels for 12% -> 15%
where the time goes in v2:
time: 198 us; the launch traced here: 197 us
  blocking collectives  55.8 us (28%)
  Pallas kernels  50.3 us (25%)
  starting transfers between devices  45.5 us (23%)
  waiting for transfers between devices  39 us (20%)
  local copies, waits for them, and re-layouts  3.17 us (2%)
    all_to_all x3, blocking collectives, everywhere(): lax.all_to_all(partial, AXES, split_axis=0, concat_axis=0, tiled=True)  55.8 us
    pallas_call x9, Pallas kernels, call(): pl.pallas_call(kernel, in_specs=[SMEM if ints(a) else HBM if i in far els...  31.7 us
    ppermute x10, starting transfers between devices, onward(): lax.ppermute(value, axis, [(i, (i + 1) % n) for i in range(n) if wrap or...  25.2 us
    ppermute x10, waiting for transfers between devices, onward(): lax.ppermute(value, axis, [(i, (i + 1) % n) for i in range(n) if wrap or...  22.5 us
    pallas_call x1, Pallas kernels, pack_call(): pl.pallas_call(functools.partial(pack_kernel, slots_each), grid=(elems //...  12.4 us
    ppermute x8, starting transfers between devices, back(): lax.ppermute(value, axis, [((i + 1) % n, i) for i in range(n) if wrap or...  12.4 us
    all_to_all x2, waiting for transfers between devices, everywhere(): lax.all_to_all(partial, AXES, split_axis=0, concat_axis=0, tiled=True)  8.62 us
    all_to_all x2, starting transfers between devices, everywhere(): lax.all_to_all(partial, AXES, split_axis=0, concat_axis=0, tiled=True)  8.01 us
  transfers between devices with their start and end apart: 20, of which 4 were waited for; matrix products, arithmetic and copies ran while one was open for 1% of the time, Pallas kernels for 15%

profile of v2, /device:TPU:0, one launch (start us, length us, event | category | flops | bytes accessed | tf_op | source)
XLA Modules:
  0.0 196.8 jit_solution(16065279270400537080)
XLA Ops:
  0.6 1.3 slice_bitcast_fusion
  2.0 2.9 %gather.2 = (f32[16,72,128]{2,1,0:T(8,128)}, f32[16,72,128]{2,1,0:T(8,128)}) custom-call(s32[16]{0:T(128)} %get-tuple-element.125.index0, s32[16]{0:T(128)} %get-tuple-element.124.index1, f32[64,64,128]{2,1,0:T(8,128)} %bitcast.21, f32[2,16,64]{2,1,0:T(8,128)} %conduct.1), custom_call_target="tpu_custom_call" | custom-call | tf_op jit(solution)/shard_map/gather/pallas_call | solution.py:164
  4.9 3.1 %collective-permute-start = (f32[16,72,128]{2,1,0:T(8,128)}, f32[16,72,128]{2,1,0:T(8,128)S(1)}, u32[]{:S(2)}, u32[]{:S(2)}) collective-permute-start(f32[16,72,128]{2,1,0:T(8,128)} %get-tuple-element.67), channel_id=1, source_target_pairs={{0,8},{8,16},{16,24},{24,0},{1,9},{9,17},{17,25},{25,1},{2,10},{10... | collective-permute-start | bytes 1769480 | tf_op jit(solution)/shard_map/ppermute | solution.py:430
  8.0 1.5 collective-permute-start.1
  9.5 1.6 collective-permute-start.2
  11.1 3.6 %collective-permute-start.3 = (s32[16]{0:T(128)S(1)}, s32[16]{0:T(128)S(1)}, u32[]{:S(2)}, u32[]{:S(2)}) collective-permute-start(s32[16]{0:T(128)S(1)} %get-tuple-element.70), channel_id=1, source_target_pairs={{0,1},{1,2},{2,3},{3,4},{4,5},{5,6},{6,7},{8,9},{9,10},{10,11},{11... | collective-permute-start | bytes 200 | tf_op jit(solution)/shard_map/ppermute | solution.py:430
  15.4 12.4 %pack.1 = (f32[4096,128]{1,0:T(8,128)}, f32[256,128]{1,0:T(8,128)}) custom-call(s32[128]{0:T(128)} %bitcast.33, s32[128]{0:T(128)} %patches.1, s32[1]{0:T(128)S(6)} %copy.16.counts, f32[64,64,128]{2,1,0:T(8,128)} %bitcast.27, bf16[128,64,256]{2,1,0:T(8,128)(2,1)} %bitcast.26, s32[64,128]{1,0:T(8,128)} %bitcast.31), custom_call_target="tpu_custom_call" | custom-call | tf_op jit(solution)/shard_map/pack/pallas_call | solution.py:98
  28.3 3.2 %gather.3 = (f32[16,64,128]{2,1,0:T(8,128)}, f32[16,64,128]{2,1,0:T(8,128)}) custom-call(s32[16]{0:T(128)} %copy-done.15, s32[16]{0:T(128)} %copy-done.17, f32[64,64,128]{2,1,0:T(8,128)} %bitcast.22, f32[2,16,64]{2,1,0:T(8,128)} %conduct.1), custom_call_target="tpu_custom_call" | custom-call | tf_op jit(solution)/shard_map/gather/pallas_call | solution.py:164
  31.6 2.3 %collective-permute-start.4 = (f32[16,64,128]{2,1,0:T(8,128)}, f32[16,64,128]{2,1,0:T(8,128)S(1)}, u32[]{:S(2)}, u32[]{:S(2)}) collective-permute-start(f32[16,64,128]{2,1,0:T(8,128)} %get-tuple-element.78), channel_id=1, source_target_pairs={{8,0},{16,8},{24,16},{0,24},{9,1},{17,9},{25,17},{1,25},{10,2},{18... | collective-permute-start | bytes 1572872 | tf_op jit(solution)/shard_map/ppermute | solution.py:435
  35.1 3.5 %all-to-all-start = ((f32[32,8,128]{2,1,0:T(8,128)}), f32[32,8,128]{2,1,0:T(8,128)S(1)}, u32[]{:S(2)}, u32[]{:S(2)}) async-start(f32[32,8,128]{2,1,0:T(8,128)} %bitcast.10), calls=%async_computation | async-start | bytes 262144 | tf_op jit(solution)/shard_map/all_to_all | solution.py:425
  38.7 7.9 %collective-permute-done.4.g1 = f32[16,64,128]{2,1,0:T(8,128)S(1)} collective-permute-done((f32[16,64,128]{2,1,0:T(8,128)}, f32[16,64,128]{2,1,0:T(8,128)S(1)}, u32[]{:S(2)}, u32[]{:S(2)}) %collective-permute-start.4) | collective-permute-done | bytes 524320 | tf_op jit(solution)/shard_map/ppermute | solution.py:435
  46.5 3.5 %all-to-all-done = f32[32,8,128]{2,1,0:T(8,128)S(1)} async-done(((f32[32,8,128]{2,1,0:T(8,128)}), f32[32,8,128]{2,1,0:T(8,128)S(1)}, u32[]{:S(2)}, u32[]{:S(2)}) %all-to-all-start) | async-done | bytes 131104 | tf_op jit(solution)/shard_map/all_to_all | solution.py:425
  50.1 4.5 %all-to-all-start.1 = ((f32[32,128,128]{2,1,0:T(8,128)}), f32[32,128,128]{2,1,0:T(8,128)S(1)}, u32[]{:S(2)}, u32[]{:S(2)}) async-start(f32[32,128,128]{2,1,0:T(8,128)} %bitcast.28), calls=%async_computation.1 | async-start | bytes 4194304 | tf_op jit(solution)/shard_map/all_to_all | solution.py:425
  56.7 7.4 %diagonal.1 = (f32[64,64,128]{2,1,0:T(8,128)}, f32[64,64,128]{2,1,0:T(8,128)}, f32[64,64,128]{2,1,0:T(8,128)}, f32[16,128]{1,0:T(8,128)}, f32[16,128]{1,0:T(8,12...) custom-call(s32[256]{0:T(256)} %select_reduce_fusion.tags, s32[64]{0:T(128)} %get-tuple-element.123.picked, ...), custom_call_target="tpu_custom_call" | custom-call | bytes 9757952 | tf_op jit(solution)/shard_map/diagonal/pallas_call | solution.py:411
  64.1 2.0 %collective-permute-start.6 = (f32[16,128]{1,0:T(8,128)}, f32[16,128]{1,0:T(8,128)S(1)}, u32[]{:S(2)}, u32[]{:S(2)}) collective-permute-start(f32[16,128]{1,0:T(8,128)} %get-tuple-element.83), channel_id=1, source_target_pairs={{0,8},{8,16},{16,24},{24,0},{1,9},{9,17},{17,25},{25,1},{2,10},{10... | collective-permute-start | bytes 24584 | tf_op jit(solution)/shard_map/ppermute | solution.py:430
  66.1 1.8 collective-permute-start.7
  67.9 1.8 collective-permute-start.8
  71.1 22.4 %collective-permute-done.6.t0 = f32[16,128]{1,0:T(8,128)S(1)} collective-permute-done((f32[16,128]{1,0:T(8,128)}, f32[16,128]{1,0:T(8,128)S(1)}, u32[]{:S(2)}, u32[]{:S(2)}) %collective-permute-start.6) | collective-permute-done | bytes 8224 | tf_op jit(solution)/shard_map/ppermute | solution.py:430
  94.1 4.5 %edges.1.start_in = f32[64,64,128]{2,1,0:T(8,128)} custom-call(s32[64]{0:T(128)} %get-tuple-element.122.placed, f32[64,64,128]{2,1,0:T(8,128)} %bitcast.24, f32[16,128]{1,0:T(8,128)} %copy-done.9, f32[16,128]{1,0:T(8,128)} %copy-done.10, f32[16,128]{1,0:T(8,128)} %copy-done.11, f32[16,128]{1,0:T(8,128)} %copy-done.12, f32[16,72,128]{2,1,0:T(8,128)} %copy-done.3, ...), custom_call_target="tpu_custom_call" | custom-call | bytes 6455552 | tf_op jit(solution)/shard_map/edges/pallas_call | solution.py:411
  98.6 5.1 %all-to-all-done.1 = f32[32,128,128]{2,1,0:T(8,128)S(1)} async-done(((f32[32,128,128]{2,1,0:T(8,128)}), f32[32,128,128]{2,1,0:T(8,128)S(1)}, u32[]{:S(2)}, u32[]{:S(2)}) %all-to-all-start.1) | async-done | bytes 2097184 | tf_op jit(solution)/shard_map/all_to_all | solution.py:425
  103.8 7.2 %assemble.1 = (f32[64,64,128]{2,1,0:T(8,128)S(1)}, bf16[64,64,192]{2,1,0:T(8,128)(2,1)S(1)}, f32[64,64,128]{2,1,0:T(8,128)S(1)}, f32[16,64,128]{2,1,0:T(8,128)S(...) custom-call(s32[256]{0:T(256)S(1)} %copy-done, ...), custom_call_target="tpu_custom_call" | custom-call | bytes 28968192 | tf_op jit(solution)/shard_map/assemble/pallas_call | solution.py:411
  111.0 5.8 %collective-permute-start.10 = (f32[16,64,128]{2,1,0:T(8,128)S(1)}, f32[16,64,128]{2,1,0:T(8,128)S(1)}, u32[]{:S(2)}, u32[]{:S(2)}) collective-permute-start(f32[16,64,128]{2,1,0:T(8,128)S(1)} %get-tuple-element.97), channel_id=1, source_target_pairs={{0,8},{8,16},{16,24},{24,0},{1,9},{9,17},{17,25},{25,1},{2,10},{10... | collective-permute-start | bytes 1572872 | tf_op jit(solution)/shard_map/ppermute | solution.py:430
  119.4 22.1 %all_to_all.25.sums.sums0 = f32[32,8,128]{2,1,0:T(8,128)S(1)} all-to-all(f32[32,8,128]{2,1,0:T(8,128)S(1)} %get-tuple-element.93), channel_id=1, replica_groups=mesh['sector'=4,'axial'=8] {'sector','axial'}, dimensions={0} | all-to-all | bytes 262144 | tf_op jit(solution)/shard_map/all_to_all | solution.py:425
  141.6 1.7 local.2.base
  143.3 1.5 second.1
  144.8 3.1 %collective-permute-start.14 = (f32[16,64,128]{2,1,0:T(8,128)S(1)}, f32[16,64,128]{2,1,0:T(8,128)S(1)}, u32[]{:S(2)}, u32[]{:S(2)}) collective-permute-start(f32[16,64,128]{2,1,0:T(8,128)S(1)} %get-tuple-element.110), channel_id=1, source_target_pairs={{0,8},{8,16},{16,24},{24,0},{1,9},{9,17},{17,25},{25,1},{2,10},{10... | collective-permute-start | bytes 1572872 | tf_op jit(solution)/shard_map/ppermute | solution.py:430
  147.9 3.1 %collective-permute-start.15 = (f32[16,64,128]{2,1,0:T(8,128)S(1)}, f32[16,64,128]{2,1,0:T(8,128)S(1)}, u32[]{:S(2)}, u32[]{:S(2)}) collective-permute-start(f32[16,64,128]{2,1,0:T(8,128)S(1)} %get-tuple-element.111), channel_id=1, source_target_pairs={{8,0},{16,8},{24,16},{0,24},{9,1},{17,9},{25,17},{1,25},{10,2},{18... | collective-permute-start | bytes 1572872 | tf_op jit(solution)/shard_map/ppermute | solution.py:435
  154.7 21.8 %all_to_all.26.sums1 = f32[32,8,128]{2,1,0:T(8,128)S(1)} all-to-all(f32[32,8,128]{2,1,0:T(8,128)S(1)} %get-tuple-element.108), channel_id=1, replica_groups=mesh['sector'=4,'axial'=8] {'sector','axial'}, dimensions={0} | all-to-all | bytes 262144 | tf_op jit(solution)/shard_map/all_to_all | solution.py:425
  176.6 1.7 local.3.base
  178.3 3.1 %second_step.1 = (f32[64,64,128]{2,1,0:T(8,128)S(1)}, f32[64,64,128]{2,1,0:T(8,128)S(1)}, f32[64,64,128]{2,1,0:T(8,128)S(1)}, f32[32,8,128]{2,1,0:T(8,128)S(1)}) custom-call(f32[32,8,128]{2,1,0:T(8,128)S(1)} %all_to_all.25.sums.sums0, f32[32,8,128]{2,1,0:T(8,128)S(1)} %all_to_all.26.sums1, s32[64]{0:T(128)S(1)} %copy-done.1, ...), custom_call_target="tpu_custom_call", output_to_operand_aliasing={{0}: (13, {})} | custom-call | bytes 23462144 | tf_op jit(solution)/shard_map/second_step/pallas_call | solution.py:411
  181.4 11.9 %all_to_all.27.sums2 = f32[32,8,128]{2,1,0:T(8,128)S(1)} all-to-all(f32[32,8,128]{2,1,0:T(8,128)S(1)} %get-tuple-element.117), channel_id=1, replica_groups=mesh['sector'=4,'axial'=8] {'sector','axial'}, dimensions={0} | all-to-all | bytes 262144 | tf_op jit(solution)/shard_map/all_to_all | solution.py:425
  193.3 3.5 %last.1 = (f32[64,64,128]{2,1,0:T(8,128)}, f32[64,64,128]{2,1,0:T(8,128)}) custom-call(f32[32,8,128]{2,1,0:T(8,128)S(1)} %all_to_all.25.sums.sums0, f32[32,8,128]{2,1,0:T(8,128)S(1)} %all_to_all.26.sums1, f32[32,8,128]{2,1,0:T(8,128)S(1)} %all_to_all.27.sums2, f32[64,64,128]{2,1,0:T(8,128)S(1)} %get-tuple-element.106.field, ...), custom_call_target="tpu_custom_call" | custom-call | bytes 19267584 | tf_op jit(solution)/shard_map/last/pallas_call | solution.py:411
  (65 shorter events, 12.2 us)
Async XLA Ops:
  4.9 22.9 %collective-permute-start = (f32[16,72,128]{2,1,0:T(8,128)}, f32[16,72,128]{2,1,0:T(8,128)S(1)}, u32[]{:S(2)}, u32[]{:S(2)}) collective-permute-start(f32[16,72,128]{2,1,0:T(8,128)} %get-tuple-element.67), channel_id=1, source_target_pairs={{0,8},{8,16},{16,24},{24,0},{1,9},{9,17},{17,25},{25,1},{2,10},{10... | collective-permute-start | bytes 1769480 | tf_op jit(solution)/shard_map/ppermute | solution.py:430
  8.0 19.8 %collective-permute-start.1 = (f32[16,72,128]{2,1,0:T(8,128)}, f32[16,72,128]{2,1,0:T(8,128)S(1)}, u32[]{:S(2)}, u32[]{:S(2)}) collective-permute-start(f32[16,72,128]{2,1,0:T(8,128)} %get-tuple-element.68), channel_id=1, source_target_pairs={{0,1},{1,2},{2,3},{3,4},{4,5},{5,6},{6,7},{8,9},{9,10},{10,11},{11... | collective-permute-start | bytes 1769480 | tf_op jit(solution)/shard_map/ppermute | solution.py:430
  9.5 18.3 %collective-permute-start.2 = (s32[16]{0:T(128)S(1)}, s32[16]{0:T(128)S(1)}, u32[]{:S(2)}, u32[]{:S(2)}) collective-permute-start(s32[16]{0:T(128)S(1)} %get-tuple-element.69), channel_id=1, source_target_pairs={{0,8},{8,16},{16,24},{24,0},{1,9},{9,17},{17,25},{25,1},{2,10},{10... | collective-permute-start | bytes 200 | tf_op jit(solution)/shard_map/ppermute | solution.py:430
  11.1 16.7 %collective-permute-start.3 = (s32[16]{0:T(128)S(1)}, s32[16]{0:T(128)S(1)}, u32[]{:S(2)}, u32[]{:S(2)}) collective-permute-start(s32[16]{0:T(128)S(1)} %get-tuple-element.70), channel_id=1, source_target_pairs={{0,1},{1,2},{2,3},{3,4},{4,5},{5,6},{6,7},{8,9},{9,10},{10,11},{11... | collective-permute-start | bytes 200 | tf_op jit(solution)/shard_map/ppermute | solution.py:430
  27.8 22.3 %copy-start.3 = (f32[16,72,128]{2,1,0:T(8,128)}, f32[16,72,128]{2,1,0:T(8,128)S(1)}, u32[]{:S(2)}) copy-start(f32[16,72,128]{2,1,0:T(8,128)S(1)} %collective-permute-done.g0) | copy-start | bytes 1769476
  27.8 22.3 %copy-start.4 = (f32[16,72,128]{2,1,0:T(8,128)}, f32[16,72,128]{2,1,0:T(8,128)S(1)}, u32[]{:S(2)}) copy-start(f32[16,72,128]{2,1,0:T(8,128)S(1)} %collective-permute-done.1.g2) | copy-start | bytes 1769476
  31.6 14.9 %collective-permute-start.4 = (f32[16,64,128]{2,1,0:T(8,128)}, f32[16,64,128]{2,1,0:T(8,128)S(1)}, u32[]{:S(2)}, u32[]{:S(2)}) collective-permute-start(f32[16,64,128]{2,1,0:T(8,128)} %get-tuple-element.78), channel_id=1, source_target_pairs={{8,0},{16,8},{24,16},{0,24},{9,1},{17,9},{25,17},{1,25},{10,2},{18... | collective-permute-start | bytes 1572872 | tf_op jit(solution)/shard_map/ppermute | solution.py:435
  33.8 12.7 %collective-permute-start.5 = (f32[16,64,128]{2,1,0:T(8,128)}, f32[16,64,128]{2,1,0:T(8,128)S(1)}, u32[]{:S(2)}, u32[]{:S(2)}) collective-permute-start(f32[16,64,128]{2,1,0:T(8,128)} %get-tuple-element.79), channel_id=1, source_target_pairs={{1,0},{2,1},{3,2},{4,3},{5,4},{6,5},{7,6},{9,8},{10,9},{11,10},{12... | collective-permute-start | bytes 1572872 | tf_op jit(solution)/shard_map/ppermute | solution.py:435
  35.1 14.9 %all-to-all-start = ((f32[32,8,128]{2,1,0:T(8,128)}), f32[32,8,128]{2,1,0:T(8,128)S(1)}, u32[]{:S(2)}, u32[]{:S(2)}) async-start(f32[32,8,128]{2,1,0:T(8,128)} %bitcast.10), calls=%async_computation | async-start | bytes 262144 | tf_op jit(solution)/shard_map/all_to_all | solution.py:425
  46.5 3.5 %copy-start.6 = (f32[16,64,128]{2,1,0:T(8,128)}, f32[16,64,128]{2,1,0:T(8,128)S(1)}, u32[]{:S(2)}) copy-start(f32[16,64,128]{2,1,0:T(8,128)S(1)} %collective-permute-done.4.g1) | copy-start | bytes 1572868
  46.5 3.5 %copy-start.7 = (f32[16,64,128]{2,1,0:T(8,128)}, f32[16,64,128]{2,1,0:T(8,128)S(1)}, u32[]{:S(2)}) copy-start(f32[16,64,128]{2,1,0:T(8,128)S(1)} %collective-permute-done.5.g3) | copy-start | bytes 1572868
  50.0 5.9 %copy-start.5 = (f32[32,8,128]{2,1,0:T(8,128)}, f32[32,8,128]{2,1,0:T(8,128)S(1)}, u32[]{:S(2)}) copy-start(f32[32,8,128]{2,1,0:T(8,128)S(1)} %all-to-all-done) | copy-start | bytes 393220
  50.0 4.6 %copy-start.8 = (f32[4096]{0:T(1024)S(1)}, f32[4096]{0:T(1024)}, u32[]{:S(2)}) copy-start(f32[4096]{0:T(1024)} %param.16) | copy-start | bytes 49156
  50.0 5.3 %copy-start.13 = (s32[16]{0:T(128)S(1)}, s32[16]{0:T(128)}, u32[]{:S(2)}) copy-start(s32[16]{0:T(128)} %get-tuple-element.124.index1) | copy-start | bytes 196
  50.0 5.3 %copy-start.14 = (s32[16]{0:T(128)S(1)}, s32[16]{0:T(128)}, u32[]{:S(2)}) copy-start(s32[16]{0:T(128)} %get-tuple-element.125.index0) | copy-start | bytes 196
  50.0 5.3 %copy-start.16 = (s32[16]{0:T(128)S(1)}, s32[16]{0:T(128)}, u32[]{:S(2)}) copy-start(s32[16]{0:T(128)} %copy-done.15) | copy-start | bytes 196
  50.0 5.3 %copy-start.18 = (s32[16]{0:T(128)S(1)}, s32[16]{0:T(128)}, u32[]{:S(2)}) copy-start(s32[16]{0:T(128)} %copy-done.17) | copy-start | bytes 196
  50.1 53.7 %all-to-all-start.1 = ((f32[32,128,128]{2,1,0:T(8,128)}), f32[32,128,128]{2,1,0:T(8,128)S(1)}, u32[]{:S(2)}, u32[]{:S(2)}) async-start(f32[32,128,128]{2,1,0:T(8,128)} %bitcast.28), calls=%async_computation.1 | async-start | bytes 4194304 | tf_op jit(solution)/shard_map/all_to_all | solution.py:425
  64.1 29.4 %collective-permute-start.6 = (f32[16,128]{1,0:T(8,128)}, f32[16,128]{1,0:T(8,128)S(1)}, u32[]{:S(2)}, u32[]{:S(2)}) collective-permute-start(f32[16,128]{1,0:T(8,128)} %get-tuple-element.83), channel_id=1, source_target_pairs={{0,8},{8,16},{16,24},{24,0},{1,9},{9,17},{17,25},{25,1},{2,10},{10... | collective-permute-start | bytes 24584 | tf_op jit(solution)/shard_map/ppermute | solution.py:430
  66.1 27.4 %collective-permute-start.7 = (f32[16,128]{1,0:T(8,128)}, f32[16,128]{1,0:T(8,128)S(1)}, u32[]{:S(2)}, u32[]{:S(2)}) collective-permute-start(f32[16,128]{1,0:T(8,128)} %get-tuple-element.84), channel_id=1, source_target_pairs={{8,0},{16,8},{24,16},{0,24},{9,1},{17,9},{25,17},{1,25},{10,2},{18... | collective-permute-start | bytes 24584 | tf_op jit(solution)/shard_map/ppermute | solution.py:435
  67.9 25.6 %collective-permute-start.8 = (f32[16,128]{1,0:T(8,128)}, f32[16,128]{1,0:T(8,128)S(1)}, u32[]{:S(2)}, u32[]{:S(2)}) collective-permute-start(f32[16,128]{1,0:T(8,128)} %get-tuple-element.85), channel_id=1, source_target_pairs={{0,1},{1,2},{2,3},{3,4},{4,5},{5,6},{6,7},{8,9},{9,10},{10,11},{11... | collective-permute-start | bytes 24584 | tf_op jit(solution)/shard_map/ppermute | solution.py:430
  69.8 23.8 %collective-permute-start.9 = (f32[16,128]{1,0:T(8,128)}, f32[16,128]{1,0:T(8,128)S(1)}, u32[]{:S(2)}, u32[]{:S(2)}) collective-permute-start(f32[16,128]{1,0:T(8,128)} %get-tuple-element.86), channel_id=1, source_target_pairs={{1,0},{2,1},{3,2},{4,3},{5,4},{6,5},{7,6},{9,8},{10,9},{11,10},{12... | collective-permute-start | bytes 24584 | tf_op jit(solution)/shard_map/ppermute | solution.py:435
  94.1 9.6 %copy-start = (s32[256]{0:T(256)S(1)}, s32[256]{0:T(256)}, u32[]{:S(2)}) copy-start(s32[256]{0:T(256)} %select_reduce_fusion.tags) | copy-start | bytes 3076
  94.1 9.6 %copy-start.2 = (s32[64]{0:T(128)S(1)}, s32[64]{0:T(128)}, u32[]{:S(2)}) copy-start(s32[64]{0:T(128)} %get-tuple-element.123.picked) | copy-start | bytes 772
  111.0 32.3 %collective-permute-start.10 = (f32[16,64,128]{2,1,0:T(8,128)S(1)}, f32[16,64,128]{2,1,0:T(8,128)S(1)}, u32[]{:S(2)}, u32[]{:S(2)}) collective-permute-start(f32[16,64,128]{2,1,0:T(8,128)S(1)} %get-tuple-element.97), channel_id=1, source_target_pairs={{0,8},{8,16},{16,24},{24,0},{1,9},{9,17},{17,25},{25,1},{2,10},{10... | collective-permute-start | bytes 1572872 | tf_op jit(solution)/shard_map/ppermute | solution.py:430
  116.8 26.5 %collective-permute-start.11 = (f32[16,64,128]{2,1,0:T(8,128)S(1)}, f32[16,64,128]{2,1,0:T(8,128)S(1)}, u32[]{:S(2)}, u32[]{:S(2)}) collective-permute-start(f32[16,64,128]{2,1,0:T(8,128)S(1)} %get-tuple-element.98), channel_id=1, source_target_pairs={{8,0},{16,8},{24,16},{0,24},{9,1},{17,9},{25,17},{1,25},{10,2},{18... | collective-permute-start | bytes 1572872 | tf_op jit(solution)/shard_map/ppermute | solution.py:435
  116.8 26.5 %collective-permute-start.12 = (f32[16,64,128]{2,1,0:T(8,128)S(1)}, f32[16,64,128]{2,1,0:T(8,128)S(1)}, u32[]{:S(2)}, u32[]{:S(2)}) collective-permute-start(f32[16,64,128]{2,1,0:T(8,128)S(1)} %get-tuple-element.99), channel_id=1, source_target_pairs={{0,1},{1,2},{2,3},{3,4},{4,5},{5,6},{6,7},{8,9},{9,10},{10,11},{11... | collective-permute-start | bytes 1572872 | tf_op jit(solution)/shard_map/ppermute | solution.py:430
  118.1 25.2 %collective-permute-start.13 = (f32[16,64,128]{2,1,0:T(8,128)S(1)}, f32[16,64,128]{2,1,0:T(8,128)S(1)}, u32[]{:S(2)}, u32[]{:S(2)}) collective-permute-start(f32[16,64,128]{2,1,0:T(8,128)S(1)} %get-tuple-element.100), channel_id=1, source_target_pairs={{1,0},{2,1},{3,2},{4,3},{5,4},{6,5},{7,6},{9,8},{10,9},{11,10},{12... | collective-permute-start | bytes 1572872 | tf_op jit(solution)/shard_map/ppermute | solution.py:435
  144.8 33.5 %collective-permute-start.14 = (f32[16,64,128]{2,1,0:T(8,128)S(1)}, f32[16,64,128]{2,1,0:T(8,128)S(1)}, u32[]{:S(2)}, u32[]{:S(2)}) collective-permute-start(f32[16,64,128]{2,1,0:T(8,128)S(1)} %get-tuple-element.110), channel_id=1, source_target_pairs={{0,8},{8,16},{16,24},{24,0},{1,9},{9,17},{17,25},{25,1},{2,10},{10... | collective-permute-start | bytes 1572872 | tf_op jit(solution)/shard_map/ppermute | solution.py:430
  147.9 30.4 %collective-permute-start.15 = (f32[16,64,128]{2,1,0:T(8,128)S(1)}, f32[16,64,128]{2,1,0:T(8,128)S(1)}, u32[]{:S(2)}, u32[]{:S(2)}) collective-permute-start(f32[16,64,128]{2,1,0:T(8,128)S(1)} %get-tuple-element.111), channel_id=1, source_target_pairs={{8,0},{16,8},{24,16},{0,24},{9,1},{17,9},{25,17},{1,25},{10,2},{18... | collective-permute-start | bytes 1572872 | tf_op jit(solution)/shard_map/ppermute | solution.py:435
  150.9 27.3 %collective-permute-start.16 = (f32[16,64,128]{2,1,0:T(8,128)S(1)}, f32[16,64,128]{2,1,0:T(8,128)S(1)}, u32[]{:S(2)}, u32[]{:S(2)}) collective-permute-start(f32[16,64,128]{2,1,0:T(8,128)S(1)} %get-tuple-element.112), channel_id=1, source_target_pairs={{0,1},{1,2},{2,3},{3,4},{4,5},{5,6},{6,7},{8,9},{9,10},{10,11},{11... | collective-permute-start | bytes 1572872 | tf_op jit(solution)/shard_map/ppermute | solution.py:430
  152.3 26.0 %collective-permute-start.17 = (f32[16,64,128]{2,1,0:T(8,128)S(1)}, f32[16,64,128]{2,1,0:T(8,128)S(1)}, u32[]{:S(2)}, u32[]{:S(2)}) collective-permute-start(f32[16,64,128]{2,1,0:T(8,128)S(1)} %get-tuple-element.113), channel_id=1, source_target_pairs={{1,0},{2,1},{3,2},{4,3},{5,4},{6,5},{7,6},{9,8},{10,9},{11,10},{12... | collective-permute-start | bytes 1572872 | tf_op jit(solution)/shard_map/ppermute | solution.py:435
  (7 other events, 5.2 us)

commit v3 on v2

--- a/solution.py
+++ b/solution.py
@@ -13,10 +13,11 @@
 HBM = pl.BlockSpec(memory_space=pltpu.HBM)
 SMEM = pl.BlockSpec(memory_space=pltpu.SMEM)
 NT = (((1,), (1,)), ((), ()))
-CHUNK = 16
+CHUNK = 32
 GROUP = 16
 LIMIT = 14 << 20
 WIDE = 60 << 20
+STRIPES = 4
 
 
 def struct(*shape, dtype=F32):
@@ -141,7 +142,7 @@
         lax.fori_loop(0, count, one, 0, unroll=4)
 
 
-def gather_kernel(index0, index1, loads, gains, out0, out1, sems):
+def gather_kernel(index0, index1, far0, far1, loads, gains, out0, out1, sems):
     bn = loads.shape[1]
     count = out0.shape[0]
     copies = []
@@ -151,25 +152,27 @@
     for copy in copies:
         copy.start()
     if out0.shape[1] > bn:
-        for which, out in enumerate((out0, out1)):
+        lane = iota((1, 128), 1)
+        for which, (far, out) in enumerate(((far0, out0), (far1, out1))):
             rows = jnp.concatenate([gains[which], gains[which]], axis=1)
             for k in range(count):
-                out[k, pl.ds(bn, 8), :] = jnp.broadcast_to(rows[k : k + 1], (8, 128))
+                row = jnp.where(lane < bn, rows[k : k + 1], far[k].astype(F32))
+                out[k, pl.ds(bn, 8), :] = jnp.broadcast_to(row, (8, 128))
     for copy in copies:
         copy.wait()
 
 
-def gather_call(index0, index1, loads, gains, extra):
+def gather_call(index0, index1, far0, far1, loads, gains, extra):
     out = struct(index0.shape[0], loads.shape[1] + extra, loads.shape[2])
     return pl.pallas_call(
         gather_kernel,
-        in_specs=[SMEM, SMEM, pl.BlockSpec(memory_space=pl.ANY), VMEM],
+        in_specs=[SMEM, SMEM, SMEM, SMEM, pl.BlockSpec(memory_space=pl.ANY), VMEM],
         out_specs=[VMEM, VMEM],
         out_shape=[out, out],
         scratch_shapes=[pltpu.SemaphoreType.DMA((2,))],
         compiler_params=pltpu.CompilerParams(vmem_limit_bytes=WIDE),
         name="gather",
-    )(index0, index1, loads, gains)
+    )(index0, index1, far0, far1, loads, gains)
 
 
 def diagonal_kernel(
@@ -251,14 +254,14 @@
 
 
 def assemble_kernel(
-    tags, picked, payload, start_in, field_in, inverse_in, loads_in, gains_in,
-    image, blocks, after, s0, s1, s2, s3, partial, field, inverse, loads, gains, packed, sems,
+    tags, picked, payload, start_in, field_in, inverse_in, gains_in,
+    image, blocks, after, s0, s1, s2, s3, field, inverse, gains, packed, sems,
 ):
     patch_dev, bn, _ = image.shape
     half, quarter = bn // 2, bn // 4
     banks = packed.shape[0]
     slots = tags.shape[0]
-    pairs = ((start_in, image), (field_in, field), (inverse_in, inverse), (loads_in, loads), (gains_in, gains))
+    pairs = ((start_in, image), (field_in, field), (inverse_in, inverse), (gains_in, gains))
     fetches = [pltpu.make_async_copy(src, dst, sems.at[i]) for i, (src, dst) in enumerate(pairs)]
     for copy in fetches:
         copy.start()
@@ -307,16 +310,14 @@
         copy.wait()
 
     def finish(p, carry):
-        here, value = image[p], field[p]
-        after[p] = inverse[p] * here
-        return carry[0] + folded(loads[p] * value), carry[1] + folded(here * value)
-
-    sums = lax.fori_loop(0, patch_dev, finish, zeros(2), unroll=2)
+        after[p] = inverse[p] * image[p]
+        return carry
+
+    lax.fori_loop(0, patch_dev, finish, 0, unroll=2)
     send_values(picked, gains, after, (s0, s1, s2, s3))
-    publish(partial, sums)
-
-
-def local_kernel(blocks, field, base, result):
+
+
+def times_all(blocks, field, base, result):
     def some(j, carry):
         group = [j * GROUP + g for g in range(GROUP)]
         products = [dot(blocks[p], stacked(field[p])) for p in group]
@@ -327,6 +328,16 @@
     lax.fori_loop(0, field.shape[0] // GROUP, some, 0)
 
 
+def first_local_kernel(blocks, after, image, loads, field, result, partial):
+    times_all(blocks, after, image, result)
+
+    def one(p, carry):
+        value = field[p]
+        return carry[0] + folded(loads[p] * value), carry[1] + folded(image[p] * value)
+
+    publish(partial, lax.fori_loop(0, loads.shape[0], one, zeros(2), unroll=2))
+
+
 def second_kernel(picked, placed, inverse, gains, g0, g1, g2, g3, base, result, after, s0, s1, s2, s3):
     take_values(placed, (g0, g1, g2, g3), result)
 
@@ -338,7 +349,10 @@
     send_values(picked, gains, after, (s0, s1, s2, s3))
 
 
-def first_step_kernel(sums, loads, field, image, second, inverse, left, left_image, partial):
+def first_step_kernel(
+    sums, blocks, after, loads, field, image, second, inverse, result, left, left_image, partial
+):
+    times_all(blocks, after, second, result)
     first = gathered(sums)
     alpha = first[0:1] / first[1:2]
 
@@ -386,7 +400,9 @@
     publish(partial, lax.fori_loop(0, field.shape[0], one, zeros(3)))
 
 
-def last_kernel(sums0, sums1, sums2, field, image, inverse, r1, w1, r2, w2, estimate, left):
+def last_kernel(
+    sums0, sums1, sums2, field, image, inverse, r1, w1, r2, w2, estimate_out, left_out, estimate, left, sems
+):
     first, then, last = gathered(sums0), gathered(sums1), gathered(sums2)
     alpha0 = first[0:1] / first[1:2]
     beta1 = then[0:1] / first[0:1]
@@ -402,16 +418,25 @@
         left[p] = r2[p] - alpha2 * (w2[p] + beta2 * (w1[p] + beta1 * image[p]))
         return carry
 
-    lax.fori_loop(0, field.shape[0], one, 0, unroll=2)
-
-
-def call(kernel, name, ins, outs, scratch=(), flops=0, alias=None, limit=None, far=()):
+    size = field.shape[0] // STRIPES
+    copies = []
+    for c in range(STRIPES):
+        lax.fori_loop(c * size, (c + 1) * size, one, 0, unroll=2)
+        part = pl.ds(c * size, size)
+        for i, (src, dst) in enumerate(((estimate, estimate_out), (left, left_out))):
+            copies.append(pltpu.make_async_copy(src.at[part], dst.at[part], sems.at[i, c]))
+            copies[-1].start()
+    for copy in copies:
+        copy.wait()
+
+
+def call(kernel, name, ins, outs, scratch=(), flops=0, alias=None, limit=None, far=(), out=VMEM):
     ints = lambda a: a.ndim == 1 and a.dtype == jnp.int32
     moved = sum(a.size * a.dtype.itemsize for a in ins) + sum(s.size * s.dtype.itemsize for s in outs)
     return pl.pallas_call(
         kernel,
         in_specs=[SMEM if ints(a) else HBM if i in far else VMEM for i, a in enumerate(ins)],
-        out_specs=[VMEM] * len(outs),
+        out_specs=[out] * len(outs),
         out_shape=list(outs),
         scratch_shapes=list(scratch),
         input_output_aliases=alias or {},
@@ -457,19 +482,17 @@
 
     table = links.transpose(0, 2, 1)
     own_sector, own_axial = table[0, 0], table[1, 0]
-    s0, s2 = gather_call(own_sector, own_axial, loads, conduct, 8)
-    owners, far_sector, far_axial, s0, s2 = lax.optimization_barrier((owners, table[0, 1], table[1, 1], s0, s2))
+    s0, s2 = gather_call(own_sector, own_axial, table[0, 1], table[1, 1], loads, conduct, 8)
+    owners, s0, s2 = lax.optimization_barrier((owners, s0, s2))
     g0, g2 = onward(s0, "sector", True), onward(s2, "axial", False)
-    far_sector, far_axial = onward(far_sector, "sector", True), onward(far_axial, "axial", False)
     payload, meta = pack_call(
         devices, owners.reshape(elems), patch_ids, counts,
         kbb.transpose(1, 2, 0), interior.transpose(0, 2, 1), node_lists.T,
     )
     slots = meta.shape[0]
-    payload, meta, g0, g2, far_sector, far_axial = lax.optimization_barrier(
-        (payload, meta, g0, g2, far_sector, far_axial)
-    )
-    s1, s3 = gather_call(far_sector, far_axial, loads, conduct, 0)
+    payload, meta, g0, g2 = lax.optimization_barrier((payload, meta, g0, g2))
+    far_sector, far_axial = g0[:, bn, bn].astype(jnp.int32), g2[:, bn, bn].astype(jnp.int32)
+    s1, s3 = gather_call(far_sector, far_axial, far_sector, far_axial, loads, conduct, 0)
     meta, s1, s3 = lax.optimization_barrier((meta, s1, s3))
     g1, g3 = back(s1, "sector", True), back(s3, "axial", False)
     meta = everywhere(meta.reshape(devices, slots // devices, 128)).reshape(slots, 128)
@@ -490,28 +513,28 @@
     (start,) = call(edges_kernel, "edges", (placed, loads, *rows, g0, g1, g2, g3), (vec,), limit=WIDE)
     image, blocks, after, *rest = call(
         assemble_kernel, "assemble",
-        (tags, picked, payload, start, field, inverse, loads, gains),
-        (vec, struct(patch_dev, bn, 3 * bn, dtype=BF16), vec, buf, buf, buf, buf, total,
-         vec, vec, vec, struct(4 * count, bn, cases)),
-        (pltpu.VMEM((4, patch_dev + 1, bn // 4, 128), F32), pltpu.SemaphoreType.DMA((5,))),
-        far=(3, 4, 5, 6, 7),
-    )
-    *sends, partial, field, inverse, loads, gains = rest
+        (tags, picked, payload, start, field, inverse, gains),
+        (vec, struct(patch_dev, bn, 3 * bn, dtype=BF16), vec, buf, buf, buf, buf,
+         vec, vec, struct(4 * count, bn, cases)),
+        (pltpu.VMEM((4, patch_dev + 1, bn // 4, 128), F32), pltpu.SemaphoreType.DMA((4,))),
+        far=(3, 4, 5, 6),
+    )
+    *sends, field, inverse, gains = rest
     got = exchange(*sends)
+    base, partial = call(first_local_kernel, "first_local", (blocks, after, image, loads, field), (vec, total))
     sums0 = everywhere(partial)
-    after, sums0 = lax.optimization_barrier((after, sums0))
-    (base,) = call(local_kernel, "local", (blocks, after, image), (vec,))
+    base, sums0 = lax.optimization_barrier((base, sums0))
     second, after, *sends = call(
         second_kernel, "second", (picked, placed, inverse, gains, *got, base),
         (vec, vec, buf, buf, buf, buf), alias={8: 0},
     )
     got = exchange(*sends)
-    r1, w1, partial = call(
-        first_step_kernel, "first_step", (sums0, loads, field, image, second, inverse), (vec, vec, total)
+    base, r1, w1, partial = call(
+        first_step_kernel, "first_step",
+        (sums0, blocks, after, loads, field, image, second, inverse), (vec, vec, vec, total),
     )
     sums1 = everywhere(partial)
-    after, sums1 = lax.optimization_barrier((after, sums1))
-    (base,) = call(local_kernel, "local", (blocks, after, second), (vec,))
+    base, sums1 = lax.optimization_barrier((base, sums1))
     _, r2, w2, partial = call(
         second_step_kernel, "second_step",
         (sums0, sums1, placed, *got, field, image, second, r1, w1, inverse, base),
@@ -519,7 +542,9 @@
     )
     sums2 = everywhere(partial)
     estimate, left = call(
-        last_kernel, "last", (sums0, sums1, sums2, field, image, inverse, r1, w1, r2, w2), (vec, vec)
+        last_kernel, "last", (sums0, sums1, sums2, field, image, inverse, r1, w1, r2, w2), (vec, vec),
+        (pltpu.VMEM(loads.shape, F32), pltpu.VMEM(loads.shape, F32), pltpu.SemaphoreType.DMA((2, STRIPES))),
+        out=pl.BlockSpec(memory_space=pl.ANY),
     )
     return estimate.reshape(points, cases), left.reshape(points, cases)
 

time: 198 us -> 189 us (0.955)
  starting transfers between devices: 45.5 us -> 39.9 us
  blocking collectives: 55.8 us -> 51.9 us
  Pallas kernels: 50.3 us -> 48 us
  waiting for transfers between devices: 39 us -> 41.1 us
    ppermute x10 -> x8, starting transfers between devices: 25.2 us -> 19.7 us  [onward(): lax.ppermute(value, axis, [(i, (i + 1) % n) for i in range(n) if wrap or...]
    all_to_all x3, blocking collectives: 55.8 us -> 51.9 us  [everywhere(): lax.all_to_all(partial, AXES, split_axis=0, concat_axis=0, tiled=True)]
    ppermute x10 -> x8, waiting for transfers between devices: 22.5 us -> 25.2 us  [onward(): lax.ppermute(value, axis, [(i, (i + 1) % n) for i in range(n) if wrap or...]
    pallas_call x9 -> x8, Pallas kernels: 31.7 us -> 31.1 us  [call(): pl.pallas_call(kernel, in_specs=[SMEM if ints(a) else HBM if i in far els...]
  transfers between devices with their start and end apart: 20 -> 18, of which waited for: 4 -> 5; matrix products, arithmetic and copies ran while one was open for 1% -> 1% of each run, Pallas kernels for 15% -> 15%
where the time goes in v3:
time: 189 us; the launch traced here: 188 us
  blocking collectives  51.9 us (27%)
  Pallas kernels  48 us (25%)
  waiting for transfers between devices  41.1 us (22%)
  starting transfers between devices  39.9 us (21%)
  local copies, waits for them, and re-layouts  2.69 us (1%)
  other arithmetic  2.68 us (1%)
    all_to_all x3, blocking collectives, everywhere(): lax.all_to_all(partial, AXES, split_axis=0, concat_axis=0, tiled=True)  51.9 us
    pallas_call x8, Pallas kernels, call(): pl.pallas_call(kernel, in_specs=[SMEM if ints(a) else HBM if i in far els...  31.1 us
    ppermute x8, waiting for transfers between devices, onward(): lax.ppermute(value, axis, [(i, (i + 1) % n) for i in range(n) if wrap or...  25.2 us
    ppermute x8, starting transfers between devices, onward(): lax.ppermute(value, axis, [(i, (i + 1) % n) for i in range(n) if wrap or...  19.7 us
    ppermute x8, starting transfers between devices, back(): lax.ppermute(value, axis, [((i + 1) % n, i) for i in range(n) if wrap or...  11.9 us
    pallas_call x1, Pallas kernels, pack_call(): pl.pallas_call(functools.partial(pack_kernel, slots_each), grid=(elems //...  10.7 us
    all_to_all x2, waiting for transfers between devices, everywhere(): lax.all_to_all(partial, AXES, split_axis=0, concat_axis=0, tiled=True)  8.96 us
    all_to_all x2, starting transfers between devices, everywhere(): lax.all_to_all(partial, AXES, split_axis=0, concat_axis=0, tiled=True)  8.23 us
  transfers between devices with their start and end apart: 18, of which 5 were waited for; matrix products, arithmetic and copies ran while one was open for 1% of the time, Pallas kernels for 15%

profile of v3, /device:TPU:0, one launch (start us, length us, event | category | flops | bytes accessed | tf_op | source)
XLA Modules:
  0.0 187.8 jit_solution(4722480155388688093)
XLA Ops:
  0.6 1.4 slice_bitcast_fusion
  2.0 3.0 %gather.2 = (f32[16,72,128]{2,1,0:T(8,128)}, f32[16,72,128]{2,1,0:T(8,128)}) custom-call(s32[16]{0:T(128)} %get-tuple-element.121.index0, s32[16]{0:T(128)} %get-tuple-element.120.index1, s32[16]{0:T(128)} %get-tuple-element.119.far0, s32[16]{0:T(128)} %get-tuple-element.118.far1, f32[64,64,128]{2,1,0:T(8,128)} %bitcast.20, f32[2,16,64]{2,1,0:T(8,128)} %conduct.1), custom_call_target="tpu_custom_call" | custom-call | tf_op jit(solution)/shard_map/gather/pallas_call | solution.py:167
  5.0 3.0 %collective-permute-start = (f32[16,72,128]{2,1,0:T(8,128)}, f32[16,72,128]{2,1,0:T(8,128)S(1)}, u32[]{:S(2)}, u32[]{:S(2)}) collective-permute-start(f32[16,72,128]{2,1,0:T(8,128)} %get-tuple-element.64), channel_id=1, source_target_pairs={{0,8},{8,16},{16,24},{24,0},{1,9},{9,17},{17,25},{25,1},{2,10},{10... | collective-permute-start | bytes 1769480 | tf_op jit(solution)/shard_map/ppermute | solution.py:455
  8.0 1.5 collective-permute-start.1
  10.2 10.7 %pack.1 = (f32[4096,128]{1,0:T(8,128)}, f32[256,128]{1,0:T(8,128)}) custom-call(s32[128]{0:T(128)} %bitcast.34, s32[128]{0:T(128)} %patches.1, s32[1]{0:T(128)S(6)} %copy.16.counts, f32[64,64,128]{2,1,0:T(8,128)} %bitcast.28, bf16[128,64,256]{2,1,0:T(8,128)(2,1)} %bitcast.27, s32[64,128]{1,0:T(8,128)} %bitcast.32), custom_call_target="tpu_custom_call" | custom-call | tf_op jit(solution)/shard_map/pack/pallas_call | solution.py:99
  20.9 2.7 %collective-permute-done.g0 = f32[16,72,128]{2,1,0:T(8,128)S(1)} collective-permute-done((f32[16,72,128]{2,1,0:T(8,128)}, f32[16,72,128]{2,1,0:T(8,128)S(1)}, u32[]{:S(2)}, u32[]{:S(2)}) %collective-permute-start) | collective-permute-done | bytes 589856 | tf_op jit(solution)/shard_map/ppermute | solution.py:455
  24.8 3.2 %gather.3 = (f32[16,64,128]{2,1,0:T(8,128)}, f32[16,64,128]{2,1,0:T(8,128)}) custom-call(s32[16]{0:T(128)} %get-tuple-element.123.index0.far0, s32[16]{0:T(128)} %get-tuple-element.122.index1.far1, s32[16]{0:T(128)} %get-tuple-element.123.index0.far0, s32[16]{0:T(128)} %get-tuple-element.122.index1.far1, f32[64,64,128]{2,1,0:T(8,128)} %bitcast.21, ...), custom_call_target="tpu_custom_call" | custom-call | tf_op jit(solution)/shard_map/gather/pallas_call | solution.py:167
  28.1 1.7 collective-permute-start.2
  31.1 4.1 %all-to-all-start = ((f32[32,8,128]{2,1,0:T(8,128)}), f32[32,8,128]{2,1,0:T(8,128)S(1)}, u32[]{:S(2)}, u32[]{:S(2)}) async-start(f32[32,8,128]{2,1,0:T(8,128)} %bitcast.10), calls=%async_computation | async-start | bytes 262144 | tf_op jit(solution)/shard_map/all_to_all | solution.py:450
  35.1 7.0 %collective-permute-done.2.g1 = f32[16,64,128]{2,1,0:T(8,128)S(1)} collective-permute-done((f32[16,64,128]{2,1,0:T(8,128)}, f32[16,64,128]{2,1,0:T(8,128)S(1)}, u32[]{:S(2)}, u32[]{:S(2)}) %collective-permute-start.2) | collective-permute-done | bytes 524320 | tf_op jit(solution)/shard_map/ppermute | solution.py:460
  42.1 3.8 %all-to-all-done = f32[32,8,128]{2,1,0:T(8,128)S(1)} async-done(((f32[32,8,128]{2,1,0:T(8,128)}), f32[32,8,128]{2,1,0:T(8,128)S(1)}, u32[]{:S(2)}, u32[]{:S(2)}) %all-to-all-start) | async-done | bytes 131104 | tf_op jit(solution)/shard_map/all_to_all | solution.py:450
  46.0 4.2 %all-to-all-start.1 = ((f32[32,128,128]{2,1,0:T(8,128)}), f32[32,128,128]{2,1,0:T(8,128)S(1)}, u32[]{:S(2)}, u32[]{:S(2)}) async-start(f32[32,128,128]{2,1,0:T(8,128)} %bitcast.29), calls=%async_computation.1 | async-start | bytes 4194304 | tf_op jit(solution)/shard_map/all_to_all | solution.py:450
  52.3 7.4 %diagonal.1 = (f32[64,64,128]{2,1,0:T(8,128)}, f32[64,64,128]{2,1,0:T(8,128)}, f32[64,64,128]{2,1,0:T(8,128)}, f32[16,128]{1,0:T(8,128)}, f32[16,128]{1,0:T(8,12...) custom-call(s32[256]{0:T(256)} %select_reduce_fusion.tags, s32[64]{0:T(128)} %get-tuple-element.117.picked, ...), custom_call_target="tpu_custom_call" | custom-call | bytes 9757952 | tf_op jit(solution)/shard_map/diagonal/pallas_call | solution.py:436
  59.7 1.9 %collective-permute-start.4 = (f32[16,128]{1,0:T(8,128)}, f32[16,128]{1,0:T(8,128)S(1)}, u32[]{:S(2)}, u32[]{:S(2)}) collective-permute-start(f32[16,128]{1,0:T(8,128)} %get-tuple-element.76), channel_id=1, source_target_pairs={{0,8},{8,16},{16,24},{24,0},{1,9},{9,17},{17,25},{25,1},{2,10},{10... | collective-permute-start | bytes 24584 | tf_op jit(solution)/shard_map/ppermute | solution.py:455
  61.6 2.0 %collective-permute-start.5 = (f32[16,128]{1,0:T(8,128)}, f32[16,128]{1,0:T(8,128)S(1)}, u32[]{:S(2)}, u32[]{:S(2)}) collective-permute-start(f32[16,128]{1,0:T(8,128)} %get-tuple-element.77), channel_id=1, source_target_pairs={{8,0},{16,8},{24,16},{0,24},{9,1},{17,9},{25,17},{1,25},{10,2},{18... | collective-permute-start | bytes 24584 | tf_op jit(solution)/shard_map/ppermute | solution.py:460
  63.6 1.7 collective-permute-start.6
  66.7 22.4 %collective-permute-done.4.t0 = f32[16,128]{1,0:T(8,128)S(1)} collective-permute-done((f32[16,128]{1,0:T(8,128)}, f32[16,128]{1,0:T(8,128)S(1)}, u32[]{:S(2)}, u32[]{:S(2)}) %collective-permute-start.4) | collective-permute-done | bytes 8224 | tf_op jit(solution)/shard_map/ppermute | solution.py:455
  89.7 4.5 %edges.1.start_in = f32[64,64,128]{2,1,0:T(8,128)} custom-call(s32[64]{0:T(128)} %get-tuple-element.116.placed, f32[64,64,128]{2,1,0:T(8,128)} %bitcast.23, f32[16,128]{1,0:T(8,128)} %copy-done.10, f32[16,128]{1,0:T(8,128)} %copy-done.11, f32[16,128]{1,0:T(8,128)} %copy-done.12, f32[16,128]{1,0:T(8,128)} %copy-done.13, f32[16,72,128]{2,1,0:T(8,128)} %copy-done.4, ...), custom_call_target="tpu_custom_call" | custom-call | bytes 6455552 | tf_op jit(solution)/shard_map/edges/pallas_call | solution.py:436
  94.2 5.1 %all-to-all-done.1 = f32[32,128,128]{2,1,0:T(8,128)S(1)} async-done(((f32[32,128,128]{2,1,0:T(8,128)}), f32[32,128,128]{2,1,0:T(8,128)S(1)}, u32[]{:S(2)}, u32[]{:S(2)}) %all-to-all-start.1) | async-done | bytes 2097184 | tf_op jit(solution)/shard_map/all_to_all | solution.py:450
  99.3 6.9 %assemble.1 = (f32[64,64,128]{2,1,0:T(8,128)S(1)}, bf16[64,64,192]{2,1,0:T(8,128)(2,1)S(1)}, f32[64,64,128]{2,1,0:T(8,128)S(1)}, f32[16,64,128]{2,1,0:T(8,128)S(...) custom-call(s32[256]{0:T(256)S(1)} %copy-done.1, ...), custom_call_target="tpu_custom_call" | custom-call | bytes 24642816 | tf_op jit(solution)/shard_map/assemble/pallas_call | solution.py:436
  106.3 5.8 %collective-permute-start.8 = (f32[16,64,128]{2,1,0:T(8,128)S(1)}, f32[16,64,128]{2,1,0:T(8,128)S(1)}, u32[]{:S(2)}, u32[]{:S(2)}) collective-permute-start(f32[16,64,128]{2,1,0:T(8,128)S(1)} %get-tuple-element.94), channel_id=1, source_target_pairs={{0,8},{8,16},{16,24},{24,0},{1,9},{9,17},{17,25},{25,1},{2,10},{10... | collective-permute-start | bytes 1572872 | tf_op jit(solution)/shard_map/ppermute | solution.py:455
  112.1 1.3 collective-permute-start.10
  114.8 2.3 %first_local.1 = (f32[64,64,128]{2,1,0:T(8,128)S(1)}, f32[32,8,128]{2,1,0:T(8,128)S(1)}) custom-call(bf16[64,64,192]{2,1,0:T(8,128)(2,1)S(1)} %get-tuple-element.85.blocks, f32[64,64,128]{2,1,0:T(8,128)S(1)} %get-tuple-element.86.after, f32[64,64,128]{2,1,0:T(8,128)S(1)} %get-tuple-element.87.image, f32[64,64,128]{2,1,0:T(8,128)S(1)} %bitcast.24, ...), custom_call_target="tpu_custom_call" | custom-call | bytes 12189696 | tf_op jit(solution)/shard_map/first_local/pallas_call | solution.py:436
  117.0 19.9 %all_to_all.25.sums.sums0 = f32[32,8,128]{2,1,0:T(8,128)S(1)} all-to-all(f32[32,8,128]{2,1,0:T(8,128)S(1)} %get-tuple-element.90), channel_id=1, replica_groups=mesh['sector'=4,'axial'=8] {'sector','axial'}, dimensions={0} | all-to-all | bytes 262144 | tf_op jit(solution)/shard_map/all_to_all | solution.py:450
  136.9 1.5 second.1
  138.4 3.1 %collective-permute-start.12 = (f32[16,64,128]{2,1,0:T(8,128)S(1)}, f32[16,64,128]{2,1,0:T(8,128)S(1)}, u32[]{:S(2)}, u32[]{:S(2)}) collective-permute-start(f32[16,64,128]{2,1,0:T(8,128)S(1)} %get-tuple-element.104), channel_id=1, source_target_pairs={{0,8},{8,16},{16,24},{24,0},{1,9},{9,17},{17,25},{25,1},{2,10},{10... | collective-permute-start | bytes 1572872 | tf_op jit(solution)/shard_map/ppermute | solution.py:455
  141.5 3.0 %collective-permute-start.13 = (f32[16,64,128]{2,1,0:T(8,128)S(1)}, f32[16,64,128]{2,1,0:T(8,128)S(1)}, u32[]{:S(2)}, u32[]{:S(2)}) collective-permute-start(f32[16,64,128]{2,1,0:T(8,128)S(1)} %get-tuple-element.105), channel_id=1, source_target_pairs={{8,0},{16,8},{24,16},{0,24},{9,1},{17,9},{25,17},{1,25},{10,2},{18... | collective-permute-start | bytes 1572872 | tf_op jit(solution)/shard_map/ppermute | solution.py:460
  147.2 2.8 %first_step.1 = (f32[64,64,128]{2,1,0:T(8,128)S(1)}, f32[64,64,128]{2,1,0:T(8,128)S(1)}, f32[64,64,128]{2,1,0:T(8,128)S(1)}, f32[32,8,128]{2,1,0:T(8,128)S(1)}) custom-call(f32[32,8,128]{2,1,0:T(8,128)S(1)} %all_to_all.25.sums.sums0, bf16[64,64,192]{2,1,0:T(8,128)(2,1)S(1)} %get-tuple-element.85.blocks, f32[64,64,128]{2,1,0:T(8,128)S(1)} %get-tuple-element.99.after, ...), custom_call_target="tpu_custom_call" | custom-call | bytes 20709376 | tf_op jit(solution)/shard_map/first_step/pallas_call | solution.py:436
  150.0 20.4 %all_to_all.26.sums1 = f32[32,8,128]{2,1,0:T(8,128)S(1)} all-to-all(f32[32,8,128]{2,1,0:T(8,128)S(1)} %get-tuple-element.102), channel_id=1, replica_groups=mesh['sector'=4,'axial'=8] {'sector','axial'}, dimensions={0} | all-to-all | bytes 262144 | tf_op jit(solution)/shard_map/all_to_all | solution.py:450
  170.4 3.2 %second_step.1 = (f32[64,64,128]{2,1,0:T(8,128)S(1)}, f32[64,64,128]{2,1,0:T(8,128)S(1)}, f32[64,64,128]{2,1,0:T(8,128)S(1)}, f32[32,8,128]{2,1,0:T(8,128)S(1)}) custom-call(f32[32,8,128]{2,1,0:T(8,128)S(1)} %all_to_all.25.sums.sums0, f32[32,8,128]{2,1,0:T(8,128)S(1)} %all_to_all.26.sums1, s32[64]{0:T(128)S(1)} %copy-done.2, ...), custom_call_target="tpu_custom_call", output_to_operand_aliasing={{0}: (13, {})} | custom-call | bytes 23462144 | tf_op jit(solution)/shard_map/second_step/pallas_call | solution.py:436
  173.6 11.6 %all_to_all.27.sums2 = f32[32,8,128]{2,1,0:T(8,128)S(1)} all-to-all(f32[32,8,128]{2,1,0:T(8,128)S(1)} %get-tuple-element.111), channel_id=1, replica_groups=mesh['sector'=4,'axial'=8] {'sector','axial'}, dimensions={0} | all-to-all | bytes 262144 | tf_op jit(solution)/shard_map/all_to_all | solution.py:450
  185.2 2.6 %last.1 = (f32[64,64,128]{2,1,0:T(8,128)}, f32[64,64,128]{2,1,0:T(8,128)}) custom-call(f32[32,8,128]{2,1,0:T(8,128)S(1)} %all_to_all.25.sums.sums0, f32[32,8,128]{2,1,0:T(8,128)S(1)} %all_to_all.26.sums1, f32[32,8,128]{2,1,0:T(8,128)S(1)} %all_to_all.27.sums2, f32[64,64,128]{2,1,0:T(8,128)S(1)} %get-tuple-element.88.field, ...), custom_call_target="tpu_custom_call" | custom-call | bytes 19267584 | tf_op jit(solution)/shard_map/last/pallas_call | solution.py:436
  (59 shorter events, 10.5 us)
Async XLA Ops:
  5.0 18.6 %collective-permute-start = (f32[16,72,128]{2,1,0:T(8,128)}, f32[16,72,128]{2,1,0:T(8,128)S(1)}, u32[]{:S(2)}, u32[]{:S(2)}) collective-permute-start(f32[16,72,128]{2,1,0:T(8,128)} %get-tuple-element.64), channel_id=1, source_target_pairs={{0,8},{8,16},{16,24},{24,0},{1,9},{9,17},{17,25},{25,1},{2,10},{10... | collective-permute-start | bytes 1769480 | tf_op jit(solution)/shard_map/ppermute | solution.py:455
  8.0 15.6 %collective-permute-start.1 = (f32[16,72,128]{2,1,0:T(8,128)}, f32[16,72,128]{2,1,0:T(8,128)S(1)}, u32[]{:S(2)}, u32[]{:S(2)}) collective-permute-start(f32[16,72,128]{2,1,0:T(8,128)} %get-tuple-element.65), channel_id=1, source_target_pairs={{0,1},{1,2},{2,3},{3,4},{4,5},{5,6},{6,7},{8,9},{9,10},{10,11},{11... | collective-permute-start | bytes 1769480 | tf_op jit(solution)/shard_map/ppermute | solution.py:455
  23.6 22.4 %copy-start.4 = (f32[16,72,128]{2,1,0:T(8,128)}, f32[16,72,128]{2,1,0:T(8,128)S(1)}, u32[]{:S(2)}) copy-start(f32[16,72,128]{2,1,0:T(8,128)S(1)} %collective-permute-done.g0) | copy-start | bytes 1769476
  23.6 22.4 %copy-start.5 = (f32[16,72,128]{2,1,0:T(8,128)}, f32[16,72,128]{2,1,0:T(8,128)S(1)}, u32[]{:S(2)}) copy-start(f32[16,72,128]{2,1,0:T(8,128)S(1)} %collective-permute-done.1.g2) | copy-start | bytes 1769476
  28.1 14.1 %collective-permute-start.2 = (f32[16,64,128]{2,1,0:T(8,128)}, f32[16,64,128]{2,1,0:T(8,128)S(1)}, u32[]{:S(2)}, u32[]{:S(2)}) collective-permute-start(f32[16,64,128]{2,1,0:T(8,128)} %get-tuple-element.73), channel_id=1, source_target_pairs={{8,0},{16,8},{24,16},{0,24},{9,1},{17,9},{25,17},{1,25},{10,2},{18... | collective-permute-start | bytes 1572872 | tf_op jit(solution)/shard_map/ppermute | solution.py:460
  29.8 12.3 %collective-permute-start.3 = (f32[16,64,128]{2,1,0:T(8,128)}, f32[16,64,128]{2,1,0:T(8,128)S(1)}, u32[]{:S(2)}, u32[]{:S(2)}) collective-permute-start(f32[16,64,128]{2,1,0:T(8,128)} %get-tuple-element.74), channel_id=1, source_target_pairs={{1,0},{2,1},{3,2},{4,3},{5,4},{6,5},{7,6},{9,8},{10,9},{11,10},{12... | collective-permute-start | bytes 1572872 | tf_op jit(solution)/shard_map/ppermute | solution.py:460
  31.1 14.9 %all-to-all-start = ((f32[32,8,128]{2,1,0:T(8,128)}), f32[32,8,128]{2,1,0:T(8,128)S(1)}, u32[]{:S(2)}, u32[]{:S(2)}) async-start(f32[32,8,128]{2,1,0:T(8,128)} %bitcast.10), calls=%async_computation | async-start | bytes 262144 | tf_op jit(solution)/shard_map/all_to_all | solution.py:450
  42.1 3.9 %copy-start.7 = (f32[16,64,128]{2,1,0:T(8,128)}, f32[16,64,128]{2,1,0:T(8,128)S(1)}, u32[]{:S(2)}) copy-start(f32[16,64,128]{2,1,0:T(8,128)S(1)} %collective-permute-done.2.g1) | copy-start | bytes 1572868
  42.1 3.9 %copy-start.8 = (f32[16,64,128]{2,1,0:T(8,128)}, f32[16,64,128]{2,1,0:T(8,128)S(1)}, u32[]{:S(2)}) copy-start(f32[16,64,128]{2,1,0:T(8,128)S(1)} %collective-permute-done.3.g3) | copy-start | bytes 1572868
  45.9 5.6 %copy-start.6 = (f32[32,8,128]{2,1,0:T(8,128)}, f32[32,8,128]{2,1,0:T(8,128)S(1)}, u32[]{:S(2)}) copy-start(f32[32,8,128]{2,1,0:T(8,128)S(1)} %all-to-all-done) | copy-start | bytes 393220
  46.0 4.2 %copy-start.9 = (f32[4096]{0:T(1024)S(1)}, f32[4096]{0:T(1024)}, u32[]{:S(2)}) copy-start(f32[4096]{0:T(1024)} %param.16) | copy-start | bytes 49156
  46.0 4.9 %copy-start.14 = (s32[16]{0:T(128)S(1)}, s32[16]{0:T(128)}, u32[]{:S(2)}) copy-start(s32[16]{0:T(128)} %get-tuple-element.122.index1.far1) | copy-start | bytes 196
  46.0 4.9 %copy-start.15 = (s32[16]{0:T(128)S(1)}, s32[16]{0:T(128)}, u32[]{:S(2)}) copy-start(s32[16]{0:T(128)} %get-tuple-element.123.index0.far0) | copy-start | bytes 196
  46.0 4.9 %copy-start.16 = (s32[16]{0:T(128)S(1)}, s32[16]{0:T(128)}, u32[]{:S(2)}) copy-start(s32[16]{0:T(128)} %get-tuple-element.120.index1) | copy-start | bytes 196
  46.0 4.9 %copy-start.17 = (s32[16]{0:T(128)S(1)}, s32[16]{0:T(128)}, u32[]{:S(2)}) copy-start(s32[16]{0:T(128)} %get-tuple-element.121.index0) | copy-start | bytes 196
  46.0 53.3 %all-to-all-start.1 = ((f32[32,128,128]{2,1,0:T(8,128)}), f32[32,128,128]{2,1,0:T(8,128)S(1)}, u32[]{:S(2)}, u32[]{:S(2)}) async-start(f32[32,128,128]{2,1,0:T(8,128)} %bitcast.29), calls=%async_computation.1 | async-start | bytes 4194304 | tf_op jit(solution)/shard_map/all_to_all | solution.py:450
  59.7 29.4 %collective-permute-start.4 = (f32[16,128]{1,0:T(8,128)}, f32[16,128]{1,0:T(8,128)S(1)}, u32[]{:S(2)}, u32[]{:S(2)}) collective-permute-start(f32[16,128]{1,0:T(8,128)} %get-tuple-element.76), channel_id=1, source_target_pairs={{0,8},{8,16},{16,24},{24,0},{1,9},{9,17},{17,25},{25,1},{2,10},{10... | collective-permute-start | bytes 24584 | tf_op jit(solution)/shard_map/ppermute | solution.py:455
  61.6 27.5 %collective-permute-start.5 = (f32[16,128]{1,0:T(8,128)}, f32[16,128]{1,0:T(8,128)S(1)}, u32[]{:S(2)}, u32[]{:S(2)}) collective-permute-start(f32[16,128]{1,0:T(8,128)} %get-tuple-element.77), channel_id=1, source_target_pairs={{8,0},{16,8},{24,16},{0,24},{9,1},{17,9},{25,17},{1,25},{10,2},{18... | collective-permute-start | bytes 24584 | tf_op jit(solution)/shard_map/ppermute | solution.py:460
  63.6 25.5 %collective-permute-start.6 = (f32[16,128]{1,0:T(8,128)}, f32[16,128]{1,0:T(8,128)S(1)}, u32[]{:S(2)}, u32[]{:S(2)}) collective-permute-start(f32[16,128]{1,0:T(8,128)} %get-tuple-element.78), channel_id=1, source_target_pairs={{0,1},{1,2},{2,3},{3,4},{4,5},{5,6},{6,7},{8,9},{9,10},{10,11},{11... | collective-permute-start | bytes 24584 | tf_op jit(solution)/shard_map/ppermute | solution.py:455
  65.4 23.8 %collective-permute-start.7 = (f32[16,128]{1,0:T(8,128)}, f32[16,128]{1,0:T(8,128)S(1)}, u32[]{:S(2)}, u32[]{:S(2)}) collective-permute-start(f32[16,128]{1,0:T(8,128)} %get-tuple-element.79), channel_id=1, source_target_pairs={{1,0},{2,1},{3,2},{4,3},{5,4},{6,5},{7,6},{9,8},{10,9},{11,10},{12... | collective-permute-start | bytes 24584 | tf_op jit(solution)/shard_map/ppermute | solution.py:460
  89.7 9.6 %copy-start.1 = (s32[256]{0:T(256)S(1)}, s32[256]{0:T(256)}, u32[]{:S(2)}) copy-start(s32[256]{0:T(256)} %select_reduce_fusion.tags) | copy-start | bytes 3076
  89.7 9.6 %copy-start.3 = (s32[64]{0:T(128)S(1)}, s32[64]{0:T(128)}, u32[]{:S(2)}) copy-start(s32[64]{0:T(128)} %get-tuple-element.117.picked) | copy-start | bytes 772
  99.3 15.4 %copy-start = (f32[4096,128]{1,0:T(8,128)S(1)}, f32[4096,128]{1,0:T(8,128)}, u32[]{:S(2)}) copy-start(f32[4096,128]{1,0:T(8,128)} %param.19) | copy-start | bytes 6291460
  106.3 30.6 %collective-permute-start.8 = (f32[16,64,128]{2,1,0:T(8,128)S(1)}, f32[16,64,128]{2,1,0:T(8,128)S(1)}, u32[]{:S(2)}, u32[]{:S(2)}) collective-permute-start(f32[16,64,128]{2,1,0:T(8,128)S(1)} %get-tuple-element.94), channel_id=1, source_target_pairs={{0,8},{8,16},{16,24},{24,0},{1,9},{9,17},{17,25},{25,1},{2,10},{10... | collective-permute-start | bytes 1572872 | tf_op jit(solution)/shard_map/ppermute | solution.py:455
  112.1 24.8 %collective-permute-start.9 = (f32[16,64,128]{2,1,0:T(8,128)S(1)}, f32[16,64,128]{2,1,0:T(8,128)S(1)}, u32[]{:S(2)}, u32[]{:S(2)}) collective-permute-start(f32[16,64,128]{2,1,0:T(8,128)S(1)} %get-tuple-element.95), channel_id=1, source_target_pairs={{8,0},{16,8},{24,16},{0,24},{9,1},{17,9},{25,17},{1,25},{10,2},{18... | collective-permute-start | bytes 1572872 | tf_op jit(solution)/shard_map/ppermute | solution.py:460
  112.1 24.8 %collective-permute-start.10 = (f32[16,64,128]{2,1,0:T(8,128)S(1)}, f32[16,64,128]{2,1,0:T(8,128)S(1)}, u32[]{:S(2)}, u32[]{:S(2)}) collective-permute-start(f32[16,64,128]{2,1,0:T(8,128)S(1)} %get-tuple-element.96), channel_id=1, source_target_pairs={{0,1},{1,2},{2,3},{3,4},{4,5},{5,6},{6,7},{8,9},{9,10},{10,11},{11... | collective-permute-start | bytes 1572872 | tf_op jit(solution)/shard_map/ppermute | solution.py:455
  113.5 23.5 %collective-permute-start.11 = (f32[16,64,128]{2,1,0:T(8,128)S(1)}, f32[16,64,128]{2,1,0:T(8,128)S(1)}, u32[]{:S(2)}, u32[]{:S(2)}) collective-permute-start(f32[16,64,128]{2,1,0:T(8,128)S(1)} %get-tuple-element.97), channel_id=1, source_target_pairs={{1,0},{2,1},{3,2},{4,3},{5,4},{6,5},{7,6},{9,8},{10,9},{11,10},{12... | collective-permute-start | bytes 1572872 | tf_op jit(solution)/shard_map/ppermute | solution.py:460
  114.8 22.2 %copy-start.2 = (s32[64]{0:T(128)S(1)}, s32[64]{0:T(128)}, u32[]{:S(2)}) copy-start(s32[64]{0:T(128)} %get-tuple-element.116.placed) | copy-start | bytes 772
  138.4 32.0 %collective-permute-start.12 = (f32[16,64,128]{2,1,0:T(8,128)S(1)}, f32[16,64,128]{2,1,0:T(8,128)S(1)}, u32[]{:S(2)}, u32[]{:S(2)}) collective-permute-start(f32[16,64,128]{2,1,0:T(8,128)S(1)} %get-tuple-element.104), channel_id=1, source_target_pairs={{0,8},{8,16},{16,24},{24,0},{1,9},{9,17},{17,25},{25,1},{2,10},{10... | collective-permute-start | bytes 1572872 | tf_op jit(solution)/shard_map/ppermute | solution.py:455
  141.5 28.9 %collective-permute-start.13 = (f32[16,64,128]{2,1,0:T(8,128)S(1)}, f32[16,64,128]{2,1,0:T(8,128)S(1)}, u32[]{:S(2)}, u32[]{:S(2)}) collective-permute-start(f32[16,64,128]{2,1,0:T(8,128)S(1)} %get-tuple-element.105), channel_id=1, source_target_pairs={{8,0},{16,8},{24,16},{0,24},{9,1},{17,9},{25,17},{1,25},{10,2},{18... | collective-permute-start | bytes 1572872 | tf_op jit(solution)/shard_map/ppermute | solution.py:460
  144.6 25.9 %collective-permute-start.14 = (f32[16,64,128]{2,1,0:T(8,128)S(1)}, f32[16,64,128]{2,1,0:T(8,128)S(1)}, u32[]{:S(2)}, u32[]{:S(2)}) collective-permute-start(f32[16,64,128]{2,1,0:T(8,128)S(1)} %get-tuple-element.106), channel_id=1, source_target_pairs={{0,1},{1,2},{2,3},{3,4},{4,5},{5,6},{6,7},{8,9},{9,10},{10,11},{11... | collective-permute-start | bytes 1572872 | tf_op jit(solution)/shard_map/ppermute | solution.py:455
  145.9 24.6 %collective-permute-start.15 = (f32[16,64,128]{2,1,0:T(8,128)S(1)}, f32[16,64,128]{2,1,0:T(8,128)S(1)}, u32[]{:S(2)}, u32[]{:S(2)}) collective-permute-start(f32[16,64,128]{2,1,0:T(8,128)S(1)} %get-tuple-element.107), channel_id=1, source_target_pairs={{1,0},{2,1},{3,2},{4,3},{5,4},{6,5},{7,6},{9,8},{10,9},{11,10},{12... | collective-permute-start | bytes 1572872 | tf_op jit(solution)/shard_map/ppermute | solution.py:460
  (4 other events, 2.4 us)

commit v4 on v3

--- a/solution.py
+++ b/solution.py
@@ -215,7 +215,7 @@
         gains[k] = jnp.broadcast_to(columns[:, k : k + 1], (bn, 128))
 
 
-def edges_kernel(placed, loads, t0, t1, t2, t3, g0, g1, g2, g3, image):
+def edges_kernel(placed, loads, t0, t1, t2, t3, g0, g1, g2, g3, image, u1, u3):
     bn = loads.shape[1]
     count = t0.shape[0]
     image[...] = loads[...]
@@ -223,7 +223,10 @@
         columns = rows[...][:, :bn].T
         for k in range(count):
             patch = placed[which * count + k]
-            image[patch] = image[patch] - jnp.broadcast_to(columns[:, k : k + 1], (bn, 128)) * got[k, pl.ds(0, bn), :]
+            value = jnp.broadcast_to(columns[:, k : k + 1], (bn, 128)) * got[k, pl.ds(0, bn), :]
+            image[patch] = image[patch] - value
+            if which % 2:
+                (u1, u3)[which // 2][k] = value
 
 
 def stacked(value):
@@ -372,21 +375,21 @@
 
 
 def second_step_kernel(
-    sums0, sums1, placed, g0, g1, g2, g3, field, image, second, r1, w1, inverse, base,
-    third, r2_out, w2_out, partial,
+    sums0, sums1, placed, u1, u3, m1, m3, q1, q3, field, image, second, after, r1, w1, inverse, base,
+    r2_out, w2_out, partial,
 ):
     first, then = gathered(sums0), gathered(sums1)
     alpha0 = first[0:1] / first[1:2]
     beta1 = then[0:1] / first[0:1]
     alpha1 = then[0:1] / (then[1:2] + beta1 * (then[2:3] + beta1 * first[1:2]))
-    take_values(placed, (g0, g1, g2, g3), third)
+    both = alpha0 * alpha1
+    count = u1.shape[0]
 
     def one(p, carry):
-        n0, w, r = second[p], w1[p], r1[p]
+        w, r = w1[p], r1[p]
         s1 = w + beta1 * image[p]
-        z1 = (n0 - alpha0 * third[p]) + beta1 * n0
         r2 = r - alpha1 * s1
-        w2 = w - alpha1 * z1
+        w2 = w - alpha1 * ((1.0 + beta1) * second[p]) + both * base[p]
         u2 = inverse[p] * r2
         p1 = inverse[p] * r + beta1 * field[p]
         r2_out[p] = r2
@@ -397,11 +400,27 @@
             carry[2] + folded(u2 * s1 + p1 * w2),
         )
 
-    publish(partial, lax.fori_loop(0, field.shape[0], one, zeros(3)))
+    sums = lax.fori_loop(0, field.shape[0], one, zeros(3), unroll=2)
+    links = zeros(2)
+    for which, (far_u, far_m, far_q) in ((1, (u1, m1, q1)), (3, (u3, m3, q3))):
+
+        def link(k, carry):
+            p = placed[which * count + k]
+            u, m, q = far_u[k], far_m[k], far_q[k]
+            u2 = inverse[p] * r2_out[p]
+            p1 = inverse[p] * r1[p] + beta1 * field[p]
+            far_p1 = (1.0 + beta1) * u - alpha0 * m
+            far_u2 = u - (alpha0 + alpha1 * (1.0 + beta1)) * m + both * q
+            here = after[p]
+            return carry[0] + folded(u2 * q + far_u2 * here), carry[1] + folded(p1 * q + far_p1 * here)
+
+        links = lax.fori_loop(0, count, link, links, unroll=2)
+    publish(partial, (sums[0], sums[1] - both * links[0], sums[2] - both * links[1]))
 
 
 def last_kernel(
-    sums0, sums1, sums2, field, image, inverse, r1, w1, r2, w2, estimate_out, left_out, estimate, left, sems
+    sums0, sums1, sums2, placed, g0, g1, g2, g3, field, image, inverse, r1, w1, r2, w2,
+    estimate_out, left_out, estimate, left, sems,
 ):
     first, then, last = gathered(sums0), gathered(sums1), gathered(sums2)
     alpha0 = first[0:1] / first[1:2]
@@ -410,22 +429,37 @@
     alpha1 = then[0:1] / curve1
     beta2 = last[0:1] / then[0:1]
     alpha2 = last[0:1] / (last[1:2] + beta2 * (last[2:3] + beta2 * curve1))
-
-    def one(p, carry):
-        p1 = inverse[p] * r1[p] + beta1 * field[p]
-        direction = inverse[p] * r2[p] + beta2 * p1
-        estimate[p] = alpha0 * field[p] + alpha1 * p1 + alpha2 * direction
-        left[p] = r2[p] - alpha2 * (w2[p] + beta2 * (w1[p] + beta1 * image[p]))
-        return carry
-
+    part = alpha2 * alpha0 * alpha1
     size = field.shape[0] // STRIPES
     copies = []
+
+    def residual(p, carry):
+        left[p] = r2[p] - alpha2 * (w2[p] + beta2 * (w1[p] + beta1 * image[p]))
+        return carry
+
+    lax.fori_loop(0, field.shape[0], residual, 0, unroll=2)
+    count = g0.shape[0]
+    for which, got in enumerate((g0, g1, g2, g3)):
+
+        def link(k, carry):
+            patch = placed[which * count + k]
+            left[patch] = left[patch] + part * got[k]
+            return carry
+
+        lax.fori_loop(0, count, link, 0, unroll=4)
+
+    def iterate(p, carry):
+        p1 = inverse[p] * r1[p] + beta1 * field[p]
+        estimate[p] = alpha0 * field[p] + alpha1 * p1 + alpha2 * (inverse[p] * r2[p] + beta2 * p1)
+        return carry
+
+    copies.append(pltpu.make_async_copy(left, left_out, sems.at[STRIPES]))
+    copies[-1].start()
     for c in range(STRIPES):
-        lax.fori_loop(c * size, (c + 1) * size, one, 0, unroll=2)
-        part = pl.ds(c * size, size)
-        for i, (src, dst) in enumerate(((estimate, estimate_out), (left, left_out))):
-            copies.append(pltpu.make_async_copy(src.at[part], dst.at[part], sems.at[i, c]))
-            copies[-1].start()
+        lax.fori_loop(c * size, (c + 1) * size, iterate, 0, unroll=2)
+        rows = pl.ds(c * size, size)
+        copies.append(pltpu.make_async_copy(estimate.at[rows], estimate_out.at[rows], sems.at[c]))
+        copies[-1].start()
     for copy in copies:
         copy.wait()
 
@@ -510,7 +544,9 @@
         (pltpu.VMEM((patch_dev + 8, 128), F32), pltpu.VMEM((4 * count, 128), F32)), limit=WIDE,
     )
     rows = exchange(*rows)
-    (start,) = call(edges_kernel, "edges", (placed, loads, *rows, g0, g1, g2, g3), (vec,), limit=WIDE)
+    start, far_u1, far_u3 = call(
+        edges_kernel, "edges", (placed, loads, *rows, g0, g1, g2, g3), (vec, buf, buf), limit=WIDE
+    )
     image, blocks, after, *rest = call(
         assemble_kernel, "assemble",
         (tags, picked, payload, start, field, inverse, gains),
@@ -524,26 +560,30 @@
     base, partial = call(first_local_kernel, "first_local", (blocks, after, image, loads, field), (vec, total))
     sums0 = everywhere(partial)
     base, sums0 = lax.optimization_barrier((base, sums0))
+    m1, m3 = got[1], got[3]
     second, after, *sends = call(
         second_kernel, "second", (picked, placed, inverse, gains, *got, base),
         (vec, vec, buf, buf, buf, buf), alias={8: 0},
     )
-    got = exchange(*sends)
+    s0, s1, s2, s3 = sends
+    q1, q3 = back(s1, "sector", True), back(s3, "axial", False)
     base, r1, w1, partial = call(
         first_step_kernel, "first_step",
         (sums0, blocks, after, loads, field, image, second, inverse), (vec, vec, vec, total),
     )
     sums1 = everywhere(partial)
-    base, sums1 = lax.optimization_barrier((base, sums1))
-    _, r2, w2, partial = call(
+    s0, s2, base, sums1 = lax.optimization_barrier((s0, s2, base, sums1))
+    q0, q2 = onward(s0, "sector", True), onward(s2, "axial", False)
+    r2, w2, partial = call(
         second_step_kernel, "second_step",
-        (sums0, sums1, placed, *got, field, image, second, r1, w1, inverse, base),
-        (vec, vec, vec, total), alias={13: 0},
+        (sums0, sums1, placed, far_u1, far_u3, m1, m3, q1, q3, field, image, second, after, r1, w1, inverse, base),
+        (vec, vec, total),
     )
     sums2 = everywhere(partial)
     estimate, left = call(
-        last_kernel, "last", (sums0, sums1, sums2, field, image, inverse, r1, w1, r2, w2), (vec, vec),
-        (pltpu.VMEM(loads.shape, F32), pltpu.VMEM(loads.shape, F32), pltpu.SemaphoreType.DMA((2, STRIPES))),
+        last_kernel, "last",
+        (sums0, sums1, sums2, placed, q0, q1, q2, q3, field, image, inverse, r1, w1, r2, w2), (vec, vec),
+        (pltpu.VMEM(loads.shape, F32), pltpu.VMEM(loads.shape, F32), pltpu.SemaphoreType.DMA((STRIPES + 1,))),
         out=pl.BlockSpec(memory_space=pl.ANY),
     )
     return estimate.reshape(points, cases), left.reshape(points, cases)

time: 189 us -> 184 us (0.974)
  blocking collectives: 51.9 us -> 43.5 us
    all_to_all x3, blocking collectives: 51.9 us -> 43.5 us  [everywhere(): lax.all_to_all(partial, AXES, split_axis=0, concat_axis=0, tiled=True)]
    ppermute x8, starting transfers between devices: 11.9 us -> 15.2 us  [back(): lax.ppermute(value, axis, [((i + 1) % n, i) for i in range(n) if wrap or...]
  transfers between devices with their start and end apart: 18 -> 18, of which waited for: 5 -> 5; matrix products, arithmetic and copies ran while one was open for 1% -> 1% of each run, Pallas kernels for 15% -> 17%
where the time goes in v4:
time: 184 us; the launch traced here: 183 us
  Pallas kernels  49.8 us (27%)
  blocking collectives  43.5 us (24%)
  starting transfers between devices  41.4 us (22%)
  waiting for transfers between devices  41 us (22%)
  other arithmetic  2.7 us (1%)
  local copies, waits for them, and re-layouts  2.68 us (1%)
    all_to_all x3, blocking collectives, everywhere(): lax.all_to_all(partial, AXES, split_axis=0, concat_axis=0, tiled=True)  43.5 us
    pallas_call x8, Pallas kernels, call(): pl.pallas_call(kernel, in_specs=[SMEM if ints(a) else HBM if i in far els...  33 us
    ppermute x8, waiting for transfers between devices, onward(): lax.ppermute(value, axis, [(i, (i + 1) % n) for i in range(n) if wrap or...  25.3 us
    ppermute x8, starting transfers between devices, onward(): lax.ppermute(value, axis, [(i, (i + 1) % n) for i in range(n) if wrap or...  18.1 us
    ppermute x8, starting transfers between devices, back(): lax.ppermute(value, axis, [((i + 1) % n, i) for i in range(n) if wrap or...  15.2 us
    pallas_call x1, Pallas kernels, pack_call(): pl.pallas_call(functools.partial(pack_kernel, slots_each), grid=(elems //...  10.7 us
    all_to_all x2, waiting for transfers between devices, everywhere(): lax.all_to_all(partial, AXES, split_axis=0, concat_axis=0, tiled=True)  8.78 us
    all_to_all x2, starting transfers between devices, everywhere(): lax.all_to_all(partial, AXES, split_axis=0, concat_axis=0, tiled=True)  8.15 us
  transfers between devices with their start and end apart: 18, of which 5 were waited for; matrix products, arithmetic and copies ran while one was open for 1% of the time, Pallas kernels for 17%

profile of v4, /device:TPU:0, one launch (start us, length us, event | category | flops | bytes accessed | tf_op | source)
XLA Modules:
  0.0 182.8 jit_solution(17104587826597664194)
XLA Ops:
  0.6 1.3 slice_bitcast_fusion
  2.0 2.9 %gather.2 = (f32[16,72,128]{2,1,0:T(8,128)}, f32[16,72,128]{2,1,0:T(8,128)}) custom-call(s32[16]{0:T(128)} %get-tuple-element.131.index0, s32[16]{0:T(128)} %get-tuple-element.130.index1, s32[16]{0:T(128)} %get-tuple-element.129.far0, s32[16]{0:T(128)} %get-tuple-element.128.far1, f32[64,64,128]{2,1,0:T(8,128)} %bitcast.20, f32[2,16,64]{2,1,0:T(8,128)} %conduct.1), custom_call_target="tpu_custom_call" | custom-call | tf_op jit(solution)/shard_map/gather/pallas_call | solution.py:167
  4.9 3.1 %collective-permute-start = (f32[16,72,128]{2,1,0:T(8,128)}, f32[16,72,128]{2,1,0:T(8,128)S(1)}, u32[]{:S(2)}, u32[]{:S(2)}) collective-permute-start(f32[16,72,128]{2,1,0:T(8,128)} %get-tuple-element.69), channel_id=1, source_target_pairs={{0,8},{8,16},{16,24},{24,0},{1,9},{9,17},{17,25},{25,1},{2,10},{10... | collective-permute-start | bytes 1769480 | tf_op jit(solution)/shard_map/ppermute | solution.py:489
  8.0 1.5 collective-permute-start.1
  10.1 10.7 %pack.1 = (f32[4096,128]{1,0:T(8,128)}, f32[256,128]{1,0:T(8,128)}) custom-call(s32[128]{0:T(128)} %bitcast.34, s32[128]{0:T(128)} %patches.1, s32[1]{0:T(128)S(6)} %copy.14.counts, f32[64,64,128]{2,1,0:T(8,128)} %bitcast.28, bf16[128,64,256]{2,1,0:T(8,128)(2,1)} %bitcast.27, s32[64,128]{1,0:T(8,128)} %bitcast.32), custom_call_target="tpu_custom_call" | custom-call | tf_op jit(solution)/shard_map/pack/pallas_call | solution.py:99
  20.8 2.7 %collective-permute-done.g0 = f32[16,72,128]{2,1,0:T(8,128)S(1)} collective-permute-done((f32[16,72,128]{2,1,0:T(8,128)}, f32[16,72,128]{2,1,0:T(8,128)S(1)}, u32[]{:S(2)}, u32[]{:S(2)}) %collective-permute-start) | collective-permute-done | bytes 589856 | tf_op jit(solution)/shard_map/ppermute | solution.py:489
  23.6 1.3 convert_reduce_fusion
  24.9 3.2 %gather.3 = (f32[16,64,128]{2,1,0:T(8,128)}, f32[16,64,128]{2,1,0:T(8,128)}) custom-call(s32[16]{0:T(128)} %get-tuple-element.133.index0.far0, s32[16]{0:T(128)} %get-tuple-element.132.index1.far1, s32[16]{0:T(128)} %get-tuple-element.133.index0.far0, s32[16]{0:T(128)} %get-tuple-element.132.index1.far1, f32[64,64,128]{2,1,0:T(8,128)} %bitcast.21, ...), custom_call_target="tpu_custom_call" | custom-call | tf_op jit(solution)/shard_map/gather/pallas_call | solution.py:167
  28.1 1.7 collective-permute-start.2
  31.2 4.1 %all-to-all-start = ((f32[32,8,128]{2,1,0:T(8,128)}), f32[32,8,128]{2,1,0:T(8,128)S(1)}, u32[]{:S(2)}, u32[]{:S(2)}) async-start(f32[32,8,128]{2,1,0:T(8,128)} %bitcast.10), calls=%async_computation | async-start | bytes 262144 | tf_op jit(solution)/shard_map/all_to_all | solution.py:484
  35.2 6.9 %collective-permute-done.2.g1 = f32[16,64,128]{2,1,0:T(8,128)S(1)} collective-permute-done((f32[16,64,128]{2,1,0:T(8,128)}, f32[16,64,128]{2,1,0:T(8,128)S(1)}, u32[]{:S(2)}, u32[]{:S(2)}) %collective-permute-start.2) | collective-permute-done | bytes 524320 | tf_op jit(solution)/shard_map/ppermute | solution.py:494
  42.2 3.9 %all-to-all-done = f32[32,8,128]{2,1,0:T(8,128)S(1)} async-done(((f32[32,8,128]{2,1,0:T(8,128)}), f32[32,8,128]{2,1,0:T(8,128)S(1)}, u32[]{:S(2)}, u32[]{:S(2)}) %all-to-all-start) | async-done | bytes 131104 | tf_op jit(solution)/shard_map/all_to_all | solution.py:484
  46.1 4.1 %all-to-all-start.1 = ((f32[32,128,128]{2,1,0:T(8,128)}), f32[32,128,128]{2,1,0:T(8,128)S(1)}, u32[]{:S(2)}, u32[]{:S(2)}) async-start(f32[32,128,128]{2,1,0:T(8,128)} %bitcast.29), calls=%async_computation.1 | async-start | bytes 4194304 | tf_op jit(solution)/shard_map/all_to_all | solution.py:484
  52.3 7.6 %diagonal.1 = (f32[64,64,128]{2,1,0:T(8,128)}, f32[64,64,128]{2,1,0:T(8,128)}, f32[64,64,128]{2,1,0:T(8,128)}, f32[16,128]{1,0:T(8,128)}, f32[16,128]{1,0:T(8,12...) custom-call(s32[256]{0:T(256)} %select_reduce_fusion.tags, s32[64]{0:T(128)} %get-tuple-element.127.picked, ...), custom_call_target="tpu_custom_call" | custom-call | bytes 9757952 | tf_op jit(solution)/shard_map/diagonal/pallas_call | solution.py:470
  59.9 1.8 collective-permute-start.4
  61.7 2.0 %collective-permute-start.5 = (f32[16,128]{1,0:T(8,128)}, f32[16,128]{1,0:T(8,128)S(1)}, u32[]{:S(2)}, u32[]{:S(2)}) collective-permute-start(f32[16,128]{1,0:T(8,128)} %get-tuple-element.82), channel_id=1, source_target_pairs={{8,0},{16,8},{24,16},{0,24},{9,1},{17,9},{25,17},{1,25},{10,2},{18... | collective-permute-start | bytes 24584 | tf_op jit(solution)/shard_map/ppermute | solution.py:494
  63.7 1.6 collective-permute-start.6
  66.6 22.5 %collective-permute-done.4.t0 = f32[16,128]{1,0:T(8,128)S(1)} collective-permute-done((f32[16,128]{1,0:T(8,128)}, f32[16,128]{1,0:T(8,128)S(1)}, u32[]{:S(2)}, u32[]{:S(2)}) %collective-permute-start.4) | collective-permute-done | bytes 8224 | tf_op jit(solution)/shard_map/ppermute | solution.py:489
  89.7 4.7 %edges.1 = (f32[64,64,128]{2,1,0:T(8,128)}, f32[16,64,128]{2,1,0:T(8,128)}, f32[16,64,128]{2,1,0:T(8,128)}) custom-call(s32[64]{0:T(128)} %get-tuple-element.126.placed, f32[64,64,128]{2,1,0:T(8,128)} %bitcast.23, f32[16,128]{1,0:T(8,128)} %copy-done.12, f32[16,128]{1,0:T(8,128)} %copy-done.13, f32[16,128]{1,0:T(8,128)} %copy-done.14, f32[16,128]{1,0:T(8,128)} %copy-done.15, ...), custom_call_target="tpu_custom_call" | custom-call | bytes 7504128 | tf_op jit(solution)/shard_map/edges/pallas_call | solution.py:470
  94.4 4.9 %all-to-all-done.1 = f32[32,128,128]{2,1,0:T(8,128)S(1)} async-done(((f32[32,128,128]{2,1,0:T(8,128)}), f32[32,128,128]{2,1,0:T(8,128)S(1)}, u32[]{:S(2)}, u32[]{:S(2)}) %all-to-all-start.1) | async-done | bytes 2097184 | tf_op jit(solution)/shard_map/all_to_all | solution.py:484
  99.4 6.9 %assemble.1 = (f32[64,64,128]{2,1,0:T(8,128)S(1)}, bf16[64,64,192]{2,1,0:T(8,128)(2,1)S(1)}, f32[64,64,128]{2,1,0:T(8,128)S(1)}, f32[16,64,128]{2,1,0:T(8,128)S(...) custom-call(s32[256]{0:T(256)S(1)} %copy-done.4, ...), custom_call_target="tpu_custom_call" | custom-call | bytes 24642816 | tf_op jit(solution)/shard_map/assemble/pallas_call | solution.py:470
  106.3 6.0 %collective-permute-start.8 = (f32[16,64,128]{2,1,0:T(8,128)S(1)}, f32[16,64,128]{2,1,0:T(8,128)S(1)}, u32[]{:S(2)}, u32[]{:S(2)}) collective-permute-start(f32[16,64,128]{2,1,0:T(8,128)S(1)} %get-tuple-element.100), channel_id=1, source_target_pairs={{0,8},{8,16},{16,24},{24,0},{1,9},{9,17},{17,25},{25,1},{2,10},{10... | collective-permute-start | bytes 1572872 | tf_op jit(solution)/shard_map/ppermute | solution.py:489
  115.0 2.3 %first_local.1 = (f32[64,64,128]{2,1,0:T(8,128)S(1)}, f32[32,8,128]{2,1,0:T(8,128)S(1)}) custom-call(bf16[64,64,192]{2,1,0:T(8,128)(2,1)S(1)} %get-tuple-element.91.blocks, f32[64,64,128]{2,1,0:T(8,128)S(1)} %get-tuple-element.92.after, f32[64,64,128]{2,1,0:T(8,128)S(1)} %get-tuple-element.93.image, f32[64,64,128]{2,1,0:T(8,128)S(1)} %bitcast.24, ...), custom_call_target="tpu_custom_call" | custom-call | bytes 12189696 | tf_op jit(solution)/shard_map/first_local/pallas_call | solution.py:470
  117.3 19.6 %all_to_all.25.sums.sums0 = f32[32,8,128]{2,1,0:T(8,128)S(1)} all-to-all(f32[32,8,128]{2,1,0:T(8,128)S(1)} %get-tuple-element.96), channel_id=1, replica_groups=mesh['sector'=4,'axial'=8] {'sector','axial'}, dimensions={0} | all-to-all | bytes 262144 | tf_op jit(solution)/shard_map/all_to_all | solution.py:484
  136.9 1.5 second.1
  138.4 6.3 %collective-permute-start.12 = (f32[16,64,128]{2,1,0:T(8,128)S(1)}, f32[16,64,128]{2,1,0:T(8,128)S(1)}, u32[]{:S(2)}, u32[]{:S(2)}) collective-permute-start(f32[16,64,128]{2,1,0:T(8,128)S(1)} %get-tuple-element.114), channel_id=1, source_target_pairs={{8,0},{16,8},{24,16},{0,24},{9,1},{17,9},{25,17},{1,25},{10,2},{18... | collective-permute-start | bytes 1572872 | tf_op jit(solution)/shard_map/ppermute | solution.py:494
  146.0 2.9 %first_step.1 = (f32[64,64,128]{2,1,0:T(8,128)S(1)}, f32[64,64,128]{2,1,0:T(8,128)S(1)}, f32[64,64,128]{2,1,0:T(8,128)S(1)}, f32[32,8,128]{2,1,0:T(8,128)S(1)}) custom-call(f32[32,8,128]{2,1,0:T(8,128)S(1)} %all_to_all.25.sums.sums0, bf16[64,64,192]{2,1,0:T(8,128)(2,1)S(1)} %get-tuple-element.91.blocks, f32[64,64,128]{2,1,0:T(8,128)S(1)} %get-tuple-element.107.after, ...), custom_call_target="tpu_custom_call" | custom-call | bytes 20709376 | tf_op jit(solution)/shard_map/first_step/pallas_call | solution.py:470
  148.9 10.4 %all_to_all.26.sums1 = f32[32,8,128]{2,1,0:T(8,128)S(1)} all-to-all(f32[32,8,128]{2,1,0:T(8,128)S(1)} %get-tuple-element.110), channel_id=1, replica_groups=mesh['sector'=4,'axial'=8] {'sector','axial'}, dimensions={0} | all-to-all | bytes 262144 | tf_op jit(solution)/shard_map/all_to_all | solution.py:484
  160.4 1.9 %collective-permute-start.15 = (f32[16,64,128]{2,1,0:T(8,128)S(1)}, f32[16,64,128]{2,1,0:T(8,128)S(1)}, u32[]{:S(2)}, u32[]{:S(2)}) collective-permute-start(f32[16,64,128]{2,1,0:T(8,128)S(1)} %get-tuple-element.121), channel_id=1, source_target_pairs={{0,1},{1,2},{2,3},{3,4},{4,5},{5,6},{6,7},{8,9},{9,10},{10,11},{11... | collective-permute-start | bytes 1572872 | tf_op jit(solution)/shard_map/ppermute | solution.py:489
  162.3 3.2 %second_step.1 = (f32[64,64,128]{2,1,0:T(8,128)S(1)}, f32[64,64,128]{2,1,0:T(8,128)S(1)}, f32[32,8,128]{2,1,0:T(8,128)S(1)}) custom-call(f32[32,8,128]{2,1,0:T(8,128)S(1)} %all_to_all.25.sums.sums0, f32[32,8,128]{2,1,0:T(8,128)S(1)} %all_to_all.26.sums1, s32[64]{0:T(128)S(1)} %copy-done.3, f32[16,64,128]{2,1,0:T(8,128)S(1)} %copy-done.1, ...), custom_call_target="tpu_custom_call" | custom-call | bytes 24510720 | tf_op jit(solution)/shard_map/second_step/pallas_call | solution.py:470
  165.5 13.5 %all_to_all.27.sums2 = f32[32,8,128]{2,1,0:T(8,128)S(1)} all-to-all(f32[32,8,128]{2,1,0:T(8,128)S(1)} %get-tuple-element.119), channel_id=1, replica_groups=mesh['sector'=4,'axial'=8] {'sector','axial'}, dimensions={0} | all-to-all | bytes 262144 | tf_op jit(solution)/shard_map/all_to_all | solution.py:484
  179.0 3.8 %last.1 = (f32[64,64,128]{2,1,0:T(8,128)}, f32[64,64,128]{2,1,0:T(8,128)}) custom-call(f32[32,8,128]{2,1,0:T(8,128)S(1)} %all_to_all.25.sums.sums0, f32[32,8,128]{2,1,0:T(8,128)S(1)} %all_to_all.26.sums1, f32[32,8,128]{2,1,0:T(8,128)S(1)} %all_to_all.27.sums2, s32[64]{0:T(128)S(1)} %copy-done.3, f32[16,64,128]{2,1,0:T(8,128)S(1)} %collective-permute-done.14.g0, ...), custom_call_target="tpu_custom_call" | custom-call | bytes 21364992 | tf_op jit(solution)/shard_map/last/pallas_call | solution.py:470
  (63 shorter events, 10.2 us)
Async XLA Ops:
  4.9 18.6 %collective-permute-start = (f32[16,72,128]{2,1,0:T(8,128)}, f32[16,72,128]{2,1,0:T(8,128)S(1)}, u32[]{:S(2)}, u32[]{:S(2)}) collective-permute-start(f32[16,72,128]{2,1,0:T(8,128)} %get-tuple-element.69), channel_id=1, source_target_pairs={{0,8},{8,16},{16,24},{24,0},{1,9},{9,17},{17,25},{25,1},{2,10},{10... | collective-permute-start | bytes 1769480 | tf_op jit(solution)/shard_map/ppermute | solution.py:489
  8.0 15.6 %collective-permute-start.1 = (f32[16,72,128]{2,1,0:T(8,128)}, f32[16,72,128]{2,1,0:T(8,128)S(1)}, u32[]{:S(2)}, u32[]{:S(2)}) collective-permute-start(f32[16,72,128]{2,1,0:T(8,128)} %get-tuple-element.70), channel_id=1, source_target_pairs={{0,1},{1,2},{2,3},{3,4},{4,5},{5,6},{6,7},{8,9},{9,10},{10,11},{11... | collective-permute-start | bytes 1769480 | tf_op jit(solution)/shard_map/ppermute | solution.py:489
  23.6 22.5 %copy-start.6 = (f32[16,72,128]{2,1,0:T(8,128)}, f32[16,72,128]{2,1,0:T(8,128)S(1)}, u32[]{:S(2)}) copy-start(f32[16,72,128]{2,1,0:T(8,128)S(1)} %collective-permute-done.g0) | copy-start | bytes 1769476
  23.6 22.5 %copy-start.7 = (f32[16,72,128]{2,1,0:T(8,128)}, f32[16,72,128]{2,1,0:T(8,128)S(1)}, u32[]{:S(2)}) copy-start(f32[16,72,128]{2,1,0:T(8,128)S(1)} %collective-permute-done.1.g2) | copy-start | bytes 1769476
  28.1 14.0 %collective-permute-start.2 = (f32[16,64,128]{2,1,0:T(8,128)}, f32[16,64,128]{2,1,0:T(8,128)S(1)}, u32[]{:S(2)}, u32[]{:S(2)}) collective-permute-start(f32[16,64,128]{2,1,0:T(8,128)} %get-tuple-element.78), channel_id=1, source_target_pairs={{8,0},{16,8},{24,16},{0,24},{9,1},{17,9},{25,17},{1,25},{10,2},{18... | collective-permute-start | bytes 1572872 | tf_op jit(solution)/shard_map/ppermute | solution.py:494
  29.9 12.3 %collective-permute-start.3 = (f32[16,64,128]{2,1,0:T(8,128)}, f32[16,64,128]{2,1,0:T(8,128)S(1)}, u32[]{:S(2)}, u32[]{:S(2)}) collective-permute-start(f32[16,64,128]{2,1,0:T(8,128)} %get-tuple-element.79), channel_id=1, source_target_pairs={{1,0},{2,1},{3,2},{4,3},{5,4},{6,5},{7,6},{9,8},{10,9},{11,10},{12... | collective-permute-start | bytes 1572872 | tf_op jit(solution)/shard_map/ppermute | solution.py:494
  31.2 14.9 %all-to-all-start = ((f32[32,8,128]{2,1,0:T(8,128)}), f32[32,8,128]{2,1,0:T(8,128)S(1)}, u32[]{:S(2)}, u32[]{:S(2)}) async-start(f32[32,8,128]{2,1,0:T(8,128)} %bitcast.10), calls=%async_computation | async-start | bytes 262144 | tf_op jit(solution)/shard_map/all_to_all | solution.py:484
  46.0 5.5 %copy-start.8 = (f32[32,8,128]{2,1,0:T(8,128)}, f32[32,8,128]{2,1,0:T(8,128)S(1)}, u32[]{:S(2)}) copy-start(f32[32,8,128]{2,1,0:T(8,128)S(1)} %all-to-all-done) | copy-start | bytes 393220
  46.0 4.2 %copy-start.11 = (f32[4096]{0:T(1024)S(1)}, f32[4096]{0:T(1024)}, u32[]{:S(2)}) copy-start(f32[4096]{0:T(1024)} %param.16) | copy-start | bytes 49156
  46.0 4.8 %copy-start.16 = (s32[16]{0:T(128)S(1)}, s32[16]{0:T(128)}, u32[]{:S(2)}) copy-start(s32[16]{0:T(128)} %get-tuple-element.132.index1.far1) | copy-start | bytes 196
  46.0 4.8 %copy-start.17 = (s32[16]{0:T(128)S(1)}, s32[16]{0:T(128)}, u32[]{:S(2)}) copy-start(s32[16]{0:T(128)} %get-tuple-element.133.index0.far0) | copy-start | bytes 196
  46.0 4.8 %copy-start.18 = (s32[16]{0:T(128)S(1)}, s32[16]{0:T(128)}, u32[]{:S(2)}) copy-start(s32[16]{0:T(128)} %get-tuple-element.130.index1) | copy-start | bytes 196
  46.0 4.8 %copy-start.19 = (s32[16]{0:T(128)S(1)}, s32[16]{0:T(128)}, u32[]{:S(2)}) copy-start(s32[16]{0:T(128)} %get-tuple-element.131.index0) | copy-start | bytes 196
  46.1 53.3 %all-to-all-start.1 = ((f32[32,128,128]{2,1,0:T(8,128)}), f32[32,128,128]{2,1,0:T(8,128)S(1)}, u32[]{:S(2)}, u32[]{:S(2)}) async-start(f32[32,128,128]{2,1,0:T(8,128)} %bitcast.29), calls=%async_computation.1 | async-start | bytes 4194304 | tf_op jit(solution)/shard_map/all_to_all | solution.py:484
  59.9 29.2 %collective-permute-start.4 = (f32[16,128]{1,0:T(8,128)}, f32[16,128]{1,0:T(8,128)S(1)}, u32[]{:S(2)}, u32[]{:S(2)}) collective-permute-start(f32[16,128]{1,0:T(8,128)} %get-tuple-element.81), channel_id=1, source_target_pairs={{0,8},{8,16},{16,24},{24,0},{1,9},{9,17},{17,25},{25,1},{2,10},{10... | collective-permute-start | bytes 24584 | tf_op jit(solution)/shard_map/ppermute | solution.py:489
  61.7 27.4 %collective-permute-start.5 = (f32[16,128]{1,0:T(8,128)}, f32[16,128]{1,0:T(8,128)S(1)}, u32[]{:S(2)}, u32[]{:S(2)}) collective-permute-start(f32[16,128]{1,0:T(8,128)} %get-tuple-element.82), channel_id=1, source_target_pairs={{8,0},{16,8},{24,16},{0,24},{9,1},{17,9},{25,17},{1,25},{10,2},{18... | collective-permute-start | bytes 24584 | tf_op jit(solution)/shard_map/ppermute | solution.py:494
  63.7 25.4 %collective-permute-start.6 = (f32[16,128]{1,0:T(8,128)}, f32[16,128]{1,0:T(8,128)S(1)}, u32[]{:S(2)}, u32[]{:S(2)}) collective-permute-start(f32[16,128]{1,0:T(8,128)} %get-tuple-element.83), channel_id=1, source_target_pairs={{0,1},{1,2},{2,3},{3,4},{4,5},{5,6},{6,7},{8,9},{9,10},{10,11},{11... | collective-permute-start | bytes 24584 | tf_op jit(solution)/shard_map/ppermute | solution.py:489
  65.3 23.9 %collective-permute-start.7 = (f32[16,128]{1,0:T(8,128)}, f32[16,128]{1,0:T(8,128)S(1)}, u32[]{:S(2)}, u32[]{:S(2)}) collective-permute-start(f32[16,128]{1,0:T(8,128)} %get-tuple-element.84), channel_id=1, source_target_pairs={{1,0},{2,1},{3,2},{4,3},{5,4},{6,5},{7,6},{9,8},{10,9},{11,10},{12... | collective-permute-start | bytes 24584 | tf_op jit(solution)/shard_map/ppermute | solution.py:494
  89.7 9.6 %copy-start.4 = (s32[256]{0:T(256)S(1)}, s32[256]{0:T(256)}, u32[]{:S(2)}) copy-start(s32[256]{0:T(256)} %select_reduce_fusion.tags) | copy-start | bytes 3076
  89.7 9.6 %copy-start.5 = (s32[64]{0:T(128)S(1)}, s32[64]{0:T(128)}, u32[]{:S(2)}) copy-start(s32[64]{0:T(128)} %get-tuple-element.127.picked) | copy-start | bytes 772
  99.4 15.6 %copy-start = (f32[4096,128]{1,0:T(8,128)S(1)}, f32[4096,128]{1,0:T(8,128)}, u32[]{:S(2)}) copy-start(f32[4096,128]{1,0:T(8,128)} %param.19) | copy-start | bytes 6291460
  106.3 30.6 %collective-permute-start.8 = (f32[16,64,128]{2,1,0:T(8,128)S(1)}, f32[16,64,128]{2,1,0:T(8,128)S(1)}, u32[]{:S(2)}, u32[]{:S(2)}) collective-permute-start(f32[16,64,128]{2,1,0:T(8,128)S(1)} %get-tuple-element.100), channel_id=1, source_target_pairs={{0,8},{8,16},{16,24},{24,0},{1,9},{9,17},{17,25},{25,1},{2,10},{10... | collective-permute-start | bytes 1572872 | tf_op jit(solution)/shard_map/ppermute | solution.py:489
  112.4 24.6 %collective-permute-start.9 = (f32[16,64,128]{2,1,0:T(8,128)S(1)}, f32[16,64,128]{2,1,0:T(8,128)S(1)}, u32[]{:S(2)}, u32[]{:S(2)}) collective-permute-start(f32[16,64,128]{2,1,0:T(8,128)S(1)} %get-tuple-element.101), channel_id=1, source_target_pairs={{8,0},{16,8},{24,16},{0,24},{9,1},{17,9},{25,17},{1,25},{10,2},{18... | collective-permute-start | bytes 1572872 | tf_op jit(solution)/shard_map/ppermute | solution.py:494
  112.4 24.6 %collective-permute-start.10 = (f32[16,64,128]{2,1,0:T(8,128)S(1)}, f32[16,64,128]{2,1,0:T(8,128)S(1)}, u32[]{:S(2)}, u32[]{:S(2)}) collective-permute-start(f32[16,64,128]{2,1,0:T(8,128)S(1)} %get-tuple-element.102), channel_id=1, source_target_pairs={{0,1},{1,2},{2,3},{3,4},{4,5},{5,6},{6,7},{8,9},{9,10},{10,11},{11... | collective-permute-start | bytes 1572872 | tf_op jit(solution)/shard_map/ppermute | solution.py:489
  113.7 23.2 %collective-permute-start.11 = (f32[16,64,128]{2,1,0:T(8,128)S(1)}, f32[16,64,128]{2,1,0:T(8,128)S(1)}, u32[]{:S(2)}, u32[]{:S(2)}) collective-permute-start(f32[16,64,128]{2,1,0:T(8,128)S(1)} %get-tuple-element.103), channel_id=1, source_target_pairs={{1,0},{2,1},{3,2},{4,3},{5,4},{6,5},{7,6},{9,8},{10,9},{11,10},{12... | collective-permute-start | bytes 1572872 | tf_op jit(solution)/shard_map/ppermute | solution.py:494
  115.0 21.9 %copy-start.3 = (s32[64]{0:T(128)S(1)}, s32[64]{0:T(128)}, u32[]{:S(2)}) copy-start(s32[64]{0:T(128)} %get-tuple-element.126.placed) | copy-start | bytes 772
  138.4 23.8 %collective-permute-start.12 = (f32[16,64,128]{2,1,0:T(8,128)S(1)}, f32[16,64,128]{2,1,0:T(8,128)S(1)}, u32[]{:S(2)}, u32[]{:S(2)}) collective-permute-start(f32[16,64,128]{2,1,0:T(8,128)S(1)} %get-tuple-element.114), channel_id=1, source_target_pairs={{8,0},{16,8},{24,16},{0,24},{9,1},{17,9},{25,17},{1,25},{10,2},{18... | collective-permute-start | bytes 1572872 | tf_op jit(solution)/shard_map/ppermute | solution.py:494
  144.7 17.5 %collective-permute-start.13 = (f32[16,64,128]{2,1,0:T(8,128)S(1)}, f32[16,64,128]{2,1,0:T(8,128)S(1)}, u32[]{:S(2)}, u32[]{:S(2)}) collective-permute-start(f32[16,64,128]{2,1,0:T(8,128)S(1)} %get-tuple-element.115), channel_id=1, source_target_pairs={{1,0},{2,1},{3,2},{4,3},{5,4},{6,5},{7,6},{9,8},{10,9},{11,10},{12... | collective-permute-start | bytes 1572872 | tf_op jit(solution)/shard_map/ppermute | solution.py:494
  146.0 16.3 %copy-start.1 = (f32[16,64,128]{2,1,0:T(8,128)S(1)}, f32[16,64,128]{2,1,0:T(8,128)}, u32[]{:S(2)}) copy-start(f32[16,64,128]{2,1,0:T(8,128)} %get-tuple-element.112.u1) | copy-start | bytes 1572868
  146.0 16.3 %copy-start.2 = (f32[16,64,128]{2,1,0:T(8,128)S(1)}, f32[16,64,128]{2,1,0:T(8,128)}, u32[]{:S(2)}) copy-start(f32[16,64,128]{2,1,0:T(8,128)} %get-tuple-element.113.u3) | copy-start | bytes 1572868
  159.4 19.6 %collective-permute-start.14 = (f32[16,64,128]{2,1,0:T(8,128)S(1)}, f32[16,64,128]{2,1,0:T(8,128)S(1)}, u32[]{:S(2)}, u32[]{:S(2)}) collective-permute-start(f32[16,64,128]{2,1,0:T(8,128)S(1)} %get-tuple-element.120), channel_id=1, source_target_pairs={{0,8},{8,16},{16,24},{24,0},{1,9},{9,17},{17,25},{25,1},{2,10},{10... | collective-permute-start | bytes 1572872 | tf_op jit(solution)/shard_map/ppermute | solution.py:489
  160.4 18.6 %collective-permute-start.15 = (f32[16,64,128]{2,1,0:T(8,128)S(1)}, f32[16,64,128]{2,1,0:T(8,128)S(1)}, u32[]{:S(2)}, u32[]{:S(2)}) collective-permute-start(f32[16,64,128]{2,1,0:T(8,128)S(1)} %get-tuple-element.121), channel_id=1, source_target_pairs={{0,1},{1,2},{2,3},{3,4},{4,5},{5,6},{6,7},{8,9},{9,10},{10,11},{11... | collective-permute-start | bytes 1572872 | tf_op jit(solution)/shard_map/ppermute | solution.py:489
  (6 other events, 10.2 us)

commit v5 on v4

--- a/solution.py
+++ b/solution.py
@@ -142,42 +142,64 @@
         lax.fori_loop(0, count, one, 0, unroll=4)
 
 
-def gather_kernel(index0, index1, far0, far1, loads, gains, out0, out1, sems):
+def own_kernel(table, loads, gains, out0, out1, sems):
     bn = loads.shape[1]
     count = out0.shape[0]
     copies = []
-    for which, (index, out) in enumerate(((index0, out0), (index1, out1))):
+    for which, out in enumerate((out0, out1)):
         for k in range(count):
-            copies.append(pltpu.make_async_copy(loads.at[index[k]], out.at[k, pl.ds(0, bn)], sems.at[which]))
+            copies.append(
+                pltpu.make_async_copy(loads.at[table[which, 0, k]], out.at[k, pl.ds(0, bn)], sems.at[which])
+            )
     for copy in copies:
         copy.start()
-    if out0.shape[1] > bn:
-        lane = iota((1, 128), 1)
-        for which, (far, out) in enumerate(((far0, out0), (far1, out1))):
-            rows = jnp.concatenate([gains[which], gains[which]], axis=1)
-            for k in range(count):
-                row = jnp.where(lane < bn, rows[k : k + 1], far[k].astype(F32))
-                out[k, pl.ds(bn, 8), :] = jnp.broadcast_to(row, (8, 128))
+    lane = iota((1, 128), 1)
+    for which, out in enumerate((out0, out1)):
+        rows = jnp.concatenate([gains[which], gains[which]], axis=1)
+        for k in range(count):
+            row = jnp.where(lane < bn, rows[k : k + 1], table[which, 1, k].astype(F32))
+            out[k, pl.ds(bn, 8), :] = jnp.broadcast_to(row, (8, 128))
     for copy in copies:
         copy.wait()
 
 
-def gather_call(index0, index1, far0, far1, loads, gains, extra):
-    out = struct(index0.shape[0], loads.shape[1] + extra, loads.shape[2])
+def far_kernel(index, loads, out, sem):
+    copies = []
+    for k in range(out.shape[0]):
+        at = index[0, 1, k] if len(index.shape) == 3 else index[k]
+        copies.append(pltpu.make_async_copy(loads.at[at], out.at[k], sem))
+    for copy in copies:
+        copy.start()
+    for copy in copies:
+        copy.wait()
+
+
+def own_call(table, loads, gains):
+    out = struct(table.shape[2], loads.shape[1] + 8, loads.shape[2])
     return pl.pallas_call(
-        gather_kernel,
-        in_specs=[SMEM, SMEM, SMEM, SMEM, pl.BlockSpec(memory_space=pl.ANY), VMEM],
+        own_kernel,
+        in_specs=[SMEM, pl.BlockSpec(memory_space=pl.ANY), VMEM],
         out_specs=[VMEM, VMEM],
         out_shape=[out, out],
         scratch_shapes=[pltpu.SemaphoreType.DMA((2,))],
         compiler_params=pltpu.CompilerParams(vmem_limit_bytes=WIDE),
-        name="gather",
-    )(index0, index1, far0, far1, loads, gains)
-
-
-def diagonal_kernel(
-    tags, picked, meta, capacity, conduct, g0, g2, loads, inverse, field, gains, t0, t1, t2, t3, total, gain_rows,
-):
+        name="own",
+    )(table, loads, gains)
+
+
+def far_call(index, loads):
+    return pl.pallas_call(
+        far_kernel,
+        in_specs=[SMEM, pl.BlockSpec(memory_space=pl.ANY)],
+        out_specs=VMEM,
+        out_shape=struct(index.shape[-1], *loads.shape[1:]),
+        scratch_shapes=[pltpu.SemaphoreType.DMA(())],
+        compiler_params=pltpu.CompilerParams(vmem_limit_bytes=WIDE),
+        name="far",
+    )(index, loads)
+
+
+def diagonal_kernel(tags, picked, meta, capacity, conduct, g0, g2, over, gain_rows, t0, t1, t2, t3, total):
     patch_dev, bn = capacity.shape
     count = conduct.shape[1]
     for which, got in enumerate((g0, g2)):
@@ -199,34 +221,31 @@
         return carry
 
     lax.fori_loop(0, gain_rows.shape[0], link, 0, unroll=4)
-    over = 1.0 / total[pl.ds(0, patch_dev), :]
-    total[pl.ds(0, patch_dev), :] = over
-    columns = over[:, :bn].T
-    for p in range(patch_dev):
+    over[...] = 1.0 / total[pl.ds(0, patch_dev), :]
+    for which, rows in enumerate((t0, t1, t2, t3)):
+        for k in range(count):
+            i = which * count + k
+            rows[pl.ds(k, 1), :] = over[pl.ds(picked[i], 1), :] * gain_rows[pl.ds(i, 1), :]
+
+
+def expand_kernel(over, gain_rows, loads, inverse, field, gains):
+    bn = loads.shape[1]
+    columns = over[...][:, :bn].T
+    for p in range(over.shape[0]):
         column = jnp.broadcast_to(columns[:, p : p + 1], (bn, 128))
         inverse[p] = column
         field[p] = column * loads[p]
-    for which, rows in enumerate((t0, t1, t2, t3)):
-        for k in range(count):
-            i = which * count + k
-            rows[pl.ds(k, 1), :] = total[pl.ds(picked[i], 1), :] * gain_rows[pl.ds(i, 1), :]
     columns = gain_rows[...][:, :bn].T
     for k in range(gain_rows.shape[0]):
         gains[k] = jnp.broadcast_to(columns[:, k : k + 1], (bn, 128))
 
 
-def edges_kernel(placed, loads, t0, t1, t2, t3, g0, g1, g2, g3, image, u1, u3):
-    bn = loads.shape[1]
-    count = t0.shape[0]
-    image[...] = loads[...]
-    for which, (rows, got) in enumerate(((t0, g0), (t1, g1), (t2, g2), (t3, g3))):
+def edges_kernel(t0, t1, t2, t3, g0, g1, g2, g3, p0, p1, p2, p3):
+    count, bn, _ = p0.shape
+    for rows, got, product in ((t0, g0, p0), (t1, g1, p1), (t2, g2, p2), (t3, g3, p3)):
         columns = rows[...][:, :bn].T
         for k in range(count):
-            patch = placed[which * count + k]
-            value = jnp.broadcast_to(columns[:, k : k + 1], (bn, 128)) * got[k, pl.ds(0, bn), :]
-            image[patch] = image[patch] - value
-            if which % 2:
-                (u1, u3)[which // 2][k] = value
+            product[k] = jnp.broadcast_to(columns[:, k : k + 1], (bn, 128)) * got[k, pl.ds(0, bn), :]
 
 
 def stacked(value):
@@ -257,14 +276,15 @@
 
 
 def assemble_kernel(
-    tags, picked, payload, start_in, field_in, inverse_in, gains_in,
-    image, blocks, after, s0, s1, s2, s3, field, inverse, gains, packed, sems,
+    tags, picked, placed, payload, loads_in, field_in, inverse_in, gains_in, p0_in, p1_in, p2_in, p3_in,
+    image, blocks, after, s0, s1, s2, s3, field, inverse, gains, packed, p0, p1, p2, p3, sems,
 ):
     patch_dev, bn, _ = image.shape
     half, quarter = bn // 2, bn // 4
     banks = packed.shape[0]
     slots = tags.shape[0]
-    pairs = ((start_in, image), (field_in, field), (inverse_in, inverse), (gains_in, gains))
+    products = ((p0_in, p0), (p1_in, p1), (p2_in, p2), (p3_in, p3))
+    pairs = ((loads_in, image), (field_in, field), *products, (inverse_in, inverse), (gains_in, gains))
     fetches = [pltpu.make_async_copy(src, dst, sems.at[i]) for i, (src, dst) in enumerate(pairs)]
     for copy in fetches:
         copy.start()
@@ -311,6 +331,7 @@
     lax.fori_loop(0, patch_dev // GROUP, build, 0)
     for copy in fetches[2:]:
         copy.wait()
+    take_values(placed, (p0, p1, p2, p3), image)
 
     def finish(p, carry):
         after[p] = inverse[p] * image[p]
@@ -515,45 +536,53 @@
     total = struct(devices, 8, cases)
 
     table = links.transpose(0, 2, 1)
-    own_sector, own_axial = table[0, 0], table[1, 0]
-    s0, s2 = gather_call(own_sector, own_axial, table[0, 1], table[1, 1], loads, conduct, 8)
-    owners, s0, s2 = lax.optimization_barrier((owners, s0, s2))
+    s0, s2 = own_call(table, loads, conduct)
+    owners, later, s0, s2 = lax.optimization_barrier((owners, table, s0, s2))
     g0, g2 = onward(s0, "sector", True), onward(s2, "axial", False)
+    behind = onward(later, "sector", True)
     payload, meta = pack_call(
         devices, owners.reshape(elems), patch_ids, counts,
         kbb.transpose(1, 2, 0), interior.transpose(0, 2, 1), node_lists.T,
     )
     slots = meta.shape[0]
-    payload, meta, g0, g2 = lax.optimization_barrier((payload, meta, g0, g2))
-    far_sector, far_axial = g0[:, bn, bn].astype(jnp.int32), g2[:, bn, bn].astype(jnp.int32)
-    s1, s3 = gather_call(far_sector, far_axial, far_sector, far_axial, loads, conduct, 0)
-    meta, s1, s3 = lax.optimization_barrier((meta, s1, s3))
-    g1, g3 = back(s1, "sector", True), back(s3, "axial", False)
+    payload, meta, behind = lax.optimization_barrier((payload, meta, behind))
+    s1 = far_call(behind, loads)
+    meta, s1 = lax.optimization_barrier((meta, s1))
+    g1 = back(s1, "sector", True)
+    payload, g0, g2 = lax.optimization_barrier((payload, g0, g2))
+    far_axial = g2[:, bn, bn].astype(jnp.int32)
+    s3 = far_call(far_axial, loads)
     meta = everywhere(meta.reshape(devices, slots // devices, 128)).reshape(slots, 128)
-    payload, g1, g3 = lax.optimization_barrier((payload, g1, g3))
+    payload, g1, s3 = lax.optimization_barrier((payload, g1, s3))
+    g3 = back(s3, "axial", False)
     payload = everywhere(payload.reshape(devices, -1, 128)).reshape(slots * bn // 4, 128)
+    own_sector, own_axial, far_sector = later[0, 0], later[1, 0], behind[0, 1]
     picked = jnp.concatenate([own_sector, far_sector, own_axial, far_axial])
     placed = jnp.concatenate([far_sector, own_sector, far_axial, own_axial])
     tags = meta[:, bn].astype(jnp.int32)
     tags = jnp.where(tags > 0, tags - 1, patch_dev)
     row = struct(count, 128)
-    inverse, field, gains, *rows = call(
+    table_out = struct(patch_dev, 128)
+    over, gain_rows, *rows = call(
         diagonal_kernel, "diagonal",
-        (tags, picked, meta, capacity.reshape(patch_dev, bn), conduct, g0, g2, loads),
-        (vec, vec, struct(4 * count, bn, cases), row, row, row, row),
-        (pltpu.VMEM((patch_dev + 8, 128), F32), pltpu.VMEM((4 * count, 128), F32)), limit=WIDE,
+        (tags, picked, meta, capacity.reshape(patch_dev, bn), conduct, g0, g2),
+        (table_out, struct(4 * count, 128), row, row, row, row),
+        (pltpu.VMEM((patch_dev + 8, 128), F32),), limit=WIDE,
     )
     rows = exchange(*rows)
-    start, far_u1, far_u3 = call(
-        edges_kernel, "edges", (placed, loads, *rows, g0, g1, g2, g3), (vec, buf, buf), limit=WIDE
-    )
+    inverse, field, gains = call(
+        expand_kernel, "expand", (over, gain_rows, loads), (vec, vec, struct(4 * count, bn, cases)), limit=WIDE
+    )
+    edges = call(edges_kernel, "edges", (*rows, g0, g1, g2, g3), (buf, buf, buf, buf), limit=WIDE)
+    far_u1, far_u3 = edges[1], edges[3]
     image, blocks, after, *rest = call(
         assemble_kernel, "assemble",
-        (tags, picked, payload, start, field, inverse, gains),
+        (tags, picked, placed, payload, loads, field, inverse, gains, *edges),
         (vec, struct(patch_dev, bn, 3 * bn, dtype=BF16), vec, buf, buf, buf, buf,
          vec, vec, struct(4 * count, bn, cases)),
-        (pltpu.VMEM((4, patch_dev + 1, bn // 4, 128), F32), pltpu.SemaphoreType.DMA((4,))),
-        far=(3, 4, 5, 6),
+        (pltpu.VMEM((4, patch_dev + 1, bn // 4, 128), F32), *[pltpu.VMEM((count, bn, cases), F32)] * 4,
+         pltpu.SemaphoreType.DMA((8,))),
+        far=(4, 5, 6, 7, 8, 9, 10, 11),
     )
     *sends, field, inverse, gains = rest
     got = exchange(*sends)
@@ -580,6 +609,7 @@
         (vec, vec, total),
     )
     sums2 = everywhere(partial)
+    r2, w2, sums2 = lax.optimization_barrier((r2, w2, sums2))
     estimate, left = call(
         last_kernel, "last",
         (sums0, sums1, sums2, placed, q0, q1, q2, q3, field, image, inverse, r1, w1, r2, w2), (vec, vec),

time: 184 us -> 182 us (0.989)
  waiting for transfers between devices: 41 us -> 34.8 us
  Pallas kernels: 49.8 us -> 52.5 us
    ppermute x8 -> x9, waiting for transfers between devices: 25.3 us -> 19 us  [onward(): lax.ppermute(value, axis, [(i, (i + 1) % n) for i in range(n) if wrap or...]
    ppermute x8 -> x9, starting transfers between devices: 18.1 us -> 20.5 us  [onward(): lax.ppermute(value, axis, [(i, (i + 1) % n) for i in range(n) if wrap or...]
    pallas_call x2 -> x3, Pallas kernels: 6.16 us -> 8.26 us  [the longest x2 5.3 us: far_call(): pl.pallas_call(far_kernel, in_specs=[SMEM, pl.BlockSpec(memory_space=pl.A...]
    pallas_call x8 -> x9, Pallas kernels: 33 us -> 33.5 us  [call(): pl.pallas_call(kernel, in_specs=[SMEM if ints(a) else HBM if i in far els...]
  transfers between devices with their start and end apart: 18 -> 19, of which waited for: 5 -> 5; matrix products, arithmetic and copies ran while one was open for 1% -> 2% of each run, Pallas kernels for 17% -> 20%
where the time goes in v5:
time: 182 us; the launch traced here: 181 us
  Pallas kernels  52.5 us (29%)
  blocking collectives  43.9 us (24%)
  starting transfers between devices  42.9 us (24%)
  waiting for transfers between devices  34.8 us (19%)
  local copies, waits for them, and re-layouts  3.4 us (2%)
  other arithmetic  2.37 us (1%)
    all_to_all x3, blocking collectives, everywhere(): lax.all_to_all(partial, AXES, split_axis=0, concat_axis=0, tiled=True)  43.9 us
    pallas_call x9, Pallas kernels, call(): pl.pallas_call(kernel, in_specs=[SMEM if ints(a) else HBM if i in far els...  33.5 us
    ppermute x9, starting transfers between devices, onward(): lax.ppermute(value, axis, [(i, (i + 1) % n) for i in range(n) if wrap or...  20.5 us
    ppermute x9, waiting for transfers between devices, onward(): lax.ppermute(value, axis, [(i, (i + 1) % n) for i in range(n) if wrap or...  19 us
    ppermute x8, starting transfers between devices, back(): lax.ppermute(value, axis, [((i + 1) % n, i) for i in range(n) if wrap or...  15 us
    pallas_call x1, Pallas kernels, pack_call(): pl.pallas_call(functools.partial(pack_kernel, slots_each), grid=(elems //...  10.7 us
    all_to_all x2, waiting for transfers between devices, everywhere(): lax.all_to_all(partial, AXES, split_axis=0, concat_axis=0, tiled=True)  8.9 us
    all_to_all x2, starting transfers between devices, everywhere(): lax.all_to_all(partial, AXES, split_axis=0, concat_axis=0, tiled=True)  7.37 us
  transfers between devices with their start and end apart: 19, of which 5 were waited for; matrix products, arithmetic and copies ran while one was open for 2% of the time, Pallas kernels for 20%

profile of v5, /device:TPU:0, one launch (start us, length us, event | category | flops | bytes accessed | tf_op | source)
XLA Modules:
  0.0 181.4 jit_solution(13762659372450686464)
XLA Ops:
  0.6 3.0 %own.1 = (f32[16,72,128]{2,1,0:T(8,128)}, f32[16,72,128]{2,1,0:T(8,128)}) custom-call(s32[2,2,16]{2,1,0:T(2,128)} %bitcast.32, f32[64,64,128]{2,1,0:T(8,128)} %bitcast.18, f32[2,16,64]{2,1,0:T(8,128)} %conduct.1), custom_call_target="tpu_custom_call" | custom-call | tf_op jit(solution)/shard_map/own/pallas_call | solution.py:179
  3.6 3.1 %collective-permute-start.1 = (f32[16,72,128]{2,1,0:T(8,128)}, f32[16,72,128]{2,1,0:T(8,128)S(1)}, u32[]{:S(2)}, u32[]{:S(2)}) collective-permute-start(f32[16,72,128]{2,1,0:T(8,128)} %get-tuple-element.80), channel_id=1, source_target_pairs={{0,8},{8,16},{16,24},{24,0},{1,9},{9,17},{17,25},{25,1},{2,10},{10... | collective-permute-start | bytes 1769480 | tf_op jit(solution)/shard_map/ppermute | solution.py:510
  6.7 1.5 collective-permute-start.2
  8.2 1.6 collective-permute-start
  10.5 10.7 %pack.1 = (f32[4096,128]{1,0:T(8,128)}, f32[256,128]{1,0:T(8,128)}) custom-call(s32[128]{0:T(128)} %bitcast.35, s32[128]{0:T(128)} %patches.1, s32[1]{0:T(128)S(6)} %copy.14.counts, f32[64,64,128]{2,1,0:T(8,128)} %bitcast.27, bf16[128,64,256]{2,1,0:T(8,128)(2,1)} %bitcast.26, s32[64,128]{1,0:T(8,128)} %bitcast.31), custom_call_target="tpu_custom_call" | custom-call | tf_op jit(solution)/shard_map/pack/pallas_call | solution.py:99
  22.9 2.5 %far.2 = f32[16,64,128]{2,1,0:T(8,128)} custom-call(s32[2,2,16]{2,1,0:T(2,128)} %copy-done.17, f32[64,64,128]{2,1,0:T(8,128)} %bitcast.19), custom_call_target="tpu_custom_call" | custom-call | tf_op jit(solution)/shard_map/far/pallas_call | solution.py:191
  25.4 1.8 collective-permute-start.3
  27.2 2.9 %all-to-all-start = ((f32[32,8,128]{2,1,0:T(8,128)}), f32[32,8,128]{2,1,0:T(8,128)S(1)}, u32[]{:S(2)}, u32[]{:S(2)}) async-start(f32[32,8,128]{2,1,0:T(8,128)} %bitcast.6), calls=%async_computation | async-start | bytes 262144 | tf_op jit(solution)/shard_map/all_to_all | solution.py:505
  31.0 2.8 %far.3 = f32[16,64,128]{2,1,0:T(8,128)} custom-call(s32[16]{0:T(128)} %convert_reduce_fusion.index, f32[64,64,128]{2,1,0:T(8,128)} %bitcast.20), custom_call_target="tpu_custom_call" | custom-call | tf_op jit(solution)/shard_map/far/pallas_call | solution.py:191
  33.8 6.8 %collective-permute-done.3.g1 = f32[16,64,128]{2,1,0:T(8,128)S(1)} collective-permute-done((f32[16,64,128]{2,1,0:T(8,128)}, f32[16,64,128]{2,1,0:T(8,128)S(1)}, u32[]{:S(2)}, u32[]{:S(2)}) %collective-permute-start.3) | collective-permute-done | bytes 524320 | tf_op jit(solution)/shard_map/ppermute | solution.py:515
  40.7 3.7 %all-to-all-done = f32[32,8,128]{2,1,0:T(8,128)S(1)} async-done(((f32[32,8,128]{2,1,0:T(8,128)}), f32[32,8,128]{2,1,0:T(8,128)S(1)}, u32[]{:S(2)}, u32[]{:S(2)}) %all-to-all-start) | async-done | bytes 131104 | tf_op jit(solution)/shard_map/all_to_all | solution.py:505
  44.4 4.5 %all-to-all-start.1 = ((f32[32,128,128]{2,1,0:T(8,128)}), f32[32,128,128]{2,1,0:T(8,128)S(1)}, u32[]{:S(2)}, u32[]{:S(2)}) async-start(f32[32,128,128]{2,1,0:T(8,128)} %bitcast.28), calls=%async_computation.1 | async-start | bytes 4194304 | tf_op jit(solution)/shard_map/all_to_all | solution.py:505
  53.0 3.8 %diagonal.1 = (f32[64,128]{1,0:T(8,128)}, f32[64,128]{1,0:T(8,128)}, f32[16,128]{1,0:T(8,128)}, f32[16,128]{1,0:T(8,128)}, f32[16,128]{1,0:T(8,128)}, /*index=5*/f32[16,128]{1,0:T(8,128)}) custom-call(s32[256]{0:T(256)} %select_reduce_fusion.tags, s32[64]{0:T(128)} %get-tuple-element.139.picked, f32[256,128]{1,0:T(8,128)} %bitcast.30, ...), custom_call_target="tpu_custom_call" | custom-call | bytes 1434880 | tf_op jit(solution)/shard_map/diagonal/pallas_call | solution.py:491
  56.8 1.8 collective-permute-start.4
  58.6 2.1 %collective-permute-start.5 = (f32[16,128]{1,0:T(8,128)}, f32[16,128]{1,0:T(8,128)S(1)}, u32[]{:S(2)}, u32[]{:S(2)}) collective-permute-start(f32[16,128]{1,0:T(8,128)} %get-tuple-element.93), channel_id=1, source_target_pairs={{8,0},{16,8},{24,16},{0,24},{9,1},{17,9},{25,17},{1,25},{10,2},{18... | collective-permute-start | bytes 24584 | tf_op jit(solution)/shard_map/ppermute | solution.py:515
  60.6 2.5 %collective-permute-start.6 = (f32[16,128]{1,0:T(8,128)}, f32[16,128]{1,0:T(8,128)S(1)}, u32[]{:S(2)}, u32[]{:S(2)}) collective-permute-start(f32[16,128]{1,0:T(8,128)} %get-tuple-element.94), channel_id=1, source_target_pairs={{0,1},{1,2},{2,3},{3,4},{4,5},{5,6},{6,7},{8,9},{9,10},{10,11},{11... | collective-permute-start | bytes 24584 | tf_op jit(solution)/shard_map/ppermute | solution.py:510
  64.5 5.4 %expand.1 = (f32[64,64,128]{2,1,0:T(8,128)}, f32[64,64,128]{2,1,0:T(8,128)}, f32[64,64,128]{2,1,0:T(8,128)}) custom-call(f32[64,128]{1,0:T(8,128)} %get-tuple-element.87.over, f32[64,128]{1,0:T(8,128)} %get-tuple-element.88.gain_rows, f32[64,64,128]{2,1,0:T(8,128)} %bitcast.21), custom_call_target="tpu_custom_call" | custom-call | bytes 8454144 | tf_op jit(solution)/shard_map/expand/pallas_call | solution.py:491
  69.9 17.9 %collective-permute-done.4.t0 = f32[16,128]{1,0:T(8,128)S(1)} collective-permute-done((f32[16,128]{1,0:T(8,128)}, f32[16,128]{1,0:T(8,128)S(1)}, u32[]{:S(2)}, u32[]{:S(2)}) %collective-permute-start.4) | collective-permute-done | bytes 8224 | tf_op jit(solution)/shard_map/ppermute | solution.py:510
  89.3 3.6 %edges.1 = (f32[16,64,128]{2,1,0:T(8,128)}, f32[16,64,128]{2,1,0:T(8,128)}, f32[16,64,128]{2,1,0:T(8,128)}, f32[16,64,128]{2,1,0:T(8,128)}) custom-call(f32[16,128]{1,0:T(8,128)} %copy-done.11, f32[16,128]{1,0:T(8,128)} %copy-done.12, f32[16,128]{1,0:T(8,128)} %copy-done.13, f32[16,128]{1,0:T(8,128)} %copy-done.14, f32[16,72,128]{2,1,0:T(8,128)} %copy-done.6, ...), custom_call_target="tpu_custom_call" | custom-call | bytes 4358144 | tf_op jit(solution)/shard_map/edges/pallas_call | solution.py:491
  92.9 5.2 %all-to-all-done.1 = f32[32,128,128]{2,1,0:T(8,128)S(1)} async-done(((f32[32,128,128]{2,1,0:T(8,128)}), f32[32,128,128]{2,1,0:T(8,128)S(1)}, u32[]{:S(2)}, u32[]{:S(2)}) %all-to-all-start.1) | async-done | bytes 2097184 | tf_op jit(solution)/shard_map/all_to_all | solution.py:505
  98.1 7.3 %assemble.1 = (f32[64,64,128]{2,1,0:T(8,128)S(1)}, bf16[64,64,192]{2,1,0:T(8,128)(2,1)S(1)}, f32[64,64,128]{2,1,0:T(8,128)S(1)}, f32[16,64,128]{2,1,0:T(8,128)S(...) custom-call(s32[256]{0:T(256)S(1)} %copy-done.3, ...), custom_call_target="tpu_custom_call" | custom-call | bytes 26740224 | tf_op jit(solution)/shard_map/assemble/pallas_call | solution.py:491
  105.4 5.7 %collective-permute-start.9 = (f32[16,64,128]{2,1,0:T(8,128)S(1)}, f32[16,64,128]{2,1,0:T(8,128)S(1)}, u32[]{:S(2)}, u32[]{:S(2)}) collective-permute-start(f32[16,64,128]{2,1,0:T(8,128)S(1)} %get-tuple-element.111), channel_id=1, source_target_pairs={{0,8},{8,16},{16,24},{24,0},{1,9},{9,17},{17,25},{25,1},{2,10},{10... | collective-permute-start | bytes 1572872 | tf_op jit(solution)/shard_map/ppermute | solution.py:510
  113.8 2.2 %first_local.1 = (f32[64,64,128]{2,1,0:T(8,128)S(1)}, f32[32,8,128]{2,1,0:T(8,128)S(1)}) custom-call(bf16[64,64,192]{2,1,0:T(8,128)(2,1)S(1)} %get-tuple-element.102.blocks, f32[64,64,128]{2,1,0:T(8,128)S(1)} %get-tuple-element.103.after, f32[64,64,128]{2,1,0:T(8,128)S(1)} %get-tuple-element.104.image, f32[64,64,128]{2,1,0:T(8,128)S(1)} %bitcast.23, ...), custom_call_target="tpu_custom_call" | custom-call | bytes 12189696 | tf_op jit(solution)/shard_map/first_local/pallas_call | solution.py:491
  116.0 20.0 %all_to_all.25.sums.sums0 = f32[32,8,128]{2,1,0:T(8,128)S(1)} all-to-all(f32[32,8,128]{2,1,0:T(8,128)S(1)} %get-tuple-element.107), channel_id=1, replica_groups=mesh['sector'=4,'axial'=8] {'sector','axial'}, dimensions={0} | all-to-all | bytes 262144 | tf_op jit(solution)/shard_map/all_to_all | solution.py:505
  136.0 1.5 second.1
  137.5 6.0 %collective-permute-start.13 = (f32[16,64,128]{2,1,0:T(8,128)S(1)}, f32[16,64,128]{2,1,0:T(8,128)S(1)}, u32[]{:S(2)}, u32[]{:S(2)}) collective-permute-start(f32[16,64,128]{2,1,0:T(8,128)S(1)} %get-tuple-element.123), channel_id=1, source_target_pairs={{8,0},{16,8},{24,16},{0,24},{9,1},{17,9},{25,17},{1,25},{10,2},{18... | collective-permute-start | bytes 1572872 | tf_op jit(solution)/shard_map/ppermute | solution.py:515
  144.8 2.8 %first_step.1 = (f32[64,64,128]{2,1,0:T(8,128)S(1)}, f32[64,64,128]{2,1,0:T(8,128)S(1)}, f32[64,64,128]{2,1,0:T(8,128)S(1)}, f32[32,8,128]{2,1,0:T(8,128)S(1)}) custom-call(f32[32,8,128]{2,1,0:T(8,128)S(1)} %all_to_all.25.sums.sums0, bf16[64,64,192]{2,1,0:T(8,128)(2,1)S(1)} %get-tuple-element.102.blocks, f32[64,64,128]{2,1,0:T(8,128)S(1)} %get-tuple-element.118.after, ...), custom_call_target="tpu_custom_call" | custom-call | bytes 20709376 | tf_op jit(solution)/shard_map/first_step/pallas_call | solution.py:491
  147.6 10.4 %all_to_all.26.sums1 = f32[32,8,128]{2,1,0:T(8,128)S(1)} all-to-all(f32[32,8,128]{2,1,0:T(8,128)S(1)} %get-tuple-element.121), channel_id=1, replica_groups=mesh['sector'=4,'axial'=8] {'sector','axial'}, dimensions={0} | all-to-all | bytes 262144 | tf_op jit(solution)/shard_map/all_to_all | solution.py:505
  159.2 1.9 %collective-permute-start.16 = (f32[16,64,128]{2,1,0:T(8,128)S(1)}, f32[16,64,128]{2,1,0:T(8,128)S(1)}, u32[]{:S(2)}, u32[]{:S(2)}) collective-permute-start(f32[16,64,128]{2,1,0:T(8,128)S(1)} %get-tuple-element.133), channel_id=1, source_target_pairs={{0,1},{1,2},{2,3},{3,4},{4,5},{5,6},{6,7},{8,9},{9,10},{10,11},{11... | collective-permute-start | bytes 1572872 | tf_op jit(solution)/shard_map/ppermute | solution.py:510
  161.1 3.2 %second_step.1 = (f32[64,64,128]{2,1,0:T(8,128)S(1)}, f32[64,64,128]{2,1,0:T(8,128)S(1)}, f32[32,8,128]{2,1,0:T(8,128)S(1)}) custom-call(f32[32,8,128]{2,1,0:T(8,128)S(1)} %all_to_all.25.sums.sums0, f32[32,8,128]{2,1,0:T(8,128)S(1)} %all_to_all.26.sums1, s32[64]{0:T(128)S(1)} %get-tuple-element.138.placed, f32[16,64,128]{2,1,0:T(8,128)S(1)} %copy-done.1, ...), custom_call_target="tpu_custom_call" | custom-call | bytes 24510720 | tf_op jit(solution)/shard_map/second_step/pallas_call | solution.py:491
  164.3 13.5 %all_to_all.27.sums2 = f32[32,8,128]{2,1,0:T(8,128)S(1)} all-to-all(f32[32,8,128]{2,1,0:T(8,128)S(1)} %get-tuple-element.130), channel_id=1, replica_groups=mesh['sector'=4,'axial'=8] {'sector','axial'}, dimensions={0} | all-to-all | bytes 262144 | tf_op jit(solution)/shard_map/all_to_all | solution.py:505
  177.8 3.6 %last.1 = (f32[64,64,128]{2,1,0:T(8,128)}, f32[64,64,128]{2,1,0:T(8,128)}) custom-call(f32[32,8,128]{2,1,0:T(8,128)S(1)} %all_to_all.25.sums.sums0, f32[32,8,128]{2,1,0:T(8,128)S(1)} %all_to_all.26.sums1, f32[32,8,128]{2,1,0:T(8,128)S(1)} %all_to_all.27.sums2, s32[64]{0:T(128)S(1)} %get-tuple-element.138.placed, ...), custom_call_target="tpu_custom_call" | custom-call | bytes 21364992 | tf_op jit(solution)/shard_map/last/pallas_call | solution.py:491
  (64 shorter events, 14.5 us)
Async XLA Ops:
  0.6 7.6 %copy-start.15 = (s32[2,16,2]{1,2,0:T(2,128)S(1)}, s32[2,16,2]{1,2,0:T(2,128)}, u32[]{:S(2)}) copy-start(s32[2,16,2]{1,2,0:T(2,128)} %param.17) | copy-start | bytes 772
  3.6 26.4 %collective-permute-start.1 = (f32[16,72,128]{2,1,0:T(8,128)}, f32[16,72,128]{2,1,0:T(8,128)S(1)}, u32[]{:S(2)}, u32[]{:S(2)}) collective-permute-start(f32[16,72,128]{2,1,0:T(8,128)} %get-tuple-element.80), channel_id=1, source_target_pairs={{0,8},{8,16},{16,24},{24,0},{1,9},{9,17},{17,25},{25,1},{2,10},{10... | collective-permute-start | bytes 1769480 | tf_op jit(solution)/shard_map/ppermute | solution.py:510
  6.7 23.4 %collective-permute-start.2 = (f32[16,72,128]{2,1,0:T(8,128)}, f32[16,72,128]{2,1,0:T(8,128)S(1)}, u32[]{:S(2)}, u32[]{:S(2)}) collective-permute-start(f32[16,72,128]{2,1,0:T(8,128)} %get-tuple-element.81), channel_id=1, source_target_pairs={{0,1},{1,2},{2,3},{3,4},{4,5},{5,6},{6,7},{8,9},{9,10},{10,11},{11... | collective-permute-start | bytes 1769480 | tf_op jit(solution)/shard_map/ppermute | solution.py:510
  8.2 14.0 %collective-permute-start = (s32[2,2,16]{2,1,0:T(2,128)S(1)}, s32[2,2,16]{2,1,0:T(2,128)S(1)}, u32[]{:S(2)}, u32[]{:S(2)}) collective-permute-start(s32[2,2,16]{2,1,0:T(2,128)S(1)} %bitcast.33), channel_id=1, source_target_pairs={{0,8},{8,16},{16,24},{24,0},{1,9},{9,17},{17,25},{25,1},{2,10},{10... | collective-permute-start | bytes 776 | tf_op jit(solution)/shard_map/ppermute | solution.py:510
  25.4 15.3 %collective-permute-start.3 = (f32[16,64,128]{2,1,0:T(8,128)}, f32[16,64,128]{2,1,0:T(8,128)S(1)}, u32[]{:S(2)}, u32[]{:S(2)}) collective-permute-start(f32[16,64,128]{2,1,0:T(8,128)} %far.2), channel_id=1, source_target_pairs={{8,0},{16,8},{24,16},{0,24},{9,1},{17,9},{25,17},{1,25},{10,2},{18... | collective-permute-start | bytes 1572872 | tf_op jit(solution)/shard_map/ppermute | solution.py:515
  27.2 17.2 %all-to-all-start = ((f32[32,8,128]{2,1,0:T(8,128)}), f32[32,8,128]{2,1,0:T(8,128)S(1)}, u32[]{:S(2)}, u32[]{:S(2)}) async-start(f32[32,8,128]{2,1,0:T(8,128)} %bitcast.6), calls=%async_computation | async-start | bytes 262144 | tf_op jit(solution)/shard_map/all_to_all | solution.py:505
  30.1 14.3 %copy-start.6 = (f32[16,72,128]{2,1,0:T(8,128)}, f32[16,72,128]{2,1,0:T(8,128)S(1)}, u32[]{:S(2)}) copy-start(f32[16,72,128]{2,1,0:T(8,128)S(1)} %collective-permute-done.1.g0) | copy-start | bytes 1769476
  30.1 14.3 %copy-start.5 = (f32[16,72,128]{2,1,0:T(8,128)}, f32[16,72,128]{2,1,0:T(8,128)S(1)}, u32[]{:S(2)}) copy-start(f32[16,72,128]{2,1,0:T(8,128)S(1)} %collective-permute-done.2.g2) | copy-start | bytes 1769476
  40.7 3.7 %copy-start.8 = (f32[16,64,128]{2,1,0:T(8,128)}, f32[16,64,128]{2,1,0:T(8,128)S(1)}, u32[]{:S(2)}) copy-start(f32[16,64,128]{2,1,0:T(8,128)S(1)} %collective-permute-done.3.g1) | copy-start | bytes 1572868
  44.4 7.2 %copy-start.7 = (f32[32,8,128]{2,1,0:T(8,128)}, f32[32,8,128]{2,1,0:T(8,128)S(1)}, u32[]{:S(2)}) copy-start(f32[32,8,128]{2,1,0:T(8,128)S(1)} %all-to-all-done) | copy-start | bytes 393220
  44.4 5.8 %copy-start.10 = (f32[4096]{0:T(1024)S(1)}, f32[4096]{0:T(1024)}, u32[]{:S(2)}) copy-start(f32[4096]{0:T(1024)} %param.16) | copy-start | bytes 49156
  44.4 8.0 %copy-start.16 = (s32[16]{0:T(128)S(1)}, s32[16]{0:T(128)}, u32[]{:S(2)}) copy-start(s32[16]{0:T(128)} %convert_reduce_fusion.index) | copy-start | bytes 196
  44.4 53.7 %all-to-all-start.1 = ((f32[32,128,128]{2,1,0:T(8,128)}), f32[32,128,128]{2,1,0:T(8,128)S(1)}, u32[]{:S(2)}, u32[]{:S(2)}) async-start(f32[32,128,128]{2,1,0:T(8,128)} %bitcast.28), calls=%async_computation.1 | async-start | bytes 4194304 | tf_op jit(solution)/shard_map/all_to_all | solution.py:505
  48.9 39.0 %collective-permute-start.8 = (f32[16,64,128]{2,1,0:T(8,128)}, f32[16,64,128]{2,1,0:T(8,128)S(1)}, u32[]{:S(2)}, u32[]{:S(2)}) collective-permute-start(f32[16,64,128]{2,1,0:T(8,128)} %far.3), channel_id=1, source_target_pairs={{1,0},{2,1},{3,2},{4,3},{5,4},{6,5},{7,6},{9,8},{10,9},{11,10},{12... | collective-permute-start | bytes 1572872 | tf_op jit(solution)/shard_map/ppermute | solution.py:515
  56.8 31.0 %collective-permute-start.4 = (f32[16,128]{1,0:T(8,128)}, f32[16,128]{1,0:T(8,128)S(1)}, u32[]{:S(2)}, u32[]{:S(2)}) collective-permute-start(f32[16,128]{1,0:T(8,128)} %get-tuple-element.92), channel_id=1, source_target_pairs={{0,8},{8,16},{16,24},{24,0},{1,9},{9,17},{17,25},{25,1},{2,10},{10... | collective-permute-start | bytes 24584 | tf_op jit(solution)/shard_map/ppermute | solution.py:510
  58.6 29.2 %collective-permute-start.5 = (f32[16,128]{1,0:T(8,128)}, f32[16,128]{1,0:T(8,128)S(1)}, u32[]{:S(2)}, u32[]{:S(2)}) collective-permute-start(f32[16,128]{1,0:T(8,128)} %get-tuple-element.93), channel_id=1, source_target_pairs={{8,0},{16,8},{24,16},{0,24},{9,1},{17,9},{25,17},{1,25},{10,2},{18... | collective-permute-start | bytes 24584 | tf_op jit(solution)/shard_map/ppermute | solution.py:515
  60.6 27.2 %collective-permute-start.6 = (f32[16,128]{1,0:T(8,128)}, f32[16,128]{1,0:T(8,128)S(1)}, u32[]{:S(2)}, u32[]{:S(2)}) collective-permute-start(f32[16,128]{1,0:T(8,128)} %get-tuple-element.94), channel_id=1, source_target_pairs={{0,1},{1,2},{2,3},{3,4},{4,5},{5,6},{6,7},{8,9},{9,10},{10,11},{11... | collective-permute-start | bytes 24584 | tf_op jit(solution)/shard_map/ppermute | solution.py:510
  63.2 24.7 %collective-permute-start.7 = (f32[16,128]{1,0:T(8,128)}, f32[16,128]{1,0:T(8,128)S(1)}, u32[]{:S(2)}, u32[]{:S(2)}) collective-permute-start(f32[16,128]{1,0:T(8,128)} %get-tuple-element.95), channel_id=1, source_target_pairs={{1,0},{2,1},{3,2},{4,3},{5,4},{6,5},{7,6},{9,8},{10,9},{11,10},{12... | collective-permute-start | bytes 24584 | tf_op jit(solution)/shard_map/ppermute | solution.py:515
  64.5 33.6 %copy-start.3 = (s32[256]{0:T(256)S(1)}, s32[256]{0:T(256)}, u32[]{:S(2)}) copy-start(s32[256]{0:T(256)} %select_reduce_fusion.tags) | copy-start | bytes 3076
  64.5 33.6 %copy-start.4 = (s32[64]{0:T(128)S(1)}, s32[64]{0:T(128)}, u32[]{:S(2)}) copy-start(s32[64]{0:T(128)} %get-tuple-element.139.picked) | copy-start | bytes 772
  88.4 0.9 copy-start.9
  98.1 15.7 %copy-start = (f32[4096,128]{1,0:T(8,128)S(1)}, f32[4096,128]{1,0:T(8,128)}, u32[]{:S(2)}) copy-start(f32[4096,128]{1,0:T(8,128)} %param.19) | copy-start | bytes 6291460
  105.4 30.6 %collective-permute-start.9 = (f32[16,64,128]{2,1,0:T(8,128)S(1)}, f32[16,64,128]{2,1,0:T(8,128)S(1)}, u32[]{:S(2)}, u32[]{:S(2)}) collective-permute-start(f32[16,64,128]{2,1,0:T(8,128)S(1)} %get-tuple-element.111), channel_id=1, source_target_pairs={{0,8},{8,16},{16,24},{24,0},{1,9},{9,17},{17,25},{25,1},{2,10},{10... | collective-permute-start | bytes 1572872 | tf_op jit(solution)/shard_map/ppermute | solution.py:510
  111.2 24.8 %collective-permute-start.10 = (f32[16,64,128]{2,1,0:T(8,128)S(1)}, f32[16,64,128]{2,1,0:T(8,128)S(1)}, u32[]{:S(2)}, u32[]{:S(2)}) collective-permute-start(f32[16,64,128]{2,1,0:T(8,128)S(1)} %get-tuple-element.112), channel_id=1, source_target_pairs={{8,0},{16,8},{24,16},{0,24},{9,1},{17,9},{25,17},{1,25},{10,2},{18... | collective-permute-start | bytes 1572872 | tf_op jit(solution)/shard_map/ppermute | solution.py:515
  111.2 24.8 %collective-permute-start.11 = (f32[16,64,128]{2,1,0:T(8,128)S(1)}, f32[16,64,128]{2,1,0:T(8,128)S(1)}, u32[]{:S(2)}, u32[]{:S(2)}) collective-permute-start(f32[16,64,128]{2,1,0:T(8,128)S(1)} %get-tuple-element.113), channel_id=1, source_target_pairs={{0,1},{1,2},{2,3},{3,4},{4,5},{5,6},{6,7},{8,9},{9,10},{10,11},{11... | collective-permute-start | bytes 1572872 | tf_op jit(solution)/shard_map/ppermute | solution.py:510
  112.5 23.5 %collective-permute-start.12 = (f32[16,64,128]{2,1,0:T(8,128)S(1)}, f32[16,64,128]{2,1,0:T(8,128)S(1)}, u32[]{:S(2)}, u32[]{:S(2)}) collective-permute-start(f32[16,64,128]{2,1,0:T(8,128)S(1)} %get-tuple-element.114), channel_id=1, source_target_pairs={{1,0},{2,1},{3,2},{4,3},{5,4},{6,5},{7,6},{9,8},{10,9},{11,10},{12... | collective-permute-start | bytes 1572872 | tf_op jit(solution)/shard_map/ppermute | solution.py:515
  137.5 23.5 %collective-permute-start.13 = (f32[16,64,128]{2,1,0:T(8,128)S(1)}, f32[16,64,128]{2,1,0:T(8,128)S(1)}, u32[]{:S(2)}, u32[]{:S(2)}) collective-permute-start(f32[16,64,128]{2,1,0:T(8,128)S(1)} %get-tuple-element.123), channel_id=1, source_target_pairs={{8,0},{16,8},{24,16},{0,24},{9,1},{17,9},{25,17},{1,25},{10,2},{18... | collective-permute-start | bytes 1572872 | tf_op jit(solution)/shard_map/ppermute | solution.py:515
  143.5 17.5 %collective-permute-start.14 = (f32[16,64,128]{2,1,0:T(8,128)S(1)}, f32[16,64,128]{2,1,0:T(8,128)S(1)}, u32[]{:S(2)}, u32[]{:S(2)}) collective-permute-start(f32[16,64,128]{2,1,0:T(8,128)S(1)} %get-tuple-element.124), channel_id=1, source_target_pairs={{1,0},{2,1},{3,2},{4,3},{5,4},{6,5},{7,6},{9,8},{10,9},{11,10},{12... | collective-permute-start | bytes 1572872 | tf_op jit(solution)/shard_map/ppermute | solution.py:515
  144.8 16.2 %copy-start.1 = (f32[16,64,128]{2,1,0:T(8,128)S(1)}, f32[16,64,128]{2,1,0:T(8,128)}, u32[]{:S(2)}) copy-start(f32[16,64,128]{2,1,0:T(8,128)} %get-tuple-element.99.p1_in.u1) | copy-start | bytes 1572868
  144.8 16.2 %copy-start.2 = (f32[16,64,128]{2,1,0:T(8,128)S(1)}, f32[16,64,128]{2,1,0:T(8,128)}, u32[]{:S(2)}) copy-start(f32[16,64,128]{2,1,0:T(8,128)} %get-tuple-element.101.p3_in.u3) | copy-start | bytes 1572868
  158.0 19.7 %collective-permute-start.15 = (f32[16,64,128]{2,1,0:T(8,128)S(1)}, f32[16,64,128]{2,1,0:T(8,128)S(1)}, u32[]{:S(2)}, u32[]{:S(2)}) collective-permute-start(f32[16,64,128]{2,1,0:T(8,128)S(1)} %get-tuple-element.132), channel_id=1, source_target_pairs={{0,8},{8,16},{16,24},{24,0},{1,9},{9,17},{17,25},{25,1},{2,10},{10... | collective-permute-start | bytes 1572872 | tf_op jit(solution)/shard_map/ppermute | solution.py:510
  159.2 18.6 %collective-permute-start.16 = (f32[16,64,128]{2,1,0:T(8,128)S(1)}, f32[16,64,128]{2,1,0:T(8,128)S(1)}, u32[]{:S(2)}, u32[]{:S(2)}) collective-permute-start(f32[16,64,128]{2,1,0:T(8,128)S(1)} %get-tuple-element.133), channel_id=1, source_target_pairs={{0,1},{1,2},{2,3},{3,4},{4,5},{5,6},{6,7},{8,9},{9,10},{10,11},{11... | collective-permute-start | bytes 1572872 | tf_op jit(solution)/shard_map/ppermute | solution.py:510
  (5 other events, 3.0 us)

commit v6 on v5

--- a/solution.py
+++ b/solution.py
@@ -262,7 +262,7 @@
 
 def publish(partial, sums):
     rows = [jnp.sum(s, axis=0, keepdims=True) for s in sums]
-    block = jnp.concatenate(rows + [jnp.zeros((8 - len(rows), 128), F32)], axis=0)
+    block = jnp.concatenate(rows + [jnp.zeros((partial.shape[1] - len(rows), 128), F32)], axis=0)
     for d in range(partial.shape[0]):
         partial[d] = block
 
@@ -373,92 +373,103 @@
     send_values(picked, gains, after, (s0, s1, s2, s3))
 
 
-def first_step_kernel(
-    sums, blocks, after, loads, field, image, second, inverse, result, left, left_image, partial
-):
+SUMS = 14
+
+
+def first_step_kernel(sums, blocks, after, loads, field, image, second, inverse, result, left, left_image, totals):
     times_all(blocks, after, second, result)
     first = gathered(sums)
     alpha = first[0:1] / first[1:2]
+    bn = loads.shape[1]
 
     def one(p, carry):
-        r = loads[p] - alpha * image[p]
-        w = image[p] - alpha * second[p]
-        u = inverse[p] * r
-        left[p] = r
-        left_image[p] = w
-        return (
-            carry[0] + folded(r * u),
-            carry[1] + folded(u * w),
-            carry[2] + folded(u * image[p] + field[p] * w),
-        )
-
-    publish(partial, lax.fori_loop(0, loads.shape[0], one, zeros(3), unroll=2))
-
-
-def second_step_kernel(
-    sums0, sums1, placed, u1, u3, m1, m3, q1, q3, field, image, second, after, r1, w1, inverse, base,
-    r2_out, w2_out, partial,
+        carry = list(carry)
+        for i in range(0, bn, 8):
+            rows = pl.ds(i, 8)
+            w0, n0, u0, over = image[p, rows], second[p, rows], field[p, rows], inverse[p, rows]
+            r1 = loads[p, rows] - alpha * w0
+            w1 = w0 - alpha * n0
+            n1 = n0 - alpha * result[p, rows]
+            left[p, rows] = r1
+            left_image[p, rows] = w1
+            u1, m1, m0 = over * r1, over * w1, over * w0
+            terms = (
+                r1 * u1, u1 * w1, u1 * w0, u0 * w1, w1 * m1, w1 * m0, w0 * m0,
+                u1 * n1, u1 * n0, m1 * n1, m1 * n0 + m0 * n1, m0 * n0, u0 * n1, u0 * n0,
+            )
+            carry = [c + t for c, t in zip(carry, terms)]
+        return tuple(carry)
+
+    for i, value in enumerate(lax.fori_loop(0, loads.shape[0], one, zeros(SUMS))):
+        totals[i] = value
+
+
+def links_kernel(
+    sums0, placed, totals, far_u0, far_u2, far_m0, far_m2, far_q0, far_q2, field, image, after, r1, w1, inverse, partial
+):
+    first = gathered(sums0)
+    alpha = first[0:1] / first[1:2]
+    count = far_u0.shape[0]
+    sums = zeros(4)
+    for which, (far_u, far_m, far_q) in ((1, (far_u0, far_m0, far_q0)), (3, (far_u2, far_m2, far_q2))):
+
+        def link(k, carry):
+            p = placed[which * count + k]
+            u, m, q = far_u[k], far_m[k], far_q[k]
+            over, here = inverse[p], after[p]
+            ends = (
+                (field[p], u),
+                (over * image[p], m),
+                (over * r1[p], u - alpha * m),
+                (over * w1[p], m - alpha * q),
+            )
+            return tuple(c + folded(own * q + far * here) for c, (own, far) in zip(carry, ends))
+
+        sums = lax.fori_loop(0, count, link, sums, unroll=2)
+    u0n, m0n, u1n, m1n = (alpha * value for value in sums)
+    added = {7: u1n, 9: m1n, 10: m0n, 12: u0n}
+    publish(partial, [totals[i] + added[i] if i in added else totals[i] for i in range(SUMS)])
+
+
+def last_kernel(
+    sums0, sums1, placed, g0, g1, g2, g3, field, image, inverse, second, base, r1, w1,
+    estimate_out, left_out, estimate, left, sems,
 ):
     first, then = gathered(sums0), gathered(sums1)
     alpha0 = first[0:1] / first[1:2]
-    beta1 = then[0:1] / first[0:1]
-    alpha1 = then[0:1] / (then[1:2] + beta1 * (then[2:3] + beta1 * first[1:2]))
-    both = alpha0 * alpha1
-    count = u1.shape[0]
-
-    def one(p, carry):
-        w, r = w1[p], r1[p]
-        s1 = w + beta1 * image[p]
-        r2 = r - alpha1 * s1
-        w2 = w - alpha1 * ((1.0 + beta1) * second[p]) + both * base[p]
-        u2 = inverse[p] * r2
-        p1 = inverse[p] * r + beta1 * field[p]
-        r2_out[p] = r2
-        w2_out[p] = w2
-        return (
-            carry[0] + folded(r2 * u2),
-            carry[1] + folded(u2 * w2),
-            carry[2] + folded(u2 * s1 + p1 * w2),
-        )
-
-    sums = lax.fori_loop(0, field.shape[0], one, zeros(3), unroll=2)
-    links = zeros(2)
-    for which, (far_u, far_m, far_q) in ((1, (u1, m1, q1)), (3, (u3, m3, q3))):
-
-        def link(k, carry):
-            p = placed[which * count + k]
-            u, m, q = far_u[k], far_m[k], far_q[k]
-            u2 = inverse[p] * r2_out[p]
-            p1 = inverse[p] * r1[p] + beta1 * field[p]
-            far_p1 = (1.0 + beta1) * u - alpha0 * m
-            far_u2 = u - (alpha0 + alpha1 * (1.0 + beta1)) * m + both * q
-            here = after[p]
-            return carry[0] + folded(u2 * q + far_u2 * here), carry[1] + folded(p1 * q + far_p1 * here)
-
-        links = lax.fori_loop(0, count, link, links, unroll=2)
-    publish(partial, (sums[0], sums[1] - both * links[0], sums[2] - both * links[1]))
-
-
-def last_kernel(
-    sums0, sums1, sums2, placed, g0, g1, g2, g3, field, image, inverse, r1, w1, r2, w2,
-    estimate_out, left_out, estimate, left, sems,
-):
-    first, then, last = gathered(sums0), gathered(sums1), gathered(sums2)
-    alpha0 = first[0:1] / first[1:2]
-    beta1 = then[0:1] / first[0:1]
-    curve1 = then[1:2] + beta1 * (then[2:3] + beta1 * first[1:2])
-    alpha1 = then[0:1] / curve1
-    beta2 = last[0:1] / then[0:1]
-    alpha2 = last[0:1] / (last[1:2] + beta2 * (last[2:3] + beta2 * curve1))
-    part = alpha2 * alpha0 * alpha1
+    (r1u1, u1w1, u1w0, u0w1, w1m1, w1m0, w0m0, u1n1, u1n0, m1n1, mixed, m0n0, u0n1, u0n0) = (
+        then[i : i + 1] for i in range(SUMS)
+    )
+    beta1 = r1u1 / first[0:1]
+    curve1 = u1w1 + beta1 * (u1w0 + u0w1 + beta1 * first[1:2])
+    a = r1u1 / curve1
+    c = a * beta1
+    r2u2 = r1u1 - 2.0 * (a * u1w1 + c * u1w0) + a * a * w1m1 + 2.0 * a * c * w1m0 + c * c * w0m0
+    u2w2 = u1w1 - a * (u1n1 + w1m1) - c * (u1n0 + w1m0) + a * a * m1n1 + a * c * mixed + c * c * m0n0
+    cross = (u1w1 - a * w1m1 - c * w1m0) + beta1 * (u1w0 - a * w1m0 - c * w0m0)
+    cross = cross + (u1w1 - a * u1n1 - c * u1n0) + beta1 * (u0w1 - a * u0n1 - c * u0n0)
+    beta2 = r2u2 / r1u1
+    alpha2 = r2u2 / (u2w2 + beta2 * (cross + beta2 * curve1))
+    steps = a + alpha2 * beta2
+    for_u0 = alpha0 + steps * beta1
+    part = alpha2 * alpha0 * a
     size = field.shape[0] // STRIPES
     copies = []
 
-    def residual(p, carry):
-        left[p] = r2[p] - alpha2 * (w2[p] + beta2 * (w1[p] + beta1 * image[p]))
-        return carry
-
-    lax.fori_loop(0, field.shape[0], residual, 0, unroll=2)
+    def one(p, carry):
+        w1p, w0p = w1[p], image[p]
+        r2 = r1[p] - a * w1p - c * w0p
+        estimate[p] = for_u0 * field[p] + inverse[p] * (steps * r1[p] + alpha2 * r2)
+        n0 = second[p]
+        w2 = w1p - a * (n0 - alpha0 * base[p]) - c * n0
+        left[p] = r2 - alpha2 * (w2 + beta2 * (w1p + beta1 * w0p))
+        return carry
+
+    for k in range(STRIPES):
+        lax.fori_loop(k * size, (k + 1) * size, one, 0, unroll=2)
+        rows = pl.ds(k * size, size)
+        copies.append(pltpu.make_async_copy(estimate.at[rows], estimate_out.at[rows], sems.at[k]))
+        copies[-1].start()
     count = g0.shape[0]
     for which, got in enumerate((g0, g1, g2, g3)):
 
@@ -468,19 +479,8 @@
             return carry
 
         lax.fori_loop(0, count, link, 0, unroll=4)
-
-    def iterate(p, carry):
-        p1 = inverse[p] * r1[p] + beta1 * field[p]
-        estimate[p] = alpha0 * field[p] + alpha1 * p1 + alpha2 * (inverse[p] * r2[p] + beta2 * p1)
-        return carry
-
     copies.append(pltpu.make_async_copy(left, left_out, sems.at[STRIPES]))
     copies[-1].start()
-    for c in range(STRIPES):
-        lax.fori_loop(c * size, (c + 1) * size, iterate, 0, unroll=2)
-        rows = pl.ds(c * size, size)
-        copies.append(pltpu.make_async_copy(estimate.at[rows], estimate_out.at[rows], sems.at[c]))
-        copies[-1].start()
     for copy in copies:
         copy.wait()
 
@@ -596,23 +596,21 @@
     )
     s0, s1, s2, s3 = sends
     q1, q3 = back(s1, "sector", True), back(s3, "axial", False)
-    base, r1, w1, partial = call(
+    q0, q2 = onward(s0, "sector", True), onward(s2, "axial", False)
+    base, r1, w1, totals = call(
         first_step_kernel, "first_step",
-        (sums0, blocks, after, loads, field, image, second, inverse), (vec, vec, vec, total),
+        (sums0, blocks, after, loads, field, image, second, inverse), (vec, vec, vec, struct(16, 8, cases)),
+    )
+    (partial,) = call(
+        links_kernel, "links",
+        (sums0, placed, totals, far_u1, far_u3, m1, m3, q1, q3, field, image, after, r1, w1, inverse),
+        (struct(devices, 16, cases),),
     )
     sums1 = everywhere(partial)
-    s0, s2, base, sums1 = lax.optimization_barrier((s0, s2, base, sums1))
-    q0, q2 = onward(s0, "sector", True), onward(s2, "axial", False)
-    r2, w2, partial = call(
-        second_step_kernel, "second_step",
-        (sums0, sums1, placed, far_u1, far_u3, m1, m3, q1, q3, field, image, second, after, r1, w1, inverse, base),
-        (vec, vec, total),
-    )
-    sums2 = everywhere(partial)
-    r2, w2, sums2 = lax.optimization_barrier((r2, w2, sums2))
+    base, sums1 = lax.optimization_barrier((base, sums1))
     estimate, left = call(
         last_kernel, "last",
-        (sums0, sums1, sums2, placed, q0, q1, q2, q3, field, image, inverse, r1, w1, r2, w2), (vec, vec),
+        (sums0, sums1, placed, q0, q1, q2, q3, field, image, inverse, second, base, r1, w1), (vec, vec),
         (pltpu.VMEM(loads.shape, F32), pltpu.VMEM(loads.shape, F32), pltpu.SemaphoreType.DMA((STRIPES + 1,))),
         out=pl.BlockSpec(memory_space=pl.ANY),
     )

time: 182 us -> 178 us (0.978)
  blocking collectives: 43.9 us -> 35.2 us
  waiting for transfers between devices: 34.8 us -> 38.1 us
    all_to_all x3 -> x2, blocking collectives: 43.9 us -> 35.2 us  [everywhere(): lax.all_to_all(partial, AXES, split_axis=0, concat_axis=0, tiled=True)]
    ppermute x8, waiting for transfers between devices: 6.87 us -> 10.1 us  [back(): lax.ppermute(value, axis, [((i + 1) % n, i) for i in range(n) if wrap or...]
  transfers between devices with their start and end apart: 19 -> 19, of which waited for: 5 -> 6; matrix products, arithmetic and copies ran while one was open for 2% -> 2% of each run, Pallas kernels for 20% -> 21%
where the time goes in v6:
time: 178 us; the launch traced here: 177 us
  Pallas kernels  53.1 us (30%)
  starting transfers between devices  43.1 us (24%)
  waiting for transfers between devices  38.1 us (21%)
  blocking collectives  35.2 us (20%)
  local copies, waits for them, and re-layouts  3.4 us (2%)
  other arithmetic  2.43 us (1%)
    all_to_all x2, blocking collectives, everywhere(): lax.all_to_all(partial, AXES, split_axis=0, concat_axis=0, tiled=True)  35.2 us
    pallas_call x9, Pallas kernels, call(): pl.pallas_call(kernel, in_specs=[SMEM if ints(a) else HBM if i in far els...  34.1 us
    ppermute x9, starting transfers between devices, onward(): lax.ppermute(value, axis, [(i, (i + 1) % n) for i in range(n) if wrap or...  20.7 us
    ppermute x9, waiting for transfers between devices, onward(): lax.ppermute(value, axis, [(i, (i + 1) % n) for i in range(n) if wrap or...  19.1 us
    ppermute x8, starting transfers between devices, back(): lax.ppermute(value, axis, [((i + 1) % n, i) for i in range(n) if wrap or...  15.1 us
    pallas_call x1, Pallas kernels, pack_call(): pl.pallas_call(functools.partial(pack_kernel, slots_each), grid=(elems //...  10.7 us
    ppermute x8, waiting for transfers between devices, back(): lax.ppermute(value, axis, [((i + 1) % n, i) for i in range(n) if wrap or...  10.1 us
    all_to_all x2, waiting for transfers between devices, everywhere(): lax.all_to_all(partial, AXES, split_axis=0, concat_axis=0, tiled=True)  8.97 us
  transfers between devices with their start and end apart: 19, of which 6 were waited for; matrix products, arithmetic and copies ran while one was open for 2% of the time, Pallas kernels for 21%

profile of v6, /device:TPU:0, one launch (start us, length us, event | category | flops | bytes accessed | tf_op | source)
XLA Modules:
  0.0 177.0 jit_solution(6736537425667299573)
XLA Ops:
  0.6 3.0 %own.1 = (f32[16,72,128]{2,1,0:T(8,128)}, f32[16,72,128]{2,1,0:T(8,128)}) custom-call(s32[2,2,16]{2,1,0:T(2,128)} %bitcast.32, f32[64,64,128]{2,1,0:T(8,128)} %bitcast.18, f32[2,16,64]{2,1,0:T(8,128)} %conduct.1), custom_call_target="tpu_custom_call" | custom-call | tf_op jit(solution)/shard_map/own/pallas_call | solution.py:179
  3.6 3.1 %collective-permute-start.1 = (f32[16,72,128]{2,1,0:T(8,128)}, f32[16,72,128]{2,1,0:T(8,128)S(1)}, u32[]{:S(2)}, u32[]{:S(2)}) collective-permute-start(f32[16,72,128]{2,1,0:T(8,128)} %get-tuple-element.72), channel_id=1, source_target_pairs={{0,8},{8,16},{16,24},{24,0},{1,9},{9,17},{17,25},{25,1},{2,10},{10... | collective-permute-start | bytes 1769480 | tf_op jit(solution)/shard_map/ppermute | solution.py:510
  6.7 1.5 collective-permute-start.2
  8.2 1.6 collective-permute-start
  10.5 10.7 %pack.1 = (f32[4096,128]{1,0:T(8,128)}, f32[256,128]{1,0:T(8,128)}) custom-call(s32[128]{0:T(128)} %bitcast.35, s32[128]{0:T(128)} %patches.1, s32[1]{0:T(128)S(6)} %copy.14.counts, f32[64,64,128]{2,1,0:T(8,128)} %bitcast.27, bf16[128,64,256]{2,1,0:T(8,128)(2,1)} %bitcast.26, s32[64,128]{1,0:T(8,128)} %bitcast.31), custom_call_target="tpu_custom_call" | custom-call | tf_op jit(solution)/shard_map/pack/pallas_call | solution.py:99
  22.9 2.5 %far.2 = f32[16,64,128]{2,1,0:T(8,128)} custom-call(s32[2,2,16]{2,1,0:T(2,128)} %copy-done.17, f32[64,64,128]{2,1,0:T(8,128)} %bitcast.19), custom_call_target="tpu_custom_call" | custom-call | tf_op jit(solution)/shard_map/far/pallas_call | solution.py:191
  25.4 1.8 %collective-permute-start.3 = (f32[16,64,128]{2,1,0:T(8,128)}, f32[16,64,128]{2,1,0:T(8,128)S(1)}, u32[]{:S(2)}, u32[]{:S(2)}) collective-permute-start(f32[16,64,128]{2,1,0:T(8,128)} %far.2), channel_id=1, source_target_pairs={{8,0},{16,8},{24,16},{0,24},{9,1},{17,9},{25,17},{1,25},{10,2},{18... | collective-permute-start | bytes 1572872 | tf_op jit(solution)/shard_map/ppermute | solution.py:515
  27.2 2.8 %all-to-all-start = ((f32[32,8,128]{2,1,0:T(8,128)}), f32[32,8,128]{2,1,0:T(8,128)S(1)}, u32[]{:S(2)}, u32[]{:S(2)}) async-start(f32[32,8,128]{2,1,0:T(8,128)} %bitcast.6), calls=%async_computation | async-start | bytes 262144 | tf_op jit(solution)/shard_map/all_to_all | solution.py:505
  31.1 2.8 %far.3 = f32[16,64,128]{2,1,0:T(8,128)} custom-call(s32[16]{0:T(128)} %convert_reduce_fusion.index, f32[64,64,128]{2,1,0:T(8,128)} %bitcast.20), custom_call_target="tpu_custom_call" | custom-call | tf_op jit(solution)/shard_map/far/pallas_call | solution.py:191
  33.9 6.7 %collective-permute-done.3.g1 = f32[16,64,128]{2,1,0:T(8,128)S(1)} collective-permute-done((f32[16,64,128]{2,1,0:T(8,128)}, f32[16,64,128]{2,1,0:T(8,128)S(1)}, u32[]{:S(2)}, u32[]{:S(2)}) %collective-permute-start.3) | collective-permute-done | bytes 524320 | tf_op jit(solution)/shard_map/ppermute | solution.py:515
  40.6 3.8 %all-to-all-done = f32[32,8,128]{2,1,0:T(8,128)S(1)} async-done(((f32[32,8,128]{2,1,0:T(8,128)}), f32[32,8,128]{2,1,0:T(8,128)S(1)}, u32[]{:S(2)}, u32[]{:S(2)}) %all-to-all-start) | async-done | bytes 131104 | tf_op jit(solution)/shard_map/all_to_all | solution.py:505
  44.4 4.5 %all-to-all-start.1 = ((f32[32,128,128]{2,1,0:T(8,128)}), f32[32,128,128]{2,1,0:T(8,128)S(1)}, u32[]{:S(2)}, u32[]{:S(2)}) async-start(f32[32,128,128]{2,1,0:T(8,128)} %bitcast.28), calls=%async_computation.1 | async-start | bytes 4194304 | tf_op jit(solution)/shard_map/all_to_all | solution.py:505
  53.0 3.7 %diagonal.1 = (f32[64,128]{1,0:T(8,128)}, f32[64,128]{1,0:T(8,128)}, f32[16,128]{1,0:T(8,128)}, f32[16,128]{1,0:T(8,128)}, f32[16,128]{1,0:T(8,128)}, /*index=5*/f32[16,128]{1,0:T(8,128)}) custom-call(s32[256]{0:T(256)} %select_reduce_fusion.tags, s32[64]{0:T(128)} %get-tuple-element.123.picked, f32[256,128]{1,0:T(8,128)} %bitcast.30, ...), custom_call_target="tpu_custom_call" | custom-call | bytes 1434880 | tf_op jit(solution)/shard_map/diagonal/pallas_call | solution.py:491
  56.7 1.7 collective-permute-start.4
  58.3 2.1 %collective-permute-start.5 = (f32[16,128]{1,0:T(8,128)}, f32[16,128]{1,0:T(8,128)S(1)}, u32[]{:S(2)}, u32[]{:S(2)}) collective-permute-start(f32[16,128]{1,0:T(8,128)} %get-tuple-element.85), channel_id=1, source_target_pairs={{8,0},{16,8},{24,16},{0,24},{9,1},{17,9},{25,17},{1,25},{10,2},{18... | collective-permute-start | bytes 24584 | tf_op jit(solution)/shard_map/ppermute | solution.py:515
  60.5 2.7 %collective-permute-start.6 = (f32[16,128]{1,0:T(8,128)}, f32[16,128]{1,0:T(8,128)S(1)}, u32[]{:S(2)}, u32[]{:S(2)}) collective-permute-start(f32[16,128]{1,0:T(8,128)} %get-tuple-element.86), channel_id=1, source_target_pairs={{0,1},{1,2},{2,3},{3,4},{4,5},{5,6},{6,7},{8,9},{9,10},{10,11},{11... | collective-permute-start | bytes 24584 | tf_op jit(solution)/shard_map/ppermute | solution.py:510
  64.5 5.4 %expand.1 = (f32[64,64,128]{2,1,0:T(8,128)}, f32[64,64,128]{2,1,0:T(8,128)}, f32[64,64,128]{2,1,0:T(8,128)}) custom-call(f32[64,128]{1,0:T(8,128)} %get-tuple-element.79.over, f32[64,128]{1,0:T(8,128)} %get-tuple-element.80.gain_rows, f32[64,64,128]{2,1,0:T(8,128)} %bitcast.21), custom_call_target="tpu_custom_call" | custom-call | bytes 8454144 | tf_op jit(solution)/shard_map/expand/pallas_call | solution.py:491
  69.9 17.9 %collective-permute-done.4.t0 = f32[16,128]{1,0:T(8,128)S(1)} collective-permute-done((f32[16,128]{1,0:T(8,128)}, f32[16,128]{1,0:T(8,128)S(1)}, u32[]{:S(2)}, u32[]{:S(2)}) %collective-permute-start.4) | collective-permute-done | bytes 8224 | tf_op jit(solution)/shard_map/ppermute | solution.py:510
  89.3 3.6 %edges.1 = (f32[16,64,128]{2,1,0:T(8,128)}, f32[16,64,128]{2,1,0:T(8,128)}, f32[16,64,128]{2,1,0:T(8,128)}, f32[16,64,128]{2,1,0:T(8,128)}) custom-call(f32[16,128]{1,0:T(8,128)} %copy-done.11, f32[16,128]{1,0:T(8,128)} %copy-done.12, f32[16,128]{1,0:T(8,128)} %copy-done.13, f32[16,128]{1,0:T(8,128)} %copy-done.14, f32[16,72,128]{2,1,0:T(8,128)} %copy-done.6, ...), custom_call_target="tpu_custom_call" | custom-call | bytes 4358144 | tf_op jit(solution)/shard_map/edges/pallas_call | solution.py:491
  92.9 5.2 %all-to-all-done.1 = f32[32,128,128]{2,1,0:T(8,128)S(1)} async-done(((f32[32,128,128]{2,1,0:T(8,128)}), f32[32,128,128]{2,1,0:T(8,128)S(1)}, u32[]{:S(2)}, u32[]{:S(2)}) %all-to-all-start.1) | async-done | bytes 2097184 | tf_op jit(solution)/shard_map/all_to_all | solution.py:505
  98.1 7.3 %assemble.1 = (f32[64,64,128]{2,1,0:T(8,128)S(1)}, bf16[64,64,192]{2,1,0:T(8,128)(2,1)S(1)}, f32[64,64,128]{2,1,0:T(8,128)S(1)}, f32[16,64,128]{2,1,0:T(8,128)S(...) custom-call(s32[256]{0:T(256)S(1)} %copy-done.3, ...), custom_call_target="tpu_custom_call" | custom-call | bytes 26740224 | tf_op jit(solution)/shard_map/assemble/pallas_call | solution.py:491
  105.4 5.8 %collective-permute-start.9 = (f32[16,64,128]{2,1,0:T(8,128)S(1)}, f32[16,64,128]{2,1,0:T(8,128)S(1)}, u32[]{:S(2)}, u32[]{:S(2)}) collective-permute-start(f32[16,64,128]{2,1,0:T(8,128)S(1)} %get-tuple-element.103), channel_id=1, source_target_pairs={{0,8},{8,16},{16,24},{24,0},{1,9},{9,17},{17,25},{25,1},{2,10},{10... | collective-permute-start | bytes 1572872 | tf_op jit(solution)/shard_map/ppermute | solution.py:510
  113.8 2.2 %first_local.1 = (f32[64,64,128]{2,1,0:T(8,128)S(1)}, f32[32,8,128]{2,1,0:T(8,128)S(1)}) custom-call(bf16[64,64,192]{2,1,0:T(8,128)(2,1)S(1)} %get-tuple-element.94.blocks, f32[64,64,128]{2,1,0:T(8,128)S(1)} %get-tuple-element.95.after, f32[64,64,128]{2,1,0:T(8,128)S(1)} %get-tuple-element.96.image, f32[64,64,128]{2,1,0:T(8,128)S(1)} %bitcast.23, ...), custom_call_target="tpu_custom_call" | custom-call | bytes 12189696 | tf_op jit(solution)/shard_map/first_local/pallas_call | solution.py:491
  116.0 20.0 %all_to_all.20.sums.sums0 = f32[32,8,128]{2,1,0:T(8,128)S(1)} all-to-all(f32[32,8,128]{2,1,0:T(8,128)S(1)} %get-tuple-element.99), channel_id=1, replica_groups=mesh['sector'=4,'axial'=8] {'sector','axial'}, dimensions={0} | all-to-all | bytes 262144 | tf_op jit(solution)/shard_map/all_to_all | solution.py:505
  136.0 1.5 second.1
  137.5 6.0 %collective-permute-start.13 = (f32[16,64,128]{2,1,0:T(8,128)S(1)}, f32[16,64,128]{2,1,0:T(8,128)S(1)}, u32[]{:S(2)}, u32[]{:S(2)}) collective-permute-start(f32[16,64,128]{2,1,0:T(8,128)S(1)} %get-tuple-element.112), channel_id=1, source_target_pairs={{8,0},{16,8},{24,16},{0,24},{9,1},{17,9},{25,17},{1,25},{10,2},{18... | collective-permute-start | bytes 1572872 | tf_op jit(solution)/shard_map/ppermute | solution.py:515
  144.9 3.1 %collective-permute-start.16 = (f32[16,64,128]{2,1,0:T(8,128)S(1)}, f32[16,64,128]{2,1,0:T(8,128)S(1)}, u32[]{:S(2)}, u32[]{:S(2)}) collective-permute-start(f32[16,64,128]{2,1,0:T(8,128)S(1)} %get-tuple-element.118), channel_id=1, source_target_pairs={{0,1},{1,2},{2,3},{3,4},{4,5},{5,6},{6,7},{8,9},{9,10},{10,11},{11... | collective-permute-start | bytes 1572872 | tf_op jit(solution)/shard_map/ppermute | solution.py:510
  148.0 4.6 %first_step.1 = (f32[64,64,128]{2,1,0:T(8,128)S(1)}, f32[64,64,128]{2,1,0:T(8,128)S(1)}, f32[64,64,128]{2,1,0:T(8,128)S(1)}, f32[16,8,128]{2,1,0:T(8,128)S(1)}) custom-call(f32[32,8,128]{2,1,0:T(8,128)S(1)} %all_to_all.20.sums.sums0, bf16[64,64,192]{2,1,0:T(8,128)(2,1)S(1)} %get-tuple-element.94.blocks, f32[64,64,128]{2,1,0:T(8,128)S(1)} %get-tuple-element.108.after, ...), custom_call_target="tpu_custom_call" | custom-call | bytes 20643840 | tf_op jit(solution)/shard_map/first_step/pallas_call | solution.py:491
  152.6 3.3 %collective-permute-done.13.far_q0.g1 = f32[16,64,128]{2,1,0:T(8,128)S(1)} collective-permute-done((f32[16,64,128]{2,1,0:T(8,128)S(1)}, f32[16,64,128]{2,1,0:T(8,128)S(1)}, u32[]{:S(2)}, u32[]{:S(2)}) %collective-permute-start.13) | collective-permute-done | bytes 524320 | tf_op jit(solution)/shard_map/ppermute | solution.py:515
  156.0 1.8 links.1
  157.7 15.2 %all_to_all.21.sums1 = f32[32,16,128]{2,1,0:T(8,128)S(1)} all-to-all(f32[32,16,128]{2,1,0:T(8,128)S(1)} %links.1), channel_id=1, replica_groups=mesh['sector'=4,'axial'=8] {'sector','axial'}, dimensions={0} | all-to-all | bytes 524288 | tf_op jit(solution)/shard_map/all_to_all | solution.py:505
  172.9 4.0 %last.1 = (f32[64,64,128]{2,1,0:T(8,128)}, f32[64,64,128]{2,1,0:T(8,128)}) custom-call(f32[32,8,128]{2,1,0:T(8,128)S(1)} %all_to_all.20.sums.sums0, f32[32,16,128]{2,1,0:T(8,128)S(1)} %all_to_all.21.sums1, s32[64]{0:T(128)S(1)} %get-tuple-element.122.placed, f32[16,64,128]{2,1,0:T(8,128)S(1)} %collective-permute-done.15.g0, ...), custom_call_target="tpu_custom_call" | custom-call | bytes 21364992 | tf_op jit(solution)/shard_map/last/pallas_call | solution.py:491
  (63 shorter events, 13.5 us)
Async XLA Ops:
  0.6 7.5 %copy-start.15 = (s32[2,16,2]{1,2,0:T(2,128)S(1)}, s32[2,16,2]{1,2,0:T(2,128)}, u32[]{:S(2)}) copy-start(s32[2,16,2]{1,2,0:T(2,128)} %param.17) | copy-start | bytes 772
  3.6 26.5 %collective-permute-start.1 = (f32[16,72,128]{2,1,0:T(8,128)}, f32[16,72,128]{2,1,0:T(8,128)S(1)}, u32[]{:S(2)}, u32[]{:S(2)}) collective-permute-start(f32[16,72,128]{2,1,0:T(8,128)} %get-tuple-element.72), channel_id=1, source_target_pairs={{0,8},{8,16},{16,24},{24,0},{1,9},{9,17},{17,25},{25,1},{2,10},{10... | collective-permute-start | bytes 1769480 | tf_op jit(solution)/shard_map/ppermute | solution.py:510
  6.7 23.4 %collective-permute-start.2 = (f32[16,72,128]{2,1,0:T(8,128)}, f32[16,72,128]{2,1,0:T(8,128)S(1)}, u32[]{:S(2)}, u32[]{:S(2)}) collective-permute-start(f32[16,72,128]{2,1,0:T(8,128)} %get-tuple-element.73), channel_id=1, source_target_pairs={{0,1},{1,2},{2,3},{3,4},{4,5},{5,6},{6,7},{8,9},{9,10},{10,11},{11... | collective-permute-start | bytes 1769480 | tf_op jit(solution)/shard_map/ppermute | solution.py:510
  8.2 14.2 %collective-permute-start = (s32[2,2,16]{2,1,0:T(2,128)S(1)}, s32[2,2,16]{2,1,0:T(2,128)S(1)}, u32[]{:S(2)}, u32[]{:S(2)}) collective-permute-start(s32[2,2,16]{2,1,0:T(2,128)S(1)} %bitcast.33), channel_id=1, source_target_pairs={{0,8},{8,16},{16,24},{24,0},{1,9},{9,17},{17,25},{25,1},{2,10},{10... | collective-permute-start | bytes 776 | tf_op jit(solution)/shard_map/ppermute | solution.py:510
  25.4 15.2 %collective-permute-start.3 = (f32[16,64,128]{2,1,0:T(8,128)}, f32[16,64,128]{2,1,0:T(8,128)S(1)}, u32[]{:S(2)}, u32[]{:S(2)}) collective-permute-start(f32[16,64,128]{2,1,0:T(8,128)} %far.2), channel_id=1, source_target_pairs={{8,0},{16,8},{24,16},{0,24},{9,1},{17,9},{25,17},{1,25},{10,2},{18... | collective-permute-start | bytes 1572872 | tf_op jit(solution)/shard_map/ppermute | solution.py:515
  27.2 17.2 %all-to-all-start = ((f32[32,8,128]{2,1,0:T(8,128)}), f32[32,8,128]{2,1,0:T(8,128)S(1)}, u32[]{:S(2)}, u32[]{:S(2)}) async-start(f32[32,8,128]{2,1,0:T(8,128)} %bitcast.6), calls=%async_computation | async-start | bytes 262144 | tf_op jit(solution)/shard_map/all_to_all | solution.py:505
  30.1 14.3 %copy-start.6 = (f32[16,72,128]{2,1,0:T(8,128)}, f32[16,72,128]{2,1,0:T(8,128)S(1)}, u32[]{:S(2)}) copy-start(f32[16,72,128]{2,1,0:T(8,128)S(1)} %collective-permute-done.1.g0) | copy-start | bytes 1769476
  30.1 14.3 %copy-start.5 = (f32[16,72,128]{2,1,0:T(8,128)}, f32[16,72,128]{2,1,0:T(8,128)S(1)}, u32[]{:S(2)}) copy-start(f32[16,72,128]{2,1,0:T(8,128)S(1)} %collective-permute-done.2.g2) | copy-start | bytes 1769476
  40.6 3.8 %copy-start.8 = (f32[16,64,128]{2,1,0:T(8,128)}, f32[16,64,128]{2,1,0:T(8,128)S(1)}, u32[]{:S(2)}) copy-start(f32[16,64,128]{2,1,0:T(8,128)S(1)} %collective-permute-done.3.g1) | copy-start | bytes 1572868
  44.4 7.2 %copy-start.7 = (f32[32,8,128]{2,1,0:T(8,128)}, f32[32,8,128]{2,1,0:T(8,128)S(1)}, u32[]{:S(2)}) copy-start(f32[32,8,128]{2,1,0:T(8,128)S(1)} %all-to-all-done) | copy-start | bytes 393220
  44.4 5.8 %copy-start.10 = (f32[4096]{0:T(1024)S(1)}, f32[4096]{0:T(1024)}, u32[]{:S(2)}) copy-start(f32[4096]{0:T(1024)} %param.16) | copy-start | bytes 49156
  44.4 7.9 %copy-start.16 = (s32[16]{0:T(128)S(1)}, s32[16]{0:T(128)}, u32[]{:S(2)}) copy-start(s32[16]{0:T(128)} %convert_reduce_fusion.index) | copy-start | bytes 196
  44.4 53.6 %all-to-all-start.1 = ((f32[32,128,128]{2,1,0:T(8,128)}), f32[32,128,128]{2,1,0:T(8,128)S(1)}, u32[]{:S(2)}, u32[]{:S(2)}) async-start(f32[32,128,128]{2,1,0:T(8,128)} %bitcast.28), calls=%async_computation.1 | async-start | bytes 4194304 | tf_op jit(solution)/shard_map/all_to_all | solution.py:505
  48.9 39.0 %collective-permute-start.8 = (f32[16,64,128]{2,1,0:T(8,128)}, f32[16,64,128]{2,1,0:T(8,128)S(1)}, u32[]{:S(2)}, u32[]{:S(2)}) collective-permute-start(f32[16,64,128]{2,1,0:T(8,128)} %far.3), channel_id=1, source_target_pairs={{1,0},{2,1},{3,2},{4,3},{5,4},{6,5},{7,6},{9,8},{10,9},{11,10},{12... | collective-permute-start | bytes 1572872 | tf_op jit(solution)/shard_map/ppermute | solution.py:515
  56.7 31.2 %collective-permute-start.4 = (f32[16,128]{1,0:T(8,128)}, f32[16,128]{1,0:T(8,128)S(1)}, u32[]{:S(2)}, u32[]{:S(2)}) collective-permute-start(f32[16,128]{1,0:T(8,128)} %get-tuple-element.84), channel_id=1, source_target_pairs={{0,8},{8,16},{16,24},{24,0},{1,9},{9,17},{17,25},{25,1},{2,10},{10... | collective-permute-start | bytes 24584 | tf_op jit(solution)/shard_map/ppermute | solution.py:510
  58.3 29.5 %collective-permute-start.5 = (f32[16,128]{1,0:T(8,128)}, f32[16,128]{1,0:T(8,128)S(1)}, u32[]{:S(2)}, u32[]{:S(2)}) collective-permute-start(f32[16,128]{1,0:T(8,128)} %get-tuple-element.85), channel_id=1, source_target_pairs={{8,0},{16,8},{24,16},{0,24},{9,1},{17,9},{25,17},{1,25},{10,2},{18... | collective-permute-start | bytes 24584 | tf_op jit(solution)/shard_map/ppermute | solution.py:515
  60.5 27.3 %collective-permute-start.6 = (f32[16,128]{1,0:T(8,128)}, f32[16,128]{1,0:T(8,128)S(1)}, u32[]{:S(2)}, u32[]{:S(2)}) collective-permute-start(f32[16,128]{1,0:T(8,128)} %get-tuple-element.86), channel_id=1, source_target_pairs={{0,1},{1,2},{2,3},{3,4},{4,5},{5,6},{6,7},{8,9},{9,10},{10,11},{11... | collective-permute-start | bytes 24584 | tf_op jit(solution)/shard_map/ppermute | solution.py:510
  63.2 24.7 %collective-permute-start.7 = (f32[16,128]{1,0:T(8,128)}, f32[16,128]{1,0:T(8,128)S(1)}, u32[]{:S(2)}, u32[]{:S(2)}) collective-permute-start(f32[16,128]{1,0:T(8,128)} %get-tuple-element.87), channel_id=1, source_target_pairs={{1,0},{2,1},{3,2},{4,3},{5,4},{6,5},{7,6},{9,8},{10,9},{11,10},{12... | collective-permute-start | bytes 24584 | tf_op jit(solution)/shard_map/ppermute | solution.py:515
  64.5 33.6 %copy-start.3 = (s32[256]{0:T(256)S(1)}, s32[256]{0:T(256)}, u32[]{:S(2)}) copy-start(s32[256]{0:T(256)} %select_reduce_fusion.tags) | copy-start | bytes 3076
  64.5 33.6 %copy-start.4 = (s32[64]{0:T(128)S(1)}, s32[64]{0:T(128)}, u32[]{:S(2)}) copy-start(s32[64]{0:T(128)} %get-tuple-element.123.picked) | copy-start | bytes 772
  88.5 0.9 copy-start.9
  98.1 15.7 %copy-start = (f32[4096,128]{1,0:T(8,128)S(1)}, f32[4096,128]{1,0:T(8,128)}, u32[]{:S(2)}) copy-start(f32[4096,128]{1,0:T(8,128)} %param.19) | copy-start | bytes 6291460
  105.4 30.6 %collective-permute-start.9 = (f32[16,64,128]{2,1,0:T(8,128)S(1)}, f32[16,64,128]{2,1,0:T(8,128)S(1)}, u32[]{:S(2)}, u32[]{:S(2)}) collective-permute-start(f32[16,64,128]{2,1,0:T(8,128)S(1)} %get-tuple-element.103), channel_id=1, source_target_pairs={{0,8},{8,16},{16,24},{24,0},{1,9},{9,17},{17,25},{25,1},{2,10},{10... | collective-permute-start | bytes 1572872 | tf_op jit(solution)/shard_map/ppermute | solution.py:510
  111.2 24.8 %collective-permute-start.10 = (f32[16,64,128]{2,1,0:T(8,128)S(1)}, f32[16,64,128]{2,1,0:T(8,128)S(1)}, u32[]{:S(2)}, u32[]{:S(2)}) collective-permute-start(f32[16,64,128]{2,1,0:T(8,128)S(1)} %get-tuple-element.104), channel_id=1, source_target_pairs={{8,0},{16,8},{24,16},{0,24},{9,1},{17,9},{25,17},{1,25},{10,2},{18... | collective-permute-start | bytes 1572872 | tf_op jit(solution)/shard_map/ppermute | solution.py:515
  111.2 24.8 %collective-permute-start.11 = (f32[16,64,128]{2,1,0:T(8,128)S(1)}, f32[16,64,128]{2,1,0:T(8,128)S(1)}, u32[]{:S(2)}, u32[]{:S(2)}) collective-permute-start(f32[16,64,128]{2,1,0:T(8,128)S(1)} %get-tuple-element.105), channel_id=1, source_target_pairs={{0,1},{1,2},{2,3},{3,4},{4,5},{5,6},{6,7},{8,9},{9,10},{10,11},{11... | collective-permute-start | bytes 1572872 | tf_op jit(solution)/shard_map/ppermute | solution.py:510
  112.5 23.5 %collective-permute-start.12 = (f32[16,64,128]{2,1,0:T(8,128)S(1)}, f32[16,64,128]{2,1,0:T(8,128)S(1)}, u32[]{:S(2)}, u32[]{:S(2)}) collective-permute-start(f32[16,64,128]{2,1,0:T(8,128)S(1)} %get-tuple-element.106), channel_id=1, source_target_pairs={{1,0},{2,1},{3,2},{4,3},{5,4},{6,5},{7,6},{9,8},{10,9},{11,10},{12... | collective-permute-start | bytes 1572872 | tf_op jit(solution)/shard_map/ppermute | solution.py:515
  137.5 18.4 %collective-permute-start.13 = (f32[16,64,128]{2,1,0:T(8,128)S(1)}, f32[16,64,128]{2,1,0:T(8,128)S(1)}, u32[]{:S(2)}, u32[]{:S(2)}) collective-permute-start(f32[16,64,128]{2,1,0:T(8,128)S(1)} %get-tuple-element.112), channel_id=1, source_target_pairs={{8,0},{16,8},{24,16},{0,24},{9,1},{17,9},{25,17},{1,25},{10,2},{18... | collective-permute-start | bytes 1572872 | tf_op jit(solution)/shard_map/ppermute | solution.py:515
  143.5 12.4 %collective-permute-start.14 = (f32[16,64,128]{2,1,0:T(8,128)S(1)}, f32[16,64,128]{2,1,0:T(8,128)S(1)}, u32[]{:S(2)}, u32[]{:S(2)}) collective-permute-start(f32[16,64,128]{2,1,0:T(8,128)S(1)} %get-tuple-element.113), channel_id=1, source_target_pairs={{1,0},{2,1},{3,2},{4,3},{5,4},{6,5},{7,6},{9,8},{10,9},{11,10},{12... | collective-permute-start | bytes 1572872 | tf_op jit(solution)/shard_map/ppermute | solution.py:515
  144.8 28.1 %collective-permute-start.15 = (f32[16,64,128]{2,1,0:T(8,128)S(1)}, f32[16,64,128]{2,1,0:T(8,128)S(1)}, u32[]{:S(2)}, u32[]{:S(2)}) collective-permute-start(f32[16,64,128]{2,1,0:T(8,128)S(1)} %get-tuple-element.117), channel_id=1, source_target_pairs={{0,8},{8,16},{16,24},{24,0},{1,9},{9,17},{17,25},{25,1},{2,10},{10... | collective-permute-start | bytes 1572872 | tf_op jit(solution)/shard_map/ppermute | solution.py:510
  144.9 28.1 %collective-permute-start.16 = (f32[16,64,128]{2,1,0:T(8,128)S(1)}, f32[16,64,128]{2,1,0:T(8,128)S(1)}, u32[]{:S(2)}, u32[]{:S(2)}) collective-permute-start(f32[16,64,128]{2,1,0:T(8,128)S(1)} %get-tuple-element.118), channel_id=1, source_target_pairs={{0,1},{1,2},{2,3},{3,4},{4,5},{5,6},{6,7},{8,9},{9,10},{10,11},{11... | collective-permute-start | bytes 1572872 | tf_op jit(solution)/shard_map/ppermute | solution.py:510
  148.0 8.0 %copy-start.1 = (f32[16,64,128]{2,1,0:T(8,128)S(1)}, f32[16,64,128]{2,1,0:T(8,128)}, u32[]{:S(2)}) copy-start(f32[16,64,128]{2,1,0:T(8,128)} %get-tuple-element.91.p1_in.far_u0) | copy-start | bytes 1572868
  148.0 8.0 %copy-start.2 = (f32[16,64,128]{2,1,0:T(8,128)S(1)}, f32[16,64,128]{2,1,0:T(8,128)}, u32[]{:S(2)}) copy-start(f32[16,64,128]{2,1,0:T(8,128)} %get-tuple-element.93.p3_in.far_u2) | copy-start | bytes 1572868
  (5 other events, 3.0 us)

commit v7 on v6

--- a/solution.py
+++ b/solution.py
@@ -13,7 +13,7 @@
 HBM = pl.BlockSpec(memory_space=pltpu.HBM)
 SMEM = pl.BlockSpec(memory_space=pltpu.SMEM)
 NT = (((1,), (1,)), ((), ()))
-CHUNK = 32
+CHUNK = 64
 GROUP = 16
 LIMIT = 14 << 20
 WIDE = 60 << 20
@@ -275,16 +275,32 @@
     return (jnp.zeros((8, 128), F32),) * n
 
 
-def assemble_kernel(
+def three_parts(folds):
+    half, bn = folds[0].shape[0] * 2, folds[0].shape[1] // 2
+    row_id = iota((half, bn), 0)
+    col_id = iota((half, bn), 1)
+    kept = (col_id >= half) | (row_id > col_id)
+    moved = (col_id < half) & (row_id < col_id)
+    wholes = []
+    for both in folds:
+        rows = jnp.concatenate([both[:, :bn], both[:, bn:]], axis=0)
+        second = jnp.where(moved, rows, 0.0)[:, :half]
+        second = jnp.concatenate([jnp.zeros((half, half), F32), second], axis=1)
+        wholes.append(jnp.concatenate([jnp.where(kept, rows, 0.0), second], axis=0))
+    wholes = [w + w.T for w in wholes]
+    pairs = [split(w) for w in wholes]
+    return [jnp.concatenate([high, low, high], axis=1) for high, low in pairs]
+
+
+def lead_kernel(
     tags, picked, placed, payload, loads_in, field_in, inverse_in, gains_in, p0_in, p1_in, p2_in, p3_in,
-    image, blocks, after, s0, s1, s2, s3, field, inverse, gains, packed, p0, p1, p2, p3, sems,
+    image, folded_blocks, s0, s1, field, inverse, gains, packed, p0, p1, p2, p3, sems,
 ):
     patch_dev, bn, _ = image.shape
-    half, quarter = bn // 2, bn // 4
+    quarter = bn // 4
     banks = packed.shape[0]
-    slots = tags.shape[0]
     products = ((p0_in, p0), (p1_in, p1), (p2_in, p2), (p3_in, p3))
-    pairs = ((loads_in, image), (field_in, field), *products, (inverse_in, inverse), (gains_in, gains))
+    pairs = ((loads_in, image), *products, (field_in, field), (inverse_in, inverse), (gains_in, gains))
     fetches = [pltpu.make_async_copy(src, dst, sems.at[i]) for i, (src, dst) in enumerate(pairs)]
     for copy in fetches:
         copy.start()
@@ -297,48 +313,56 @@
             packed[bank, patch] = packed[bank, patch] + payload[pl.ds(pl.multiple_of(i * quarter, quarter), quarter), :]
         return carry
 
-    lax.fori_loop(0, slots // banks, add, 0, unroll=2)
-    fetches[0].wait()
-    fetches[1].wait()
-    row_id = iota((half, bn), 0)
-    col_id = iota((half, bn), 1)
-    kept = (col_id >= half) | (row_id > col_id)
-    moved = (col_id < half) & (row_id < col_id)
+    lax.fori_loop(0, tags.shape[0] // banks, add, 0, unroll=4)
+
+    def join(p, carry):
+        both = packed[0, p]
+        for bank in range(1, banks):
+            both = both + packed[bank, p]
+        folded_blocks[p] = both
+        return carry
+
+    lax.fori_loop(0, patch_dev, join, 0, unroll=4)
+    for copy in fetches[:6]:
+        copy.wait()
+    take_values(placed, (p0, p1, p2, p3), image)
+    count = s0.shape[0]
+    for which, send in enumerate((s0, s1)):
+        for first in range(0, count, GROUP):
+            group = [which * count + first + g for g in range(min(GROUP, count - first))]
+            patches = [picked[i] for i in group]
+            threes = three_parts([folded_blocks[p] for p in patches])
+            values = [dot(three, stacked(field[p])) for p, three in zip(patches, threes)]
+            if which == 0 and first == 0:
+                fetches[6].wait()
+                fetches[7].wait()
+            for i, p, product in zip(group, patches, values):
+                send[i - which * count] = gains[i] * (inverse[p] * (image[p] + product))
+
+
+def assemble_kernel(picked, folded_blocks, start, field, inverse, gains, image, blocks, after, s2, s3):
+    patch_dev = start.shape[0]
 
     def build(j, carry):
         group = [j * GROUP + g for g in range(GROUP)]
-        wholes = []
-        for p in group:
-            both = packed[0, p]
-            for bank in range(1, banks):
-                both = both + packed[bank, p]
-            rows = jnp.concatenate([both[:, :bn], both[:, bn:]], axis=0)
-            second = jnp.where(moved, rows, 0.0)[:, :half]
-            second = jnp.concatenate([jnp.zeros((half, half), F32), second], axis=1)
-            wholes.append(jnp.concatenate([jnp.where(kept, rows, 0.0), second], axis=0))
-        wholes = [w + w.T for w in wholes]
-        threes = []
-        for w in wholes:
-            high, low = split(w)
-            threes.append(jnp.concatenate([high, low, high], axis=1))
-        for p, three in zip(group, threes):
+        threes = three_parts([folded_blocks[p] for p in group])
+        products = [dot(three, stacked(field[p])) for p, three in zip(group, threes)]
+        for p, three, product in zip(group, threes, products):
             blocks[p] = three
-        products = [dot(three, stacked(field[p])) for p, three in zip(group, threes)]
-        for p, product in zip(group, products):
-            image[p] = image[p] + product
+            here = start[p] + product
+            image[p] = here
+            after[p] = inverse[p] * here
         return carry
 
     lax.fori_loop(0, patch_dev // GROUP, build, 0)
-    for copy in fetches[2:]:
-        copy.wait()
-    take_values(placed, (p0, p1, p2, p3), image)
-
-    def finish(p, carry):
-        after[p] = inverse[p] * image[p]
-        return carry
-
-    lax.fori_loop(0, patch_dev, finish, 0, unroll=2)
-    send_values(picked, gains, after, (s0, s1, s2, s3))
+    count = s2.shape[0]
+    for which, send in ((2, s2), (3, s3)):
+
+        def one(k, carry):
+            send[k] = gains[which * count + k] * after[picked[which * count + k]]
+            return carry
+
+        lax.fori_loop(0, count, one, 0, unroll=4)
 
 
 def times_all(blocks, field, base, result):
@@ -575,17 +599,20 @@
     )
     edges = call(edges_kernel, "edges", (*rows, g0, g1, g2, g3), (buf, buf, buf, buf), limit=WIDE)
     far_u1, far_u3 = edges[1], edges[3]
-    image, blocks, after, *rest = call(
-        assemble_kernel, "assemble",
+    start, folded_blocks, s0, s1, field, inverse, gains = call(
+        lead_kernel, "lead",
         (tags, picked, placed, payload, loads, field, inverse, gains, *edges),
-        (vec, struct(patch_dev, bn, 3 * bn, dtype=BF16), vec, buf, buf, buf, buf,
-         vec, vec, struct(4 * count, bn, cases)),
+        (vec, struct(patch_dev, bn // 4, 128), buf, buf, vec, vec, struct(4 * count, bn, cases)),
         (pltpu.VMEM((4, patch_dev + 1, bn // 4, 128), F32), *[pltpu.VMEM((count, bn, cases), F32)] * 4,
          pltpu.SemaphoreType.DMA((8,))),
         far=(4, 5, 6, 7, 8, 9, 10, 11),
     )
-    *sends, field, inverse, gains = rest
-    got = exchange(*sends)
+    got0, got1 = onward(s0, "sector", True), back(s1, "sector", True)
+    image, blocks, after, s2, s3 = call(
+        assemble_kernel, "assemble", (picked, folded_blocks, start, field, inverse, gains),
+        (vec, struct(patch_dev, bn, 3 * bn, dtype=BF16), vec, buf, buf),
+    )
+    got = (got0, got1, onward(s2, "axial", False), back(s3, "axial", False))
     base, partial = call(first_local_kernel, "first_local", (blocks, after, image, loads, field), (vec, total))
     sums0 = everywhere(partial)
     base, sums0 = lax.optimization_barrier((base, sums0))

time: 178 us -> 176 us (0.989)
  blocking collectives: 35.2 us -> 30.9 us
  Pallas kernels: 53.1 us -> 55.6 us
    all_to_all x2, blocking collectives: 35.2 us -> 30.9 us  [everywhere(): lax.all_to_all(partial, AXES, split_axis=0, concat_axis=0, tiled=True)]
    pallas_call x9 -> x10, Pallas kernels: 34.1 us -> 36.7 us  [call(): pl.pallas_call(kernel, in_specs=[SMEM if ints(a) else HBM if i in far els...]
  transfers between devices with their start and end apart: 19 -> 19, of which waited for: 6 -> 6; matrix products, arithmetic and copies ran while one was open for 2% -> 2% of each run, Pallas kernels for 21% -> 24%
where the time goes in v7:
time: 176 us; the launch traced here: 175 us
  Pallas kernels  55.6 us (32%)
  starting transfers between devices  43.1 us (24%)
  waiting for transfers between devices  38.4 us (22%)
  blocking collectives  30.9 us (18%)
  local copies, waits for them, and re-layouts  3.4 us (2%)
  other arithmetic  2.37 us (1%)
    pallas_call x10, Pallas kernels, call(): pl.pallas_call(kernel, in_specs=[SMEM if ints(a) else HBM if i in far els...  36.7 us
    all_to_all x2, blocking collectives, everywhere(): lax.all_to_all(partial, AXES, split_axis=0, concat_axis=0, tiled=True)  30.9 us
    ppermute x9, starting transfers between devices, onward(): lax.ppermute(value, axis, [(i, (i + 1) % n) for i in range(n) if wrap or...  20.6 us
    ppermute x9, waiting for transfers between devices, onward(): lax.ppermute(value, axis, [(i, (i + 1) % n) for i in range(n) if wrap or...  19.3 us
    ppermute x8, starting transfers between devices, back(): lax.ppermute(value, axis, [((i + 1) % n, i) for i in range(n) if wrap or...  15.1 us
    pallas_call x1, Pallas kernels, pack_call(): pl.pallas_call(functools.partial(pack_kernel, slots_each), grid=(elems //...  10.6 us
    ppermute x8, waiting for transfers between devices, back(): lax.ppermute(value, axis, [((i + 1) % n, i) for i in range(n) if wrap or...  10.1 us
    all_to_all x2, waiting for transfers between devices, everywhere(): lax.all_to_all(partial, AXES, split_axis=0, concat_axis=0, tiled=True)  8.9 us
  transfers between devices with their start and end apart: 19, of which 6 were waited for; matrix products, arithmetic and copies ran while one was open for 2% of the time, Pallas kernels for 24%

profile of v7, /device:TPU:0, one launch (start us, length us, event | category | flops | bytes accessed | tf_op | source)
XLA Modules:
  0.0 175.2 jit_solution(13775413725640090445)
XLA Ops:
  0.6 3.0 %own.1 = (f32[16,72,128]{2,1,0:T(8,128)}, f32[16,72,128]{2,1,0:T(8,128)}) custom-call(s32[2,2,16]{2,1,0:T(2,128)} %bitcast.32, f32[64,64,128]{2,1,0:T(8,128)} %bitcast.18, f32[2,16,64]{2,1,0:T(8,128)} %conduct.1), custom_call_target="tpu_custom_call" | custom-call | tf_op jit(solution)/shard_map/own/pallas_call | solution.py:179
  3.6 3.1 %collective-permute-start.1 = (f32[16,72,128]{2,1,0:T(8,128)}, f32[16,72,128]{2,1,0:T(8,128)S(1)}, u32[]{:S(2)}, u32[]{:S(2)}) collective-permute-start(f32[16,72,128]{2,1,0:T(8,128)} %get-tuple-element.72), channel_id=1, source_target_pairs={{0,8},{8,16},{16,24},{24,0},{1,9},{9,17},{17,25},{25,1},{2,10},{10... | collective-permute-start | bytes 1769480 | tf_op jit(solution)/shard_map/ppermute | solution.py:534
  8.2 1.6 collective-permute-start
  10.5 10.6 %pack.1 = (f32[4096,128]{1,0:T(8,128)}, f32[256,128]{1,0:T(8,128)}) custom-call(s32[128]{0:T(128)} %bitcast.35, s32[128]{0:T(128)} %patches.1, s32[1]{0:T(128)S(6)} %copy.14.counts, f32[64,64,128]{2,1,0:T(8,128)} %bitcast.27, bf16[128,64,256]{2,1,0:T(8,128)(2,1)} %bitcast.26, s32[64,128]{1,0:T(8,128)} %bitcast.31), custom_call_target="tpu_custom_call" | custom-call | tf_op jit(solution)/shard_map/pack/pallas_call | solution.py:99
  22.9 2.5 %far.2 = f32[16,64,128]{2,1,0:T(8,128)} custom-call(s32[2,2,16]{2,1,0:T(2,128)} %copy-done.17, f32[64,64,128]{2,1,0:T(8,128)} %bitcast.19), custom_call_target="tpu_custom_call" | custom-call | tf_op jit(solution)/shard_map/far/pallas_call | solution.py:191
  25.4 1.8 %collective-permute-start.3 = (f32[16,64,128]{2,1,0:T(8,128)}, f32[16,64,128]{2,1,0:T(8,128)S(1)}, u32[]{:S(2)}, u32[]{:S(2)}) collective-permute-start(f32[16,64,128]{2,1,0:T(8,128)} %far.2), channel_id=1, source_target_pairs={{8,0},{16,8},{24,16},{0,24},{9,1},{17,9},{25,17},{1,25},{10,2},{18... | collective-permute-start | bytes 1572872 | tf_op jit(solution)/shard_map/ppermute | solution.py:539
  27.2 2.8 %all-to-all-start = ((f32[32,8,128]{2,1,0:T(8,128)}), f32[32,8,128]{2,1,0:T(8,128)S(1)}, u32[]{:S(2)}, u32[]{:S(2)}) async-start(f32[32,8,128]{2,1,0:T(8,128)} %bitcast.9), calls=%async_computation | async-start | bytes 262144 | tf_op jit(solution)/shard_map/all_to_all | solution.py:529
  31.0 2.8 %far.3 = f32[16,64,128]{2,1,0:T(8,128)} custom-call(s32[16]{0:T(128)} %convert_reduce_fusion.index, f32[64,64,128]{2,1,0:T(8,128)} %bitcast.20), custom_call_target="tpu_custom_call" | custom-call | tf_op jit(solution)/shard_map/far/pallas_call | solution.py:191
  33.8 6.8 %collective-permute-done.3.g1 = f32[16,64,128]{2,1,0:T(8,128)S(1)} collective-permute-done((f32[16,64,128]{2,1,0:T(8,128)}, f32[16,64,128]{2,1,0:T(8,128)S(1)}, u32[]{:S(2)}, u32[]{:S(2)}) %collective-permute-start.3) | collective-permute-done | bytes 524320 | tf_op jit(solution)/shard_map/ppermute | solution.py:539
  40.6 3.7 %all-to-all-done = f32[32,8,128]{2,1,0:T(8,128)S(1)} async-done(((f32[32,8,128]{2,1,0:T(8,128)}), f32[32,8,128]{2,1,0:T(8,128)S(1)}, u32[]{:S(2)}, u32[]{:S(2)}) %all-to-all-start) | async-done | bytes 131104 | tf_op jit(solution)/shard_map/all_to_all | solution.py:529
  44.3 4.5 %all-to-all-start.1 = ((f32[32,128,128]{2,1,0:T(8,128)}), f32[32,128,128]{2,1,0:T(8,128)S(1)}, u32[]{:S(2)}, u32[]{:S(2)}) async-start(f32[32,128,128]{2,1,0:T(8,128)} %bitcast.28), calls=%async_computation.1 | async-start | bytes 4194304 | tf_op jit(solution)/shard_map/all_to_all | solution.py:529
  53.0 3.8 %diagonal.1 = (f32[64,128]{1,0:T(8,128)}, f32[64,128]{1,0:T(8,128)}, f32[16,128]{1,0:T(8,128)}, f32[16,128]{1,0:T(8,128)}, f32[16,128]{1,0:T(8,128)}, /*index=5*/f32[16,128]{1,0:T(8,128)}) custom-call(s32[256]{0:T(256)} %select_reduce_fusion.tags, s32[64]{0:T(128)} %get-tuple-element.127.picked, f32[256,128]{1,0:T(8,128)} %bitcast.30, ...), custom_call_target="tpu_custom_call" | custom-call | bytes 1434880 | tf_op jit(solution)/shard_map/diagonal/pallas_call | solution.py:515
  56.7 1.8 %collective-permute-start.4 = (f32[16,128]{1,0:T(8,128)}, f32[16,128]{1,0:T(8,128)S(1)}, u32[]{:S(2)}, u32[]{:S(2)}) collective-permute-start(f32[16,128]{1,0:T(8,128)} %get-tuple-element.86), channel_id=1, source_target_pairs={{0,8},{8,16},{16,24},{24,0},{1,9},{9,17},{17,25},{25,1},{2,10},{10... | collective-permute-start | bytes 24584 | tf_op jit(solution)/shard_map/ppermute | solution.py:534
  58.5 2.0 %collective-permute-start.5 = (f32[16,128]{1,0:T(8,128)}, f32[16,128]{1,0:T(8,128)S(1)}, u32[]{:S(2)}, u32[]{:S(2)}) collective-permute-start(f32[16,128]{1,0:T(8,128)} %get-tuple-element.87), channel_id=1, source_target_pairs={{8,0},{16,8},{24,16},{0,24},{9,1},{17,9},{25,17},{1,25},{10,2},{18... | collective-permute-start | bytes 24584 | tf_op jit(solution)/shard_map/ppermute | solution.py:539
  60.6 2.4 %collective-permute-start.6 = (f32[16,128]{1,0:T(8,128)}, f32[16,128]{1,0:T(8,128)S(1)}, u32[]{:S(2)}, u32[]{:S(2)}) collective-permute-start(f32[16,128]{1,0:T(8,128)} %get-tuple-element.88), channel_id=1, source_target_pairs={{0,1},{1,2},{2,3},{3,4},{4,5},{5,6},{6,7},{8,9},{9,10},{10,11},{11... | collective-permute-start | bytes 24584 | tf_op jit(solution)/shard_map/ppermute | solution.py:534
  64.3 5.4 %expand.1 = (f32[64,64,128]{2,1,0:T(8,128)}, f32[64,64,128]{2,1,0:T(8,128)}, f32[64,64,128]{2,1,0:T(8,128)}) custom-call(f32[64,128]{1,0:T(8,128)} %get-tuple-element.81.over, f32[64,128]{1,0:T(8,128)} %get-tuple-element.82.gain_rows, f32[64,64,128]{2,1,0:T(8,128)} %bitcast.21), custom_call_target="tpu_custom_call" | custom-call | bytes 8454144 | tf_op jit(solution)/shard_map/expand/pallas_call | solution.py:515
  69.7 18.0 %collective-permute-done.4.t0 = f32[16,128]{1,0:T(8,128)S(1)} collective-permute-done((f32[16,128]{1,0:T(8,128)}, f32[16,128]{1,0:T(8,128)S(1)}, u32[]{:S(2)}, u32[]{:S(2)}) %collective-permute-start.4) | collective-permute-done | bytes 8224 | tf_op jit(solution)/shard_map/ppermute | solution.py:534
  89.2 3.6 %edges.1 = (f32[16,64,128]{2,1,0:T(8,128)}, f32[16,64,128]{2,1,0:T(8,128)}, f32[16,64,128]{2,1,0:T(8,128)}, f32[16,64,128]{2,1,0:T(8,128)}) custom-call(f32[16,128]{1,0:T(8,128)} %copy-done.11, f32[16,128]{1,0:T(8,128)} %copy-done.12, f32[16,128]{1,0:T(8,128)} %copy-done.13, f32[16,128]{1,0:T(8,128)} %copy-done.14, f32[16,72,128]{2,1,0:T(8,128)} %copy-done.6, ...), custom_call_target="tpu_custom_call" | custom-call | bytes 4358144 | tf_op jit(solution)/shard_map/edges/pallas_call | solution.py:515
  92.8 5.2 %all-to-all-done.1 = f32[32,128,128]{2,1,0:T(8,128)S(1)} async-done(((f32[32,128,128]{2,1,0:T(8,128)}), f32[32,128,128]{2,1,0:T(8,128)S(1)}, u32[]{:S(2)}, u32[]{:S(2)}) %all-to-all-start.1) | async-done | bytes 2097184 | tf_op jit(solution)/shard_map/all_to_all | solution.py:529
  98.0 5.7 %lead.1 = (f32[64,64,128]{2,1,0:T(8,128)S(1)}, f32[64,16,128]{2,1,0:T(8,128)S(1)}, f32[16,64,128]{2,1,0:T(8,128)S(1)}, f32[16,64,128]{2,1,0:T(8,128)S(1)}, f32[6...) custom-call(s32[256]{0:T(256)S(1)} %copy-done.4, s32[64]{0:T(128)S(1)} %copy-done.3, ...), custom_call_target="tpu_custom_call" | custom-call | bytes 22545920 | tf_op jit(solution)/shard_map/lead/pallas_call | solution.py:515
  103.7 5.8 %collective-permute-start.9 = (f32[16,64,128]{2,1,0:T(8,128)S(1)}, f32[16,64,128]{2,1,0:T(8,128)S(1)}, u32[]{:S(2)}, u32[]{:S(2)}) collective-permute-start(f32[16,64,128]{2,1,0:T(8,128)S(1)} %get-tuple-element.107), channel_id=1, source_target_pairs={{0,8},{8,16},{16,24},{24,0},{1,9},{9,17},{17,25},{25,1},{2,10},{10... | collective-permute-start | bytes 1572872 | tf_op jit(solution)/shard_map/ppermute | solution.py:534
  109.5 4.1 %assemble.1 = (f32[64,64,128]{2,1,0:T(8,128)S(1)}, bf16[64,64,192]{2,1,0:T(8,128)(2,1)S(1)}, f32[64,64,128]{2,1,0:T(8,128)S(1)}, f32[16,64,128]{2,1,0:T(8,128)S(1)}, f32[16,64,128]{2,1,0:T(8,128)S(1)}) custom-call(s32[64]{0:T(128)S(1)} %copy-done.3, f32[64,16,128]{2,1,0:T(8,128)S(1)} %get-tuple-element.96.folded_blocks, ...), custom_call_target="tpu_custom_call" | custom-call | bytes 15728896 | tf_op jit(solution)/shard_map/assemble/pallas_call | solution.py:515
  116.2 2.3 %first_local.1 = (f32[64,64,128]{2,1,0:T(8,128)S(1)}, f32[32,8,128]{2,1,0:T(8,128)S(1)}) custom-call(bf16[64,64,192]{2,1,0:T(8,128)(2,1)S(1)} %get-tuple-element.101.blocks, f32[64,64,128]{2,1,0:T(8,128)S(1)} %get-tuple-element.102.after, f32[64,64,128]{2,1,0:T(8,128)S(1)} %get-tuple-element.103.image, f32[64,64,128]{2,1,0:T(8,128)S(1)} %bitcast.23, ...), custom_call_target="tpu_custom_call" | custom-call | bytes 12189696 | tf_op jit(solution)/shard_map/first_local/pallas_call | solution.py:515
  118.5 15.7 %all_to_all.20.sums.sums0 = f32[32,8,128]{2,1,0:T(8,128)S(1)} all-to-all(f32[32,8,128]{2,1,0:T(8,128)S(1)} %get-tuple-element.105), channel_id=1, replica_groups=mesh['sector'=4,'axial'=8] {'sector','axial'}, dimensions={0} | all-to-all | bytes 262144 | tf_op jit(solution)/shard_map/all_to_all | solution.py:529
  134.2 1.5 second.1
  135.7 6.1 %collective-permute-start.13 = (f32[16,64,128]{2,1,0:T(8,128)S(1)}, f32[16,64,128]{2,1,0:T(8,128)S(1)}, u32[]{:S(2)}, u32[]{:S(2)}) collective-permute-start(f32[16,64,128]{2,1,0:T(8,128)S(1)} %get-tuple-element.116), channel_id=1, source_target_pairs={{8,0},{16,8},{24,16},{0,24},{9,1},{17,9},{25,17},{1,25},{10,2},{18... | collective-permute-start | bytes 1572872 | tf_op jit(solution)/shard_map/ppermute | solution.py:539
  143.2 3.1 %collective-permute-start.16 = (f32[16,64,128]{2,1,0:T(8,128)S(1)}, f32[16,64,128]{2,1,0:T(8,128)S(1)}, u32[]{:S(2)}, u32[]{:S(2)}) collective-permute-start(f32[16,64,128]{2,1,0:T(8,128)S(1)} %get-tuple-element.122), channel_id=1, source_target_pairs={{0,1},{1,2},{2,3},{3,4},{4,5},{5,6},{6,7},{8,9},{9,10},{10,11},{11... | collective-permute-start | bytes 1572872 | tf_op jit(solution)/shard_map/ppermute | solution.py:534
  146.3 4.6 %first_step.1 = (f32[64,64,128]{2,1,0:T(8,128)S(1)}, f32[64,64,128]{2,1,0:T(8,128)S(1)}, f32[64,64,128]{2,1,0:T(8,128)S(1)}, f32[16,8,128]{2,1,0:T(8,128)S(1)}) custom-call(f32[32,8,128]{2,1,0:T(8,128)S(1)} %all_to_all.20.sums.sums0, bf16[64,64,192]{2,1,0:T(8,128)(2,1)S(1)} %get-tuple-element.101.blocks, f32[64,64,128]{2,1,0:T(8,128)S(1)} %get-tuple-element.112.after, ...), custom_call_target="tpu_custom_call" | custom-call | bytes 20643840 | tf_op jit(solution)/shard_map/first_step/pallas_call | solution.py:515
  150.9 3.3 %collective-permute-done.13.far_q0.g1 = f32[16,64,128]{2,1,0:T(8,128)S(1)} collective-permute-done((f32[16,64,128]{2,1,0:T(8,128)S(1)}, f32[16,64,128]{2,1,0:T(8,128)S(1)}, u32[]{:S(2)}, u32[]{:S(2)}) %collective-permute-start.13) | collective-permute-done | bytes 524320 | tf_op jit(solution)/shard_map/ppermute | solution.py:539
  154.2 1.8 %links.1 = f32[32,16,128]{2,1,0:T(8,128)S(1)} custom-call(f32[32,8,128]{2,1,0:T(8,128)S(1)} %all_to_all.20.sums.sums0, s32[64]{0:T(128)S(1)} %get-tuple-element.126.placed, f32[16,8,128]{2,1,0:T(8,128)S(1)} %get-tuple-element.115.totals, f32[16,64,128]{2,1,0:T(8,128)S(1)} %copy-done.1, f32[16,64,128]{2,1,0:T(8,128)S(1)} %copy-done.2, ...), custom_call_target="tpu_custom_call" | custom-call | bytes 16187648 | tf_op jit(solution)/shard_map/links/pallas_call | solution.py:515
  156.0 15.2 %all_to_all.21.sums1 = f32[32,16,128]{2,1,0:T(8,128)S(1)} all-to-all(f32[32,16,128]{2,1,0:T(8,128)S(1)} %links.1), channel_id=1, replica_groups=mesh['sector'=4,'axial'=8] {'sector','axial'}, dimensions={0} | all-to-all | bytes 524288 | tf_op jit(solution)/shard_map/all_to_all | solution.py:529
  171.2 4.0 %last.1 = (f32[64,64,128]{2,1,0:T(8,128)}, f32[64,64,128]{2,1,0:T(8,128)}) custom-call(f32[32,8,128]{2,1,0:T(8,128)S(1)} %all_to_all.20.sums.sums0, f32[32,16,128]{2,1,0:T(8,128)S(1)} %all_to_all.21.sums1, s32[64]{0:T(128)S(1)} %get-tuple-element.126.placed, f32[16,64,128]{2,1,0:T(8,128)S(1)} %collective-permute-done.15.g0, ...), custom_call_target="tpu_custom_call" | custom-call | bytes 21364992 | tf_op jit(solution)/shard_map/last/pallas_call | solution.py:515
  (64 shorter events, 15.1 us)
Async XLA Ops:
  0.6 7.6 %copy-start.15 = (s32[2,16,2]{1,2,0:T(2,128)S(1)}, s32[2,16,2]{1,2,0:T(2,128)}, u32[]{:S(2)}) copy-start(s32[2,16,2]{1,2,0:T(2,128)} %param.17) | copy-start | bytes 772
  3.6 26.4 %collective-permute-start.1 = (f32[16,72,128]{2,1,0:T(8,128)}, f32[16,72,128]{2,1,0:T(8,128)S(1)}, u32[]{:S(2)}, u32[]{:S(2)}) collective-permute-start(f32[16,72,128]{2,1,0:T(8,128)} %get-tuple-element.72), channel_id=1, source_target_pairs={{0,8},{8,16},{16,24},{24,0},{1,9},{9,17},{17,25},{25,1},{2,10},{10... | collective-permute-start | bytes 1769480 | tf_op jit(solution)/shard_map/ppermute | solution.py:534
  6.7 23.3 %collective-permute-start.2 = (f32[16,72,128]{2,1,0:T(8,128)}, f32[16,72,128]{2,1,0:T(8,128)S(1)}, u32[]{:S(2)}, u32[]{:S(2)}) collective-permute-start(f32[16,72,128]{2,1,0:T(8,128)} %get-tuple-element.73), channel_id=1, source_target_pairs={{0,1},{1,2},{2,3},{3,4},{4,5},{5,6},{6,7},{8,9},{9,10},{10,11},{11... | collective-permute-start | bytes 1769480 | tf_op jit(solution)/shard_map/ppermute | solution.py:534
  8.2 14.1 %collective-permute-start = (s32[2,2,16]{2,1,0:T(2,128)S(1)}, s32[2,2,16]{2,1,0:T(2,128)S(1)}, u32[]{:S(2)}, u32[]{:S(2)}) collective-permute-start(s32[2,2,16]{2,1,0:T(2,128)S(1)} %bitcast.33), channel_id=1, source_target_pairs={{0,8},{8,16},{16,24},{24,0},{1,9},{9,17},{17,25},{25,1},{2,10},{10... | collective-permute-start | bytes 776 | tf_op jit(solution)/shard_map/ppermute | solution.py:534
  25.4 15.2 %collective-permute-start.3 = (f32[16,64,128]{2,1,0:T(8,128)}, f32[16,64,128]{2,1,0:T(8,128)S(1)}, u32[]{:S(2)}, u32[]{:S(2)}) collective-permute-start(f32[16,64,128]{2,1,0:T(8,128)} %far.2), channel_id=1, source_target_pairs={{8,0},{16,8},{24,16},{0,24},{9,1},{17,9},{25,17},{1,25},{10,2},{18... | collective-permute-start | bytes 1572872 | tf_op jit(solution)/shard_map/ppermute | solution.py:539
  27.2 17.1 %all-to-all-start = ((f32[32,8,128]{2,1,0:T(8,128)}), f32[32,8,128]{2,1,0:T(8,128)S(1)}, u32[]{:S(2)}, u32[]{:S(2)}) async-start(f32[32,8,128]{2,1,0:T(8,128)} %bitcast.9), calls=%async_computation | async-start | bytes 262144 | tf_op jit(solution)/shard_map/all_to_all | solution.py:529
  30.0 14.3 %copy-start.6 = (f32[16,72,128]{2,1,0:T(8,128)}, f32[16,72,128]{2,1,0:T(8,128)S(1)}, u32[]{:S(2)}) copy-start(f32[16,72,128]{2,1,0:T(8,128)S(1)} %collective-permute-done.1.g0) | copy-start | bytes 1769476
  30.0 14.3 %copy-start.5 = (f32[16,72,128]{2,1,0:T(8,128)}, f32[16,72,128]{2,1,0:T(8,128)S(1)}, u32[]{:S(2)}) copy-start(f32[16,72,128]{2,1,0:T(8,128)S(1)} %collective-permute-done.2.g2) | copy-start | bytes 1769476
  40.6 3.7 %copy-start.8 = (f32[16,64,128]{2,1,0:T(8,128)}, f32[16,64,128]{2,1,0:T(8,128)S(1)}, u32[]{:S(2)}) copy-start(f32[16,64,128]{2,1,0:T(8,128)S(1)} %collective-permute-done.3.g1) | copy-start | bytes 1572868
  44.3 7.2 %copy-start.7 = (f32[32,8,128]{2,1,0:T(8,128)}, f32[32,8,128]{2,1,0:T(8,128)S(1)}, u32[]{:S(2)}) copy-start(f32[32,8,128]{2,1,0:T(8,128)S(1)} %all-to-all-done) | copy-start | bytes 393220
  44.3 5.9 %copy-start.10 = (f32[4096]{0:T(1024)S(1)}, f32[4096]{0:T(1024)}, u32[]{:S(2)}) copy-start(f32[4096]{0:T(1024)} %param.16) | copy-start | bytes 49156
  44.3 8.0 %copy-start.16 = (s32[16]{0:T(128)S(1)}, s32[16]{0:T(128)}, u32[]{:S(2)}) copy-start(s32[16]{0:T(128)} %convert_reduce_fusion.index) | copy-start | bytes 196
  44.3 53.7 %all-to-all-start.1 = ((f32[32,128,128]{2,1,0:T(8,128)}), f32[32,128,128]{2,1,0:T(8,128)S(1)}, u32[]{:S(2)}, u32[]{:S(2)}) async-start(f32[32,128,128]{2,1,0:T(8,128)} %bitcast.28), calls=%async_computation.1 | async-start | bytes 4194304 | tf_op jit(solution)/shard_map/all_to_all | solution.py:529
  48.8 39.0 %collective-permute-start.8 = (f32[16,64,128]{2,1,0:T(8,128)}, f32[16,64,128]{2,1,0:T(8,128)S(1)}, u32[]{:S(2)}, u32[]{:S(2)}) collective-permute-start(f32[16,64,128]{2,1,0:T(8,128)} %far.3), channel_id=1, source_target_pairs={{1,0},{2,1},{3,2},{4,3},{5,4},{6,5},{7,6},{9,8},{10,9},{11,10},{12... | collective-permute-start | bytes 1572872 | tf_op jit(solution)/shard_map/ppermute | solution.py:539
  56.7 31.0 %collective-permute-start.4 = (f32[16,128]{1,0:T(8,128)}, f32[16,128]{1,0:T(8,128)S(1)}, u32[]{:S(2)}, u32[]{:S(2)}) collective-permute-start(f32[16,128]{1,0:T(8,128)} %get-tuple-element.86), channel_id=1, source_target_pairs={{0,8},{8,16},{16,24},{24,0},{1,9},{9,17},{17,25},{25,1},{2,10},{10... | collective-permute-start | bytes 24584 | tf_op jit(solution)/shard_map/ppermute | solution.py:534
  58.5 29.2 %collective-permute-start.5 = (f32[16,128]{1,0:T(8,128)}, f32[16,128]{1,0:T(8,128)S(1)}, u32[]{:S(2)}, u32[]{:S(2)}) collective-permute-start(f32[16,128]{1,0:T(8,128)} %get-tuple-element.87), channel_id=1, source_target_pairs={{8,0},{16,8},{24,16},{0,24},{9,1},{17,9},{25,17},{1,25},{10,2},{18... | collective-permute-start | bytes 24584 | tf_op jit(solution)/shard_map/ppermute | solution.py:539
  60.6 27.2 %collective-permute-start.6 = (f32[16,128]{1,0:T(8,128)}, f32[16,128]{1,0:T(8,128)S(1)}, u32[]{:S(2)}, u32[]{:S(2)}) collective-permute-start(f32[16,128]{1,0:T(8,128)} %get-tuple-element.88), channel_id=1, source_target_pairs={{0,1},{1,2},{2,3},{3,4},{4,5},{5,6},{6,7},{8,9},{9,10},{10,11},{11... | collective-permute-start | bytes 24584 | tf_op jit(solution)/shard_map/ppermute | solution.py:534
  63.0 24.8 %collective-permute-start.7 = (f32[16,128]{1,0:T(8,128)}, f32[16,128]{1,0:T(8,128)S(1)}, u32[]{:S(2)}, u32[]{:S(2)}) collective-permute-start(f32[16,128]{1,0:T(8,128)} %get-tuple-element.89), channel_id=1, source_target_pairs={{1,0},{2,1},{3,2},{4,3},{5,4},{6,5},{7,6},{9,8},{10,9},{11,10},{12... | collective-permute-start | bytes 24584 | tf_op jit(solution)/shard_map/ppermute | solution.py:539
  64.3 33.7 %copy-start.3 = (s32[64]{0:T(128)S(1)}, s32[64]{0:T(128)}, u32[]{:S(2)}) copy-start(s32[64]{0:T(128)} %get-tuple-element.127.picked) | copy-start | bytes 772
  64.3 33.7 %copy-start.4 = (s32[256]{0:T(256)S(1)}, s32[256]{0:T(256)}, u32[]{:S(2)}) copy-start(s32[256]{0:T(256)} %select_reduce_fusion.tags) | copy-start | bytes 3076
  88.4 0.9 copy-start.9
  103.7 30.4 %collective-permute-start.9 = (f32[16,64,128]{2,1,0:T(8,128)S(1)}, f32[16,64,128]{2,1,0:T(8,128)S(1)}, u32[]{:S(2)}, u32[]{:S(2)}) collective-permute-start(f32[16,64,128]{2,1,0:T(8,128)S(1)} %get-tuple-element.107), channel_id=1, source_target_pairs={{0,8},{8,16},{16,24},{24,0},{1,9},{9,17},{17,25},{25,1},{2,10},{10... | collective-permute-start | bytes 1572872 | tf_op jit(solution)/shard_map/ppermute | solution.py:534
  109.5 24.7 %collective-permute-start.10 = (f32[16,64,128]{2,1,0:T(8,128)S(1)}, f32[16,64,128]{2,1,0:T(8,128)S(1)}, u32[]{:S(2)}, u32[]{:S(2)}) collective-permute-start(f32[16,64,128]{2,1,0:T(8,128)S(1)} %get-tuple-element.108), channel_id=1, source_target_pairs={{8,0},{16,8},{24,16},{0,24},{9,1},{17,9},{25,17},{1,25},{10,2},{18... | collective-permute-start | bytes 1572872 | tf_op jit(solution)/shard_map/ppermute | solution.py:539
  109.5 6.7 %copy-start = (f32[4096,128]{1,0:T(8,128)S(1)}, f32[4096,128]{1,0:T(8,128)}, u32[]{:S(2)}) copy-start(f32[4096,128]{1,0:T(8,128)} %param.19) | copy-start | bytes 6291460
  113.6 20.6 %collective-permute-start.11 = (f32[16,64,128]{2,1,0:T(8,128)S(1)}, f32[16,64,128]{2,1,0:T(8,128)S(1)}, u32[]{:S(2)}, u32[]{:S(2)}) collective-permute-start(f32[16,64,128]{2,1,0:T(8,128)S(1)} %get-tuple-element.109), channel_id=1, source_target_pairs={{0,1},{1,2},{2,3},{3,4},{4,5},{5,6},{6,7},{8,9},{9,10},{10,11},{11... | collective-permute-start | bytes 1572872 | tf_op jit(solution)/shard_map/ppermute | solution.py:534
  114.9 19.2 %collective-permute-start.12 = (f32[16,64,128]{2,1,0:T(8,128)S(1)}, f32[16,64,128]{2,1,0:T(8,128)S(1)}, u32[]{:S(2)}, u32[]{:S(2)}) collective-permute-start(f32[16,64,128]{2,1,0:T(8,128)S(1)} %get-tuple-element.110), channel_id=1, source_target_pairs={{1,0},{2,1},{3,2},{4,3},{5,4},{6,5},{7,6},{9,8},{10,9},{11,10},{12... | collective-permute-start | bytes 1572872 | tf_op jit(solution)/shard_map/ppermute | solution.py:539
  135.7 18.6 %collective-permute-start.13 = (f32[16,64,128]{2,1,0:T(8,128)S(1)}, f32[16,64,128]{2,1,0:T(8,128)S(1)}, u32[]{:S(2)}, u32[]{:S(2)}) collective-permute-start(f32[16,64,128]{2,1,0:T(8,128)S(1)} %get-tuple-element.116), channel_id=1, source_target_pairs={{8,0},{16,8},{24,16},{0,24},{9,1},{17,9},{25,17},{1,25},{10,2},{18... | collective-permute-start | bytes 1572872 | tf_op jit(solution)/shard_map/ppermute | solution.py:539
  141.8 12.4 %collective-permute-start.14 = (f32[16,64,128]{2,1,0:T(8,128)S(1)}, f32[16,64,128]{2,1,0:T(8,128)S(1)}, u32[]{:S(2)}, u32[]{:S(2)}) collective-permute-start(f32[16,64,128]{2,1,0:T(8,128)S(1)} %get-tuple-element.117), channel_id=1, source_target_pairs={{1,0},{2,1},{3,2},{4,3},{5,4},{6,5},{7,6},{9,8},{10,9},{11,10},{12... | collective-permute-start | bytes 1572872 | tf_op jit(solution)/shard_map/ppermute | solution.py:539
  143.1 28.1 %collective-permute-start.15 = (f32[16,64,128]{2,1,0:T(8,128)S(1)}, f32[16,64,128]{2,1,0:T(8,128)S(1)}, u32[]{:S(2)}, u32[]{:S(2)}) collective-permute-start(f32[16,64,128]{2,1,0:T(8,128)S(1)} %get-tuple-element.121), channel_id=1, source_target_pairs={{0,8},{8,16},{16,24},{24,0},{1,9},{9,17},{17,25},{25,1},{2,10},{10... | collective-permute-start | bytes 1572872 | tf_op jit(solution)/shard_map/ppermute | solution.py:534
  143.2 28.1 %collective-permute-start.16 = (f32[16,64,128]{2,1,0:T(8,128)S(1)}, f32[16,64,128]{2,1,0:T(8,128)S(1)}, u32[]{:S(2)}, u32[]{:S(2)}) collective-permute-start(f32[16,64,128]{2,1,0:T(8,128)S(1)} %get-tuple-element.122), channel_id=1, source_target_pairs={{0,1},{1,2},{2,3},{3,4},{4,5},{5,6},{6,7},{8,9},{9,10},{10,11},{11... | collective-permute-start | bytes 1572872 | tf_op jit(solution)/shard_map/ppermute | solution.py:534
  146.2 8.0 %copy-start.1 = (f32[16,64,128]{2,1,0:T(8,128)S(1)}, f32[16,64,128]{2,1,0:T(8,128)}, u32[]{:S(2)}) copy-start(f32[16,64,128]{2,1,0:T(8,128)} %get-tuple-element.93.p1_in.far_u0) | copy-start | bytes 1572868
  146.2 8.0 %copy-start.2 = (f32[16,64,128]{2,1,0:T(8,128)S(1)}, f32[16,64,128]{2,1,0:T(8,128)}, u32[]{:S(2)}) copy-start(f32[16,64,128]{2,1,0:T(8,128)} %get-tuple-element.95.p3_in.far_u2) | copy-start | bytes 1572868
  (5 other events, 3.0 us)

commit v8 on v7

--- a/solution.py
+++ b/solution.py
@@ -313,7 +313,7 @@
             packed[bank, patch] = packed[bank, patch] + payload[pl.ds(pl.multiple_of(i * quarter, quarter), quarter), :]
         return carry
 
-    lax.fori_loop(0, tags.shape[0] // banks, add, 0, unroll=4)
+    lax.fori_loop(0, tags.shape[0] // banks, add, 0, unroll=8)
 
     def join(p, carry):
         both = packed[0, p]
@@ -603,7 +603,7 @@
         lead_kernel, "lead",
         (tags, picked, placed, payload, loads, field, inverse, gains, *edges),
         (vec, struct(patch_dev, bn // 4, 128), buf, buf, vec, vec, struct(4 * count, bn, cases)),
-        (pltpu.VMEM((4, patch_dev + 1, bn // 4, 128), F32), *[pltpu.VMEM((count, bn, cases), F32)] * 4,
+        (pltpu.VMEM((2, patch_dev + 1, bn // 4, 128), F32), *[pltpu.VMEM((count, bn, cases), F32)] * 4,
          pltpu.SemaphoreType.DMA((8,))),
         far=(4, 5, 6, 7, 8, 9, 10, 11),
     )

time: 176 us -> 176 us (level)
  no operation moved by 1% of the time
where the time goes in v8:
time: 176 us; the launch traced here: 175 us
  Pallas kernels  55.4 us (31%)
  starting transfers between devices  43.4 us (25%)
  waiting for transfers between devices  38.2 us (22%)
  blocking collectives  30.9 us (18%)
  local copies, waits for them, and re-layouts  3.4 us (2%)
  other arithmetic  2.37 us (1%)
    pallas_call x10, Pallas kernels, call(): pl.pallas_call(kernel, in_specs=[SMEM if ints(a) else HBM if i in far els...  36.5 us
    all_to_all x2, blocking collectives, everywhere(): lax.all_to_all(partial, AXES, split_axis=0, concat_axis=0, tiled=True)  30.9 us
    ppermute x9, starting transfers between devices, onward(): lax.ppermute(value, axis, [(i, (i + 1) % n) for i in range(n) if wrap or...  20.6 us
    ppermute x9, waiting for transfers between devices, onward(): lax.ppermute(value, axis, [(i, (i + 1) % n) for i in range(n) if wrap or...  19.2 us
    ppermute x8, starting transfers between devices, back(): lax.ppermute(value, axis, [((i + 1) % n, i) for i in range(n) if wrap or...  15.4 us
    pallas_call x1, Pallas kernels, pack_call(): pl.pallas_call(functools.partial(pack_kernel, slots_each), grid=(elems //...  10.6 us
    ppermute x8, waiting for transfers between devices, back(): lax.ppermute(value, axis, [((i + 1) % n, i) for i in range(n) if wrap or...  10.2 us
    all_to_all x2, waiting for transfers between devices, everywhere(): lax.all_to_all(partial, AXES, split_axis=0, concat_axis=0, tiled=True)  8.88 us
  transfers between devices with their start and end apart: 19, of which 6 were waited for; matrix products, arithmetic and copies ran while one was open for 2% of the time, Pallas kernels for 24%

profile of v8, /device:TPU:0, one launch (start us, length us, event | category | flops | bytes accessed | tf_op | source)
XLA Modules:
  0.0 175.2 jit_solution(12028448821572456590)
XLA Ops:
  0.6 3.0 %own.1 = (f32[16,72,128]{2,1,0:T(8,128)}, f32[16,72,128]{2,1,0:T(8,128)}) custom-call(s32[2,2,16]{2,1,0:T(2,128)} %bitcast.32, f32[64,64,128]{2,1,0:T(8,128)} %bitcast.18, f32[2,16,64]{2,1,0:T(8,128)} %conduct.1), custom_call_target="tpu_custom_call" | custom-call | tf_op jit(solution)/shard_map/own/pallas_call | solution.py:179
  3.6 3.1 %collective-permute-start.1 = (f32[16,72,128]{2,1,0:T(8,128)}, f32[16,72,128]{2,1,0:T(8,128)S(1)}, u32[]{:S(2)}, u32[]{:S(2)}) collective-permute-start(f32[16,72,128]{2,1,0:T(8,128)} %get-tuple-element.72), channel_id=1, source_target_pairs={{0,8},{8,16},{16,24},{24,0},{1,9},{9,17},{17,25},{25,1},{2,10},{10... | collective-permute-start | bytes 1769480 | tf_op jit(solution)/shard_map/ppermute | solution.py:534
  8.2 1.6 collective-permute-start
  10.5 10.6 %pack.1 = (f32[4096,128]{1,0:T(8,128)}, f32[256,128]{1,0:T(8,128)}) custom-call(s32[128]{0:T(128)} %bitcast.35, s32[128]{0:T(128)} %patches.1, s32[1]{0:T(128)S(6)} %copy.14.counts, f32[64,64,128]{2,1,0:T(8,128)} %bitcast.27, bf16[128,64,256]{2,1,0:T(8,128)(2,1)} %bitcast.26, s32[64,128]{1,0:T(8,128)} %bitcast.31), custom_call_target="tpu_custom_call" | custom-call | tf_op jit(solution)/shard_map/pack/pallas_call | solution.py:99
  22.9 2.5 %far.2 = f32[16,64,128]{2,1,0:T(8,128)} custom-call(s32[2,2,16]{2,1,0:T(2,128)} %copy-done.17, f32[64,64,128]{2,1,0:T(8,128)} %bitcast.19), custom_call_target="tpu_custom_call" | custom-call | tf_op jit(solution)/shard_map/far/pallas_call | solution.py:191
  25.4 1.8 %collective-permute-start.3 = (f32[16,64,128]{2,1,0:T(8,128)}, f32[16,64,128]{2,1,0:T(8,128)S(1)}, u32[]{:S(2)}, u32[]{:S(2)}) collective-permute-start(f32[16,64,128]{2,1,0:T(8,128)} %far.2), channel_id=1, source_target_pairs={{8,0},{16,8},{24,16},{0,24},{9,1},{17,9},{25,17},{1,25},{10,2},{18... | collective-permute-start | bytes 1572872 | tf_op jit(solution)/shard_map/ppermute | solution.py:539
  27.2 2.8 %all-to-all-start = ((f32[32,8,128]{2,1,0:T(8,128)}), f32[32,8,128]{2,1,0:T(8,128)S(1)}, u32[]{:S(2)}, u32[]{:S(2)}) async-start(f32[32,8,128]{2,1,0:T(8,128)} %bitcast.9), calls=%async_computation | async-start | bytes 262144 | tf_op jit(solution)/shard_map/all_to_all | solution.py:529
  31.0 2.8 %far.3 = f32[16,64,128]{2,1,0:T(8,128)} custom-call(s32[16]{0:T(128)} %convert_reduce_fusion.index, f32[64,64,128]{2,1,0:T(8,128)} %bitcast.20), custom_call_target="tpu_custom_call" | custom-call | tf_op jit(solution)/shard_map/far/pallas_call | solution.py:191
  33.8 6.8 %collective-permute-done.3.g1 = f32[16,64,128]{2,1,0:T(8,128)S(1)} collective-permute-done((f32[16,64,128]{2,1,0:T(8,128)}, f32[16,64,128]{2,1,0:T(8,128)S(1)}, u32[]{:S(2)}, u32[]{:S(2)}) %collective-permute-start.3) | collective-permute-done | bytes 524320 | tf_op jit(solution)/shard_map/ppermute | solution.py:539
  40.6 3.7 %all-to-all-done = f32[32,8,128]{2,1,0:T(8,128)S(1)} async-done(((f32[32,8,128]{2,1,0:T(8,128)}), f32[32,8,128]{2,1,0:T(8,128)S(1)}, u32[]{:S(2)}, u32[]{:S(2)}) %all-to-all-start) | async-done | bytes 131104 | tf_op jit(solution)/shard_map/all_to_all | solution.py:529
  44.3 4.6 %all-to-all-start.1 = ((f32[32,128,128]{2,1,0:T(8,128)}), f32[32,128,128]{2,1,0:T(8,128)S(1)}, u32[]{:S(2)}, u32[]{:S(2)}) async-start(f32[32,128,128]{2,1,0:T(8,128)} %bitcast.28), calls=%async_computation.1 | async-start | bytes 4194304 | tf_op jit(solution)/shard_map/all_to_all | solution.py:529
  53.0 3.6 %diagonal.1 = (f32[64,128]{1,0:T(8,128)}, f32[64,128]{1,0:T(8,128)}, f32[16,128]{1,0:T(8,128)}, f32[16,128]{1,0:T(8,128)}, f32[16,128]{1,0:T(8,128)}, /*index=5*/f32[16,128]{1,0:T(8,128)}) custom-call(s32[256]{0:T(256)} %select_reduce_fusion.tags, s32[64]{0:T(128)} %get-tuple-element.127.picked, f32[256,128]{1,0:T(8,128)} %bitcast.30, ...), custom_call_target="tpu_custom_call" | custom-call | bytes 1434880 | tf_op jit(solution)/shard_map/diagonal/pallas_call | solution.py:515
  56.5 1.5 collective-permute-start.4
  58.1 2.3 %collective-permute-start.5 = (f32[16,128]{1,0:T(8,128)}, f32[16,128]{1,0:T(8,128)S(1)}, u32[]{:S(2)}, u32[]{:S(2)}) collective-permute-start(f32[16,128]{1,0:T(8,128)} %get-tuple-element.87), channel_id=1, source_target_pairs={{8,0},{16,8},{24,16},{0,24},{9,1},{17,9},{25,17},{1,25},{10,2},{18... | collective-permute-start | bytes 24584 | tf_op jit(solution)/shard_map/ppermute | solution.py:539
  60.4 2.7 %collective-permute-start.6 = (f32[16,128]{1,0:T(8,128)}, f32[16,128]{1,0:T(8,128)S(1)}, u32[]{:S(2)}, u32[]{:S(2)}) collective-permute-start(f32[16,128]{1,0:T(8,128)} %get-tuple-element.88), channel_id=1, source_target_pairs={{0,1},{1,2},{2,3},{3,4},{4,5},{5,6},{6,7},{8,9},{9,10},{10,11},{11... | collective-permute-start | bytes 24584 | tf_op jit(solution)/shard_map/ppermute | solution.py:534
  64.4 5.4 %expand.1 = (f32[64,64,128]{2,1,0:T(8,128)}, f32[64,64,128]{2,1,0:T(8,128)}, f32[64,64,128]{2,1,0:T(8,128)}) custom-call(f32[64,128]{1,0:T(8,128)} %get-tuple-element.81.over, f32[64,128]{1,0:T(8,128)} %get-tuple-element.82.gain_rows, f32[64,64,128]{2,1,0:T(8,128)} %bitcast.21), custom_call_target="tpu_custom_call" | custom-call | bytes 8454144 | tf_op jit(solution)/shard_map/expand/pallas_call | solution.py:515
  69.8 17.9 %collective-permute-done.4.t0 = f32[16,128]{1,0:T(8,128)S(1)} collective-permute-done((f32[16,128]{1,0:T(8,128)}, f32[16,128]{1,0:T(8,128)S(1)}, u32[]{:S(2)}, u32[]{:S(2)}) %collective-permute-start.4) | collective-permute-done | bytes 8224 | tf_op jit(solution)/shard_map/ppermute | solution.py:534
  89.2 3.6 %edges.1 = (f32[16,64,128]{2,1,0:T(8,128)}, f32[16,64,128]{2,1,0:T(8,128)}, f32[16,64,128]{2,1,0:T(8,128)}, f32[16,64,128]{2,1,0:T(8,128)}) custom-call(f32[16,128]{1,0:T(8,128)} %copy-done.11, f32[16,128]{1,0:T(8,128)} %copy-done.12, f32[16,128]{1,0:T(8,128)} %copy-done.13, f32[16,128]{1,0:T(8,128)} %copy-done.14, f32[16,72,128]{2,1,0:T(8,128)} %copy-done.6, ...), custom_call_target="tpu_custom_call" | custom-call | bytes 4358144 | tf_op jit(solution)/shard_map/edges/pallas_call | solution.py:515
  92.8 5.2 %all-to-all-done.1 = f32[32,128,128]{2,1,0:T(8,128)S(1)} async-done(((f32[32,128,128]{2,1,0:T(8,128)}), f32[32,128,128]{2,1,0:T(8,128)S(1)}, u32[]{:S(2)}, u32[]{:S(2)}) %all-to-all-start.1) | async-done | bytes 2097184 | tf_op jit(solution)/shard_map/all_to_all | solution.py:529
  98.0 5.7 %lead.1 = (f32[64,64,128]{2,1,0:T(8,128)S(1)}, f32[64,16,128]{2,1,0:T(8,128)S(1)}, f32[16,64,128]{2,1,0:T(8,128)S(1)}, f32[16,64,128]{2,1,0:T(8,128)S(1)}, f32[6...) custom-call(s32[256]{0:T(256)S(1)} %copy-done.4, s32[64]{0:T(128)S(1)} %copy-done.3, ...), custom_call_target="tpu_custom_call" | custom-call | bytes 22545920 | tf_op jit(solution)/shard_map/lead/pallas_call | solution.py:515
  103.7 5.8 %collective-permute-start.9 = (f32[16,64,128]{2,1,0:T(8,128)S(1)}, f32[16,64,128]{2,1,0:T(8,128)S(1)}, u32[]{:S(2)}, u32[]{:S(2)}) collective-permute-start(f32[16,64,128]{2,1,0:T(8,128)S(1)} %get-tuple-element.107), channel_id=1, source_target_pairs={{0,8},{8,16},{16,24},{24,0},{1,9},{9,17},{17,25},{25,1},{2,10},{10... | collective-permute-start | bytes 1572872 | tf_op jit(solution)/shard_map/ppermute | solution.py:534
  109.5 4.1 %assemble.1 = (f32[64,64,128]{2,1,0:T(8,128)S(1)}, bf16[64,64,192]{2,1,0:T(8,128)(2,1)S(1)}, f32[64,64,128]{2,1,0:T(8,128)S(1)}, f32[16,64,128]{2,1,0:T(8,128)S(1)}, f32[16,64,128]{2,1,0:T(8,128)S(1)}) custom-call(s32[64]{0:T(128)S(1)} %copy-done.3, f32[64,16,128]{2,1,0:T(8,128)S(1)} %get-tuple-element.96.folded_blocks, ...), custom_call_target="tpu_custom_call" | custom-call | bytes 15728896 | tf_op jit(solution)/shard_map/assemble/pallas_call | solution.py:515
  116.2 2.3 %first_local.1 = (f32[64,64,128]{2,1,0:T(8,128)S(1)}, f32[32,8,128]{2,1,0:T(8,128)S(1)}) custom-call(bf16[64,64,192]{2,1,0:T(8,128)(2,1)S(1)} %get-tuple-element.101.blocks, f32[64,64,128]{2,1,0:T(8,128)S(1)} %get-tuple-element.102.after, f32[64,64,128]{2,1,0:T(8,128)S(1)} %get-tuple-element.103.image, f32[64,64,128]{2,1,0:T(8,128)S(1)} %bitcast.23, ...), custom_call_target="tpu_custom_call" | custom-call | bytes 12189696 | tf_op jit(solution)/shard_map/first_local/pallas_call | solution.py:515
  118.5 15.7 %all_to_all.20.sums.sums0 = f32[32,8,128]{2,1,0:T(8,128)S(1)} all-to-all(f32[32,8,128]{2,1,0:T(8,128)S(1)} %get-tuple-element.105), channel_id=1, replica_groups=mesh['sector'=4,'axial'=8] {'sector','axial'}, dimensions={0} | all-to-all | bytes 262144 | tf_op jit(solution)/shard_map/all_to_all | solution.py:529
  134.2 1.5 second.1
  135.7 6.1 %collective-permute-start.13 = (f32[16,64,128]{2,1,0:T(8,128)S(1)}, f32[16,64,128]{2,1,0:T(8,128)S(1)}, u32[]{:S(2)}, u32[]{:S(2)}) collective-permute-start(f32[16,64,128]{2,1,0:T(8,128)S(1)} %get-tuple-element.116), channel_id=1, source_target_pairs={{8,0},{16,8},{24,16},{0,24},{9,1},{17,9},{25,17},{1,25},{10,2},{18... | collective-permute-start | bytes 1572872 | tf_op jit(solution)/shard_map/ppermute | solution.py:539
  143.2 3.1 %collective-permute-start.16 = (f32[16,64,128]{2,1,0:T(8,128)S(1)}, f32[16,64,128]{2,1,0:T(8,128)S(1)}, u32[]{:S(2)}, u32[]{:S(2)}) collective-permute-start(f32[16,64,128]{2,1,0:T(8,128)S(1)} %get-tuple-element.122), channel_id=1, source_target_pairs={{0,1},{1,2},{2,3},{3,4},{4,5},{5,6},{6,7},{8,9},{9,10},{10,11},{11... | collective-permute-start | bytes 1572872 | tf_op jit(solution)/shard_map/ppermute | solution.py:534
  146.3 4.6 %first_step.1 = (f32[64,64,128]{2,1,0:T(8,128)S(1)}, f32[64,64,128]{2,1,0:T(8,128)S(1)}, f32[64,64,128]{2,1,0:T(8,128)S(1)}, f32[16,8,128]{2,1,0:T(8,128)S(1)}) custom-call(f32[32,8,128]{2,1,0:T(8,128)S(1)} %all_to_all.20.sums.sums0, bf16[64,64,192]{2,1,0:T(8,128)(2,1)S(1)} %get-tuple-element.101.blocks, f32[64,64,128]{2,1,0:T(8,128)S(1)} %get-tuple-element.112.after, ...), custom_call_target="tpu_custom_call" | custom-call | bytes 20643840 | tf_op jit(solution)/shard_map/first_step/pallas_call | solution.py:515
  150.9 3.3 %collective-permute-done.13.far_q0.g1 = f32[16,64,128]{2,1,0:T(8,128)S(1)} collective-permute-done((f32[16,64,128]{2,1,0:T(8,128)S(1)}, f32[16,64,128]{2,1,0:T(8,128)S(1)}, u32[]{:S(2)}, u32[]{:S(2)}) %collective-permute-start.13) | collective-permute-done | bytes 524320 | tf_op jit(solution)/shard_map/ppermute | solution.py:539
  154.2 1.8 %links.1 = f32[32,16,128]{2,1,0:T(8,128)S(1)} custom-call(f32[32,8,128]{2,1,0:T(8,128)S(1)} %all_to_all.20.sums.sums0, s32[64]{0:T(128)S(1)} %get-tuple-element.126.placed, f32[16,8,128]{2,1,0:T(8,128)S(1)} %get-tuple-element.115.totals, f32[16,64,128]{2,1,0:T(8,128)S(1)} %copy-done.1, f32[16,64,128]{2,1,0:T(8,128)S(1)} %copy-done.2, ...), custom_call_target="tpu_custom_call" | custom-call | bytes 16187648 | tf_op jit(solution)/shard_map/links/pallas_call | solution.py:515
  156.0 15.2 %all_to_all.21.sums1 = f32[32,16,128]{2,1,0:T(8,128)S(1)} all-to-all(f32[32,16,128]{2,1,0:T(8,128)S(1)} %links.1), channel_id=1, replica_groups=mesh['sector'=4,'axial'=8] {'sector','axial'}, dimensions={0} | all-to-all | bytes 524288 | tf_op jit(solution)/shard_map/all_to_all | solution.py:529
  171.2 4.0 %last.1 = (f32[64,64,128]{2,1,0:T(8,128)}, f32[64,64,128]{2,1,0:T(8,128)}) custom-call(f32[32,8,128]{2,1,0:T(8,128)S(1)} %all_to_all.20.sums.sums0, f32[32,16,128]{2,1,0:T(8,128)S(1)} %all_to_all.21.sums1, s32[64]{0:T(128)S(1)} %get-tuple-element.126.placed, f32[16,64,128]{2,1,0:T(8,128)S(1)} %collective-permute-done.15.g0, ...), custom_call_target="tpu_custom_call" | custom-call | bytes 21364992 | tf_op jit(solution)/shard_map/last/pallas_call | solution.py:515
  (64 shorter events, 15.1 us)
Async XLA Ops:
  0.6 7.5 %copy-start.15 = (s32[2,16,2]{1,2,0:T(2,128)S(1)}, s32[2,16,2]{1,2,0:T(2,128)}, u32[]{:S(2)}) copy-start(s32[2,16,2]{1,2,0:T(2,128)} %param.17) | copy-start | bytes 772
  3.6 26.4 %collective-permute-start.1 = (f32[16,72,128]{2,1,0:T(8,128)}, f32[16,72,128]{2,1,0:T(8,128)S(1)}, u32[]{:S(2)}, u32[]{:S(2)}) collective-permute-start(f32[16,72,128]{2,1,0:T(8,128)} %get-tuple-element.72), channel_id=1, source_target_pairs={{0,8},{8,16},{16,24},{24,0},{1,9},{9,17},{17,25},{25,1},{2,10},{10... | collective-permute-start | bytes 1769480 | tf_op jit(solution)/shard_map/ppermute | solution.py:534
  6.7 23.3 %collective-permute-start.2 = (f32[16,72,128]{2,1,0:T(8,128)}, f32[16,72,128]{2,1,0:T(8,128)S(1)}, u32[]{:S(2)}, u32[]{:S(2)}) collective-permute-start(f32[16,72,128]{2,1,0:T(8,128)} %get-tuple-element.73), channel_id=1, source_target_pairs={{0,1},{1,2},{2,3},{3,4},{4,5},{5,6},{6,7},{8,9},{9,10},{10,11},{11... | collective-permute-start | bytes 1769480 | tf_op jit(solution)/shard_map/ppermute | solution.py:534
  8.2 14.1 %collective-permute-start = (s32[2,2,16]{2,1,0:T(2,128)S(1)}, s32[2,2,16]{2,1,0:T(2,128)S(1)}, u32[]{:S(2)}, u32[]{:S(2)}) collective-permute-start(s32[2,2,16]{2,1,0:T(2,128)S(1)} %bitcast.33), channel_id=1, source_target_pairs={{0,8},{8,16},{16,24},{24,0},{1,9},{9,17},{17,25},{25,1},{2,10},{10... | collective-permute-start | bytes 776 | tf_op jit(solution)/shard_map/ppermute | solution.py:534
  25.4 15.2 %collective-permute-start.3 = (f32[16,64,128]{2,1,0:T(8,128)}, f32[16,64,128]{2,1,0:T(8,128)S(1)}, u32[]{:S(2)}, u32[]{:S(2)}) collective-permute-start(f32[16,64,128]{2,1,0:T(8,128)} %far.2), channel_id=1, source_target_pairs={{8,0},{16,8},{24,16},{0,24},{9,1},{17,9},{25,17},{1,25},{10,2},{18... | collective-permute-start | bytes 1572872 | tf_op jit(solution)/shard_map/ppermute | solution.py:539
  27.2 17.1 %all-to-all-start = ((f32[32,8,128]{2,1,0:T(8,128)}), f32[32,8,128]{2,1,0:T(8,128)S(1)}, u32[]{:S(2)}, u32[]{:S(2)}) async-start(f32[32,8,128]{2,1,0:T(8,128)} %bitcast.9), calls=%async_computation | async-start | bytes 262144 | tf_op jit(solution)/shard_map/all_to_all | solution.py:529
  30.0 14.3 %copy-start.6 = (f32[16,72,128]{2,1,0:T(8,128)}, f32[16,72,128]{2,1,0:T(8,128)S(1)}, u32[]{:S(2)}) copy-start(f32[16,72,128]{2,1,0:T(8,128)S(1)} %collective-permute-done.1.g0) | copy-start | bytes 1769476
  30.0 14.3 %copy-start.5 = (f32[16,72,128]{2,1,0:T(8,128)}, f32[16,72,128]{2,1,0:T(8,128)S(1)}, u32[]{:S(2)}) copy-start(f32[16,72,128]{2,1,0:T(8,128)S(1)} %collective-permute-done.2.g2) | copy-start | bytes 1769476
  40.6 3.7 %copy-start.8 = (f32[16,64,128]{2,1,0:T(8,128)}, f32[16,64,128]{2,1,0:T(8,128)S(1)}, u32[]{:S(2)}) copy-start(f32[16,64,128]{2,1,0:T(8,128)S(1)} %collective-permute-done.3.g1) | copy-start | bytes 1572868
  44.2 7.3 %copy-start.7 = (f32[32,8,128]{2,1,0:T(8,128)}, f32[32,8,128]{2,1,0:T(8,128)S(1)}, u32[]{:S(2)}) copy-start(f32[32,8,128]{2,1,0:T(8,128)S(1)} %all-to-all-done) | copy-start | bytes 393220
  44.2 5.9 %copy-start.10 = (f32[4096]{0:T(1024)S(1)}, f32[4096]{0:T(1024)}, u32[]{:S(2)}) copy-start(f32[4096]{0:T(1024)} %param.16) | copy-start | bytes 49156
  44.2 8.1 %copy-start.16 = (s32[16]{0:T(128)S(1)}, s32[16]{0:T(128)}, u32[]{:S(2)}) copy-start(s32[16]{0:T(128)} %convert_reduce_fusion.index) | copy-start | bytes 196
  44.3 53.7 %all-to-all-start.1 = ((f32[32,128,128]{2,1,0:T(8,128)}), f32[32,128,128]{2,1,0:T(8,128)S(1)}, u32[]{:S(2)}, u32[]{:S(2)}) async-start(f32[32,128,128]{2,1,0:T(8,128)} %bitcast.28), calls=%async_computation.1 | async-start | bytes 4194304 | tf_op jit(solution)/shard_map/all_to_all | solution.py:529
  48.9 39.0 %collective-permute-start.8 = (f32[16,64,128]{2,1,0:T(8,128)}, f32[16,64,128]{2,1,0:T(8,128)S(1)}, u32[]{:S(2)}, u32[]{:S(2)}) collective-permute-start(f32[16,64,128]{2,1,0:T(8,128)} %far.3), channel_id=1, source_target_pairs={{1,0},{2,1},{3,2},{4,3},{5,4},{6,5},{7,6},{9,8},{10,9},{11,10},{12... | collective-permute-start | bytes 1572872 | tf_op jit(solution)/shard_map/ppermute | solution.py:539
  56.5 31.2 %collective-permute-start.4 = (f32[16,128]{1,0:T(8,128)}, f32[16,128]{1,0:T(8,128)S(1)}, u32[]{:S(2)}, u32[]{:S(2)}) collective-permute-start(f32[16,128]{1,0:T(8,128)} %get-tuple-element.86), channel_id=1, source_target_pairs={{0,8},{8,16},{16,24},{24,0},{1,9},{9,17},{17,25},{25,1},{2,10},{10... | collective-permute-start | bytes 24584 | tf_op jit(solution)/shard_map/ppermute | solution.py:534
  58.1 29.7 %collective-permute-start.5 = (f32[16,128]{1,0:T(8,128)}, f32[16,128]{1,0:T(8,128)S(1)}, u32[]{:S(2)}, u32[]{:S(2)}) collective-permute-start(f32[16,128]{1,0:T(8,128)} %get-tuple-element.87), channel_id=1, source_target_pairs={{8,0},{16,8},{24,16},{0,24},{9,1},{17,9},{25,17},{1,25},{10,2},{18... | collective-permute-start | bytes 24584 | tf_op jit(solution)/shard_map/ppermute | solution.py:539
  60.4 27.4 %collective-permute-start.6 = (f32[16,128]{1,0:T(8,128)}, f32[16,128]{1,0:T(8,128)S(1)}, u32[]{:S(2)}, u32[]{:S(2)}) collective-permute-start(f32[16,128]{1,0:T(8,128)} %get-tuple-element.88), channel_id=1, source_target_pairs={{0,1},{1,2},{2,3},{3,4},{4,5},{5,6},{6,7},{8,9},{9,10},{10,11},{11... | collective-permute-start | bytes 24584 | tf_op jit(solution)/shard_map/ppermute | solution.py:534
  63.1 24.7 %collective-permute-start.7 = (f32[16,128]{1,0:T(8,128)}, f32[16,128]{1,0:T(8,128)S(1)}, u32[]{:S(2)}, u32[]{:S(2)}) collective-permute-start(f32[16,128]{1,0:T(8,128)} %get-tuple-element.89), channel_id=1, source_target_pairs={{1,0},{2,1},{3,2},{4,3},{5,4},{6,5},{7,6},{9,8},{10,9},{11,10},{12... | collective-permute-start | bytes 24584 | tf_op jit(solution)/shard_map/ppermute | solution.py:539
  64.4 33.6 %copy-start.3 = (s32[64]{0:T(128)S(1)}, s32[64]{0:T(128)}, u32[]{:S(2)}) copy-start(s32[64]{0:T(128)} %get-tuple-element.127.picked) | copy-start | bytes 772
  64.4 33.6 %copy-start.4 = (s32[256]{0:T(256)S(1)}, s32[256]{0:T(256)}, u32[]{:S(2)}) copy-start(s32[256]{0:T(256)} %select_reduce_fusion.tags) | copy-start | bytes 3076
  88.4 0.9 copy-start.9
  103.7 30.4 %collective-permute-start.9 = (f32[16,64,128]{2,1,0:T(8,128)S(1)}, f32[16,64,128]{2,1,0:T(8,128)S(1)}, u32[]{:S(2)}, u32[]{:S(2)}) collective-permute-start(f32[16,64,128]{2,1,0:T(8,128)S(1)} %get-tuple-element.107), channel_id=1, source_target_pairs={{0,8},{8,16},{16,24},{24,0},{1,9},{9,17},{17,25},{25,1},{2,10},{10... | collective-permute-start | bytes 1572872 | tf_op jit(solution)/shard_map/ppermute | solution.py:534
  109.5 24.7 %collective-permute-start.10 = (f32[16,64,128]{2,1,0:T(8,128)S(1)}, f32[16,64,128]{2,1,0:T(8,128)S(1)}, u32[]{:S(2)}, u32[]{:S(2)}) collective-permute-start(f32[16,64,128]{2,1,0:T(8,128)S(1)} %get-tuple-element.108), channel_id=1, source_target_pairs={{8,0},{16,8},{24,16},{0,24},{9,1},{17,9},{25,17},{1,25},{10,2},{18... | collective-permute-start | bytes 1572872 | tf_op jit(solution)/shard_map/ppermute | solution.py:539
  109.5 6.8 %copy-start = (f32[4096,128]{1,0:T(8,128)S(1)}, f32[4096,128]{1,0:T(8,128)}, u32[]{:S(2)}) copy-start(f32[4096,128]{1,0:T(8,128)} %param.19) | copy-start | bytes 6291460
  113.6 20.6 %collective-permute-start.11 = (f32[16,64,128]{2,1,0:T(8,128)S(1)}, f32[16,64,128]{2,1,0:T(8,128)S(1)}, u32[]{:S(2)}, u32[]{:S(2)}) collective-permute-start(f32[16,64,128]{2,1,0:T(8,128)S(1)} %get-tuple-element.109), channel_id=1, source_target_pairs={{0,1},{1,2},{2,3},{3,4},{4,5},{5,6},{6,7},{8,9},{9,10},{10,11},{11... | collective-permute-start | bytes 1572872 | tf_op jit(solution)/shard_map/ppermute | solution.py:534
  114.9 19.2 %collective-permute-start.12 = (f32[16,64,128]{2,1,0:T(8,128)S(1)}, f32[16,64,128]{2,1,0:T(8,128)S(1)}, u32[]{:S(2)}, u32[]{:S(2)}) collective-permute-start(f32[16,64,128]{2,1,0:T(8,128)S(1)} %get-tuple-element.110), channel_id=1, source_target_pairs={{1,0},{2,1},{3,2},{4,3},{5,4},{6,5},{7,6},{9,8},{10,9},{11,10},{12... | collective-permute-start | bytes 1572872 | tf_op jit(solution)/shard_map/ppermute | solution.py:539
  135.7 18.6 %collective-permute-start.13 = (f32[16,64,128]{2,1,0:T(8,128)S(1)}, f32[16,64,128]{2,1,0:T(8,128)S(1)}, u32[]{:S(2)}, u32[]{:S(2)}) collective-permute-start(f32[16,64,128]{2,1,0:T(8,128)S(1)} %get-tuple-element.116), channel_id=1, source_target_pairs={{8,0},{16,8},{24,16},{0,24},{9,1},{17,9},{25,17},{1,25},{10,2},{18... | collective-permute-start | bytes 1572872 | tf_op jit(solution)/shard_map/ppermute | solution.py:539
  141.8 12.4 %collective-permute-start.14 = (f32[16,64,128]{2,1,0:T(8,128)S(1)}, f32[16,64,128]{2,1,0:T(8,128)S(1)}, u32[]{:S(2)}, u32[]{:S(2)}) collective-permute-start(f32[16,64,128]{2,1,0:T(8,128)S(1)} %get-tuple-element.117), channel_id=1, source_target_pairs={{1,0},{2,1},{3,2},{4,3},{5,4},{6,5},{7,6},{9,8},{10,9},{11,10},{12... | collective-permute-start | bytes 1572872 | tf_op jit(solution)/shard_map/ppermute | solution.py:539
  143.1 28.1 %collective-permute-start.15 = (f32[16,64,128]{2,1,0:T(8,128)S(1)}, f32[16,64,128]{2,1,0:T(8,128)S(1)}, u32[]{:S(2)}, u32[]{:S(2)}) collective-permute-start(f32[16,64,128]{2,1,0:T(8,128)S(1)} %get-tuple-element.121), channel_id=1, source_target_pairs={{0,8},{8,16},{16,24},{24,0},{1,9},{9,17},{17,25},{25,1},{2,10},{10... | collective-permute-start | bytes 1572872 | tf_op jit(solution)/shard_map/ppermute | solution.py:534
  143.2 28.1 %collective-permute-start.16 = (f32[16,64,128]{2,1,0:T(8,128)S(1)}, f32[16,64,128]{2,1,0:T(8,128)S(1)}, u32[]{:S(2)}, u32[]{:S(2)}) collective-permute-start(f32[16,64,128]{2,1,0:T(8,128)S(1)} %get-tuple-element.122), channel_id=1, source_target_pairs={{0,1},{1,2},{2,3},{3,4},{4,5},{5,6},{6,7},{8,9},{9,10},{10,11},{11... | collective-permute-start | bytes 1572872 | tf_op jit(solution)/shard_map/ppermute | solution.py:534
  146.2 8.0 %copy-start.1 = (f32[16,64,128]{2,1,0:T(8,128)S(1)}, f32[16,64,128]{2,1,0:T(8,128)}, u32[]{:S(2)}) copy-start(f32[16,64,128]{2,1,0:T(8,128)} %get-tuple-element.93.p1_in.far_u0) | copy-start | bytes 1572868
  146.2 8.0 %copy-start.2 = (f32[16,64,128]{2,1,0:T(8,128)S(1)}, f32[16,64,128]{2,1,0:T(8,128)}, u32[]{:S(2)}) copy-start(f32[16,64,128]{2,1,0:T(8,128)} %get-tuple-element.95.p3_in.far_u2) | copy-start | bytes 1572868
  (5 other events, 3.0 us)
